TPU v7x, 128 devices: a whole 4x4x4 slice. The times are simulated.
128 devices in a mesh: gx: 8 (over z, core), gy: 16 (over y, x).
Axes of the slice: x: 4, y: 4, z: 4, core: 2. Of those that a mesh axis runs over, the one named last changes fastest.
Arguments:
- stored_vectors: bfloat16 [2, 16, 64, 8192], P(None, None, 'gx', 'gy'), may hold values from -4 to 4
- disorder: float32 [2, 64, 8192], P(None, 'gx', 'gy'), may hold values from -1.5 to 1.5
- vacancy: int32 [2, 64, 8192], P(None, 'gx', 'gy'), may hold values 0 or 1
- plan: int32 [64], replicated, may hold values from 0 to 63, as said below
Outputs:
- local_moments: float32 [4, 2, 64, 8192], P(None, None, 'gx', 'gy')
- trace_moments: float32 [4, 16], replicated
Inputs may be any that keep to these rules, and one draw needn't show every extreme that they name: plan is a permutation of 0 to 63; stored block b is held by the device at gy index b // 4. The 4 lattice blocks of one device come from 4 different devices, and the 4 stored blocks of one device go to 4 different devices.
All inputs are finite; a program needn't handle non-finite values. No bound on the sum of `vacancy` on one device may be relied on, other than what follows from the above.
Results may differ from a plain program's by a relative error of at most 0.0003.
Values may be sent and summed in bfloat16 or wider, within the bound.
No kernel may reach another device: no remote copies, remote signals or barrier semaphores. Data moves between devices by JAX's collectives and lax.ppermute only.
A program may use at most 64 MiB of HBM per device.

v0:
```python
import jax
import jax.numpy as jnp
from jax import lax
from jax.sharding import Mesh
from jax.sharding import PartitionSpec as P

BLOCK = 128
R = 16
TERMS = 4
GY = ("gy_0", "gy_1")
GX = ("gx_0", "gx_1")
GX_GY = ("gx_0", "gx_1", "gy_0", "gy_1")


HOP_NEAR = 1.0
HOP_NEXT = 0.3
TWIST_COS = 0.4535961214255773
TWIST_SIN = 0.8912073600614354
SPREAD = 6.5
NEAR_A = ((0, 0), (-1, 0), (0, -1))
NEAR_B = ((0, 0), (1, 0), (0, 1))
SECOND = ((1, 0), (-1, 1), (0, -1))


def extended(block, sides, width):
    for axis, dim in sides:
        count = lax.axis_size(axis)
        forward = [(i, i + 1) for i in range(count - 1)]
        forward.append((count - 1, 0))
        backward = [(target, source) for source, target in forward]
        low = lax.ppermute(
            lax.slice_in_dim(block, block.shape[dim] - width, None, axis=dim), axis, forward
        )
        high = lax.ppermute(lax.slice_in_dim(block, 0, width, axis=dim), axis, backward)
        block = jnp.concatenate([low, block, high], axis=dim)
    return block


def one_axis_at_a_time(array, axes):
    for axis in axes:
        array = lax.psum(array, axis)
    return array


def collect_sum(fetch, field, shifts):
    total = fetch(field, shifts[0])
    for shift in shifts[1:]:
        total = total + fetch(field, shift)
    return total


def hamilton(fetch, real, imag, onsite, keep):
    backs = tuple(((-a, -b) for a, b in SECOND))
    out_real = []
    out_imag = []
    for sublat, chiral, bonds in ((0, 1.0, NEAR_A), (1, -1.0, NEAR_B)):
        other = 1 - sublat
        near_real = collect_sum(fetch, real[other], bonds)
        forward_real = collect_sum(fetch, real[sublat], SECOND)
        backward_real = collect_sum(fetch, real[sublat], backs)
        centre_real = fetch(real[sublat], (0, 0))
        mixed_real = TWIST_COS * (forward_real + backward_real)
        mixed_imag = chiral * TWIST_SIN * (forward_real - backward_real)
        level = onsite[sublat][None]
        if imag is None:
            result_imag = HOP_NEXT * mixed_imag
        else:
            near_imag = collect_sum(fetch, imag[other], bonds)
            forward_imag = collect_sum(fetch, imag[sublat], SECOND)
            backward_imag = collect_sum(fetch, imag[sublat], backs)
            centre_imag = fetch(imag[sublat], (0, 0))
            mixed_real = mixed_real - chiral * TWIST_SIN * (forward_imag - backward_imag)
            mixed_imag = mixed_imag + TWIST_COS * (forward_imag + backward_imag)
            result_imag = level * centre_imag - HOP_NEAR * near_imag + HOP_NEXT * mixed_imag
        result_real = level * centre_real - HOP_NEAR * near_real + HOP_NEXT * mixed_real
        factor = keep[sublat][None] / SPREAD
        out_real.append(result_real * factor)
        out_imag.append(result_imag * factor)
    return (jnp.stack(out_real), jnp.stack(out_imag))


def local(stored_vectors, disorder, vacancy, plan):
    column = lax.axis_index(GY)
    columns = lax.axis_size(GY)
    vectors = stored_vectors.shape[1]
    width_x = stored_vectors.shape[2]
    width_y = stored_vectors.shape[3]
    blocks_here = width_y // BLOCK
    total_blocks = plan.shape[0]
    wanted = lax.dynamic_slice_in_dim(plan, column * blocks_here, blocks_here)
    pieces = stored_vectors.reshape(2, vectors, width_x, blocks_here, BLOCK)
    held = column * blocks_here + jnp.arange(blocks_here, dtype=jnp.int32)
    matches = (plan[None, :] == held[:, None]).astype(jnp.int32)
    target = jnp.sum(jnp.arange(total_blocks, dtype=jnp.int32)[None, :] * matches, axis=1)
    target_device = target // blocks_here
    sender = (jnp.arange(columns, dtype=jnp.int32)[:, None] == target_device[None, :]).astype(
        jnp.bfloat16
    )
    outgoing = jnp.einsum(
        "pb,srxbc->psrxc", sender, pieces, preferred_element_type=jnp.float32
    ).astype(jnp.bfloat16)
    incoming = lax.all_to_all(outgoing, GY, split_axis=0, concat_axis=0, tiled=True)
    source_device = wanted // blocks_here
    picker = (jnp.arange(columns, dtype=jnp.int32)[None, :] == source_device[:, None]).astype(
        jnp.bfloat16
    )
    arranged = jnp.einsum("kp,psrxc->srxkc", picker, incoming, preferred_element_type=jnp.float32)
    lattice = arranged.reshape(2, vectors, width_x, width_y)
    keep = vacancy.astype(jnp.float32)
    start = lattice * keep[:, None]
    sites_total = 2 * width_x * lax.axis_size(GX) * width_y * columns

    def operate(real, imag):
        if imag is None:
            joined = real[None]
        else:
            joined = jnp.stack([real, imag])
        padded = extended(joined, ((GX, 3), (GY, 4)), 1)

        def fetch(field, shift):
            return field[
                :, 1 + shift[0] : 1 + shift[0] + width_x, 1 + shift[1] : 1 + shift[1] + width_y
            ]

        padded_imag = None if imag is None else padded[1]
        return hamilton(fetch, padded[0], padded_imag, disorder, keep)

    locals_list = []
    partials = []

    def record(field_real):
        product = start * field_real
        locals_list.append(jnp.sum(product, axis=1) / R)
        partial_value = jnp.sum(product, axis=(0, 2, 3))
        partials.append(partial_value)

    previous_real, previous_imag = (start, None)
    current_real, current_imag = operate(start, None)
    record(current_real)
    for term in range(1, TERMS):
        image_real, image_imag = operate(current_real, current_imag)
        next_real = 2.0 * image_real - previous_real
        if previous_imag is None:
            next_imag = 2.0 * image_imag
        else:
            next_imag = 2.0 * image_imag - previous_imag
        previous_real, previous_imag = (current_real, current_imag)
        current_real, current_imag = (next_real, next_imag)
        record(current_real)
    summed = one_axis_at_a_time(jnp.stack(partials), GX_GY)
    return (jnp.stack(locals_list), summed / sites_total)


def solution(mesh):
    torus = Mesh(mesh.devices.reshape(4, 2, 4, 4), ("gx_0", "gx_1", "gy_0", "gy_1"))
    placed = (P(None, None, GX, GY), P(None, GX, GY), P(None, GX, GY), P())
    return jax.shard_map(
        local, mesh=torus, in_specs=placed, out_specs=(P(None, None, GX, GY), P()), check_vma=False
    )
```

profile of v0, /device:TPU:1, one launch (start us, length us, event | category | flops | bytes accessed | tf_op | source)
XLA Modules:
  0.0 174.3 jit_solution(8323656978280587597)
XLA Ops:
  0.7 0.9 select_reduce_fusion
  2.2 1.2 copy.10
  3.5 7.7 %all-to-all-start = ((bf16[16,2,16,8,128]{4,3,2,1,0:T(8,128)(2,1)}), bf16[16,2,16,8,128]{4,3,2,1,0:T(8,128)(2,1)S(1)}, u32[]{:S(2)}, u32[]{:S(2)}) async-start(bf16[16,2,16,8,128]{4,3,2,1,0:T(8,128)(2,1)} %copy.10), calls=%async_computation | async-start | bytes 2097152 | tf_op jit(solution)/shard_map/all_to_all | solution.py:102
  11.9 15.3 %all-to-all-done = bf16[16,2,16,8,128]{4,3,2,1,0:T(8,128)(2,1)S(1)} async-done(((bf16[16,2,16,8,128]{4,3,2,1,0:T(8,128)(2,1)}), bf16[16,2,16,8,128]{4,3,2,1,0:T(8,128)(2,1)S(1)}, u32[]{:S(2)}, u32[]{:S(2)}) %all-to-all-start) | async-done | bytes 1048608 | tf_op jit(solution)/shard_map/all_to_all | solution.py:102
  28.2 4.1 %collective-permute-start = (f32[1,2,16,1,512]{4,3,2,1,0:T(1,128)S(1)}, f32[1,2,16,1,512]{4,3,2,1,0:T(1,128)S(1)}, u32[]{:S(2)}, u32[]{:S(2)}) collective-permute-start(f32[1,2,16,1,512]{4,3,2,1,0:T(1,128)S(1)} %get-tuple-element.53), channel_id=1, source_target_pairs={{0,16},{16,32},{32,48},{48,64},{64,80},{80,96},{96,112},{112,0},{1... | collective-permute-start | bytes 196616 | tf_op jit(solution)/shard_map/ppermute | solution.py:31
  32.4 1.3 collective-permute-done
  33.7 2.4 %collective-permute-done.1 = f32[1,2,16,1,512]{4,3,2,1,0:T(1,128)S(1)} collective-permute-done((f32[1,2,16,1,512]{4,3,2,1,0:T(1,128)S(1)}, f32[1,2,16,1,512]{4,3,2,1,0:T(1,128)S(1)}, u32[]{:S(2)}, u32[]{:S(2)}) %collective-permute-start.1) | collective-permute-done | bytes 65568 | tf_op jit(solution)/shard_map/ppermute | solution.py:34
  36.3 4.8 %collective-permute-start.3 = (f32[1,2,16,10,1]{4,3,2,1,0:T(8,128)S(1)}, f32[1,2,16,10,1]{4,3,2,1,0:T(8,128)S(1)}, u32[]{:S(2)}, u32[]{:S(2)}) collective-permute-start(f32[1,2,16,10,1]{4,3,2,1,0:T(8,128)S(1)} %get-tuple-element.48), channel_id=1, source_target_pairs={{1,0},{2,1},{3,2},{4,3},{5,4},{6,5},{7,6},{8,7},{9,8},{10,9},{11,1... | collective-permute-start | bytes 3848 | tf_op jit(solution)/shard_map/ppermute | solution.py:34
  41.1 6.7 %collective-permute-done.2 = f32[1,2,16,10,1]{4,3,2,1,0:T(8,128)S(1)} collective-permute-done((f32[1,2,16,10,1]{4,3,2,1,0:T(8,128)S(1)}, f32[1,2,16,10,1]{4,3,2,1,0:T(8,128)S(1)}, u32[]{:S(2)}, u32[]{:S(2)}) %collective-permute-start.2) | collective-permute-done | bytes 1312 | tf_op jit(solution)/shard_map/ppermute | solution.py:31
  47.8 0.9 pad_maximum_fusion.3
  50.7 1.4 collective-permute-done.4
  52.1 2.8 %collective-permute-done.5 = f32[2,2,16,1,512]{4,3,2,1,0:T(1,128)S(1)} collective-permute-done((f32[2,2,16,1,512]{4,3,2,1,0:T(1,128)S(1)}, f32[2,2,16,1,512]{4,3,2,1,0:T(1,128)S(1)}, u32[]{:S(2)}, u32[]{:S(2)}) %collective-permute-start.5) | collective-permute-done | bytes 131104 | tf_op jit(solution)/shard_map/ppermute | solution.py:34
  55.3 5.6 %collective-permute-start.7 = (f32[2,2,16,10,1]{4,3,2,1,0:T(8,128)S(1)}, f32[2,2,16,10,1]{4,3,2,1,0:T(8,128)S(1)}, u32[]{:S(2)}, u32[]{:S(2)}) collective-permute-start(f32[2,2,16,10,1]{4,3,2,1,0:T(8,128)S(1)} %get-tuple-element.33), channel_id=1, source_target_pairs={{1,0},{2,1},{3,2},{4,3},{5,4},{6,5},{7,6},{8,7},{9,8},{10,9},{11,1... | collective-permute-start | bytes 7688 | tf_op jit(solution)/shard_map/ppermute | solution.py:34
  60.9 10.8 %collective-permute-done.6 = f32[2,2,16,10,1]{4,3,2,1,0:T(8,128)S(1)} collective-permute-done((f32[2,2,16,10,1]{4,3,2,1,0:T(8,128)S(1)}, f32[2,2,16,10,1]{4,3,2,1,0:T(8,128)S(1)}, u32[]{:S(2)}, u32[]{:S(2)}) %collective-permute-start.6) | collective-permute-done | bytes 2592 | tf_op jit(solution)/shard_map/ppermute | solution.py:31
  71.6 1.9 %pad_maximum_fusion = f32[2,2,16,10,514]{4,3,2,1,0:T(8,128)S(1)} fusion(f32[2,2,16,10,1]{4,3,2,1,0:T(8,128)S(1)} %collective-permute-done.7, f32[2,2,16,1,512]{4,3,2,1,0:T(1,128)S(1)} %collective-permute-done.5, f32[1,2,16,8,512]{4,3,2,1,0:T(8,128)S(1)} %maximum_bitcast_fusion.1, f32[1,2,16,8,512]{4,3,2,1,0:T(8,128)S(1)} %maximum_bitcast_fusion, ...), kind=kLoop, calls=%fused_computation | loop fusion | flops 1644800 | bytes 2631680 | tf_op jit(solution)/shard_map/concatenate | solution.py:35
  73.8 0.8 add_multiply_fusion.3
  74.6 0.9 add_multiply_fusion.2
  75.5 0.8 multiply_bitcast_fusion.3
  76.3 0.9 multiply_bitcast_fusion.2
  77.6 1.8 %collective-permute-start.9 = (f32[2,2,16,1,512]{4,3,2,1,0:T(1,128)S(1)}, f32[2,2,16,1,512]{4,3,2,1,0:T(1,128)S(1)}, u32[]{:S(2)}, u32[]{:S(2)}) collective-permute-start(f32[2,2,16,1,512]{4,3,2,1,0:T(1,128)S(1)} %get-tuple-element.44), channel_id=1, source_target_pairs={{16,0},{32,16},{48,32},{64,48},{80,64},{96,80},{112,96},{0,112},{1... | collective-permute-start | bytes 393224 | tf_op jit(solution)/shard_map/ppermute | solution.py:34
  79.4 0.8 collective-permute-done.8
  80.2 1.8 %collective-permute-done.9 = f32[2,2,16,1,512]{4,3,2,1,0:T(1,128)S(1)} collective-permute-done((f32[2,2,16,1,512]{4,3,2,1,0:T(1,128)S(1)}, f32[2,2,16,1,512]{4,3,2,1,0:T(1,128)S(1)}, u32[]{:S(2)}, u32[]{:S(2)}) %collective-permute-start.9) | collective-permute-done | bytes 131104 | tf_op jit(solution)/shard_map/ppermute | solution.py:34
  82.5 5.8 %collective-permute-start.11 = (f32[2,2,16,10,1]{4,3,2,1,0:T(8,128)S(1)}, f32[2,2,16,10,1]{4,3,2,1,0:T(8,128)S(1)}, u32[]{:S(2)}, u32[]{:S(2)}) collective-permute-start(f32[2,2,16,10,1]{4,3,2,1,0:T(8,128)S(1)} %get-tuple-element.31), channel_id=1, source_target_pairs={{1,0},{2,1},{3,2},{4,3},{5,4},{6,5},{7,6},{8,7},{9,8},{10,9},{11,1... | collective-permute-start | bytes 7688 | tf_op jit(solution)/shard_map/ppermute | solution.py:34
  88.3 9.4 %collective-permute-done.10 = f32[2,2,16,10,1]{4,3,2,1,0:T(8,128)S(1)} collective-permute-done((f32[2,2,16,10,1]{4,3,2,1,0:T(8,128)S(1)}, f32[2,2,16,10,1]{4,3,2,1,0:T(8,128)S(1)}, u32[]{:S(2)}, u32[]{:S(2)}) %collective-permute-start.10) | collective-permute-done | bytes 2592 | tf_op jit(solution)/shard_map/ppermute | solution.py:31
  97.7 1.9 %pad_maximum_fusion.1 = f32[2,2,16,10,514]{4,3,2,1,0:T(8,128)S(1)} fusion(f32[2,2,16,10,1]{4,3,2,1,0:T(8,128)S(1)} %collective-permute-done.11, f32[2,2,16,1,512]{4,3,2,1,0:T(1,128)S(1)} %collective-permute-done.9, f32[1,2,16,8,512]{4,3,2,1,0:T(8,128)S(1)} %maximum_multiply_fusion.2, f32[1,2,16,8,512]{4,3,2,1,0:T(8,128)S(1)} %fusion.2, ...), kind=kLoop, calls=%fused_computation.1 | loop fusion | flops 1644800 | bytes 2631680 | tf_op jit(solution)/shard_map/concatenate | solution.py:35
  99.8 0.8 add_multiply_fusion.1
  100.6 0.9 add_multiply_fusion
  101.5 0.8 multiply_bitcast_fusion.1
  102.3 0.9 multiply_bitcast_fusion
  103.4 0.9 pad_maximum_fusion.20
  105.0 2.5 %collective-permute-start.13 = (f32[2,2,16,1,512]{4,3,2,1,0:T(1,128)}, f32[2,2,16,1,512]{4,3,2,1,0:T(1,128)}, u32[]{:S(2)}, u32[]{:S(2)}) collective-permute-start(f32[2,2,16,1,512]{4,3,2,1,0:T(1,128)} %get-tuple-element.42), channel_id=1, source_target_pairs={{16,0},{32,16},{48,32},{64,48},{80,64},{96,80},{112,96},{0,112},{1... | collective-permute-start | bytes 393224 | tf_op jit(solution)/shard_map/ppermute | solution.py:34
  108.1 0.8 stack.134
  108.9 0.8 stack.135
  109.7 1.0 constant_dynamic-update-slice_fusion.1
  110.7 2.1 %pad_maximum_fusion.7 = (f32[2,2,16,10,1]{4,3,2,1,0:T(8,128)}, f32[2,2,16,10,1]{4,3,2,1,0:T(8,128)}) fusion(f32[2,2,16,1,512]{4,3,2,1,0:T(1,128)} %collective-permute-done.13, f32[2,2,16,1,512]{4,3,2,1,0:T(1,128)} %collective-permute-done.12, f32[1,2,16,8,512]{4,3,2,1,0:T(8,128)S(1)} %fusion.6, f32[1,2,16,8,512]{4,3,2,1,0:T(8,128)S(1)} %fusion.5), kind=kLoop, calls=%fused_computation.24 | loop fusion | flops 3840 | bytes 1315840 | tf_op jit(solution)/shard_map/slice | solution.py:32
  112.8 5.1 %collective-permute-start.15 = (f32[2,2,16,10,1]{4,3,2,1,0:T(8,128)}, f32[2,2,16,10,1]{4,3,2,1,0:T(8,128)}, u32[]{:S(2)}, u32[]{:S(2)}) collective-permute-start(f32[2,2,16,10,1]{4,3,2,1,0:T(8,128)} %get-tuple-element.29), channel_id=1, source_target_pairs={{1,0},{2,1},{3,2},{4,3},{5,4},{6,5},{7,6},{8,7},{9,8},{10,9},{11,1... | collective-permute-start | bytes 7688 | tf_op jit(solution)/shard_map/ppermute | solution.py:34
  118.0 0.9 stack.146
  119.6 0.8 stack.156
  121.2 6.3 %collective-permute-done.14 = f32[2,2,16,10,1]{4,3,2,1,0:T(8,128)} collective-permute-done((f32[2,2,16,10,1]{4,3,2,1,0:T(8,128)}, f32[2,2,16,10,1]{4,3,2,1,0:T(8,128)}, u32[]{:S(2)}, u32[]{:S(2)}) %collective-permute-start.14) | collective-permute-done | bytes 2592 | tf_op jit(solution)/shard_map/ppermute | solution.py:31
  127.5 3.1 %pad_maximum_fusion.2 = f32[2,2,16,10,514]{4,3,2,1,0:T(8,128)S(1)} fusion(f32[2,2,16,10,1]{4,3,2,1,0:T(8,128)} %collective-permute-done.15, f32[2,2,16,1,512]{4,3,2,1,0:T(1,128)} %collective-permute-done.13, f32[1,2,16,8,512]{4,3,2,1,0:T(8,128)S(1)} %fusion.6, f32[1,2,16,8,512]{4,3,2,1,0:T(8,128)S(1)} %fusion.5, ...), kind=kLoop, calls=%fused_computation.2 | loop fusion | flops 1644800 | bytes 2631680 | tf_op jit(solution)/shard_map/concatenate | solution.py:35
  130.9 0.8 fusion.23
  132.5 2.4 %fusion.14 = f32[16,8,512]{2,1,0:T(8,128)} fusion(f32[16,10,514]{2,1,0:T(8,128)S(1)} %get-tuple-element.17, f32[16,10,514]{2,1,0:T(8,128)S(1)} %get-tuple-element.18, f32[16,10,514]{2,1,0:T(8,128)S(1)} %get-tuple-element.19, f32[8,512]{1,0:T(8,128)S(1)} %get-tuple-element.60, f32[8,512]{1,0:T(8,128)} %copy-done.5), kind=kLoop, calls=%fused_computation.58 | loop fusion | flops 1310720 | bytes 4489216 | tf_op jit(solution)/shard_map/mul | solution.py:77
  134.9 1.0 stack.173
  135.9 2.0 %fusion.38 = (f32[16]{0:T(128)S(1)}, f32[2,8,4,128]{3,2,1,0:T(4,128)S(1)}, f32[2,16,8,4,128]{4,3,2,1,0:T(4,128)S(1)}, f32[2,16,8,4,128]{4,3,2,1,0:T(4,128)S(1)}, f32[2,16,8,4,128]{4,3,2,1,0:T(4,128)S(1)}) fusion(f32[2,16,8,4,128]{4,3,2,1,0:T(4,128)S(1)} %copy-done.2, f32[2,16,8,4,128]{4,3,2,1,0:T(4,128)S(1)} %convolution_bitcast_fusion, ...), kind=kLoop, calls=%fused_computation.148 | loop fusion | flops 2088944 | bytes 4259904 | tf_op jit(solution)/shard_map/reduce_sum | solution.py:134
  138.6 13.3 %psum.28 = f32[4,16]{1,0:T(4,128)S(1)} all-reduce(f32[4,16]{1,0:T(4,128)S(1)} %pad_maximum_fusion.26), channel_id=1, replica_groups=mesh['gx_0'=4,'gx_1'=2,'gy_0'=4,'gy_1'=4] {'gx_0'}, use_global_device_ids=true, to_apply=%region_9.10 | all-reduce | flops 64 | bytes 512 | tf_op jit(solution)/shard_map/psum | solution.py:41
  151.9 3.4 %psum.29 = f32[4,16]{1,0:T(4,128)S(1)} all-reduce(f32[4,16]{1,0:T(4,128)S(1)} %psum.28), channel_id=1, replica_groups=mesh['gx_0'=4,'gx_1'=2,'gy_0'=4,'gy_1'=4] {'gx_1'}, use_global_device_ids=true, to_apply=%region_10.11 | all-reduce | flops 64 | bytes 512 | tf_op jit(solution)/shard_map/psum | solution.py:41
  155.3 6.1 %psum.30 = f32[4,16]{1,0:T(4,128)S(1)} all-reduce(f32[4,16]{1,0:T(4,128)S(1)} %psum.29), channel_id=1, replica_groups=mesh['gx_0'=4,'gx_1'=2,'gy_0'=4,'gy_1'=4] {'gy_0'}, use_global_device_ids=true, to_apply=%region_11.12 | all-reduce | flops 64 | bytes 512 | tf_op jit(solution)/shard_map/psum | solution.py:41
  161.3 11.5 %psum.31 = f32[4,16]{1,0:T(4,128)S(1)} all-reduce(f32[4,16]{1,0:T(4,128)S(1)} %psum.30), channel_id=1, replica_groups=mesh['gx_0'=4,'gx_1'=2,'gy_0'=4,'gy_1'=4] {'gy_1'}, use_global_device_ids=true, to_apply=%region_12.13 | all-reduce | flops 64 | bytes 512 | tf_op jit(solution)/shard_map/psum | solution.py:41
  (82 shorter events, 12.5 us)
Async XLA Ops:
  0.6 1.0 copy-start
  1.6 9.6 %copy-start.9 = (s32[64]{0:T(128)S(1)}, s32[64]{0:T(128)}, u32[]{:S(2)}) copy-start(s32[64]{0:T(128)} %param.7) | copy-start | bytes 772
  1.6 9.7 %copy-start.7 = (s32[2,8,512]{2,1,0:T(8,128)S(1)}, s32[2,8,512]{2,1,0:T(8,128)}, u32[]{:S(2)}) copy-start(s32[2,8,512]{2,1,0:T(8,128)} %param.6) | copy-start | bytes 98308
  3.4 28.9 %copy-start.8 = (f32[2,8,512]{2,1,0:T(8,128)S(1)}, f32[2,8,512]{2,1,0:T(8,128)}, u32[]{:S(2)}) copy-start(f32[2,8,512]{2,1,0:T(8,128)} %param.5) | copy-start | bytes 98308
  3.5 23.7 %all-to-all-start = ((bf16[16,2,16,8,128]{4,3,2,1,0:T(8,128)(2,1)}), bf16[16,2,16,8,128]{4,3,2,1,0:T(8,128)(2,1)S(1)}, u32[]{:S(2)}, u32[]{:S(2)}) async-start(bf16[16,2,16,8,128]{4,3,2,1,0:T(8,128)(2,1)} %copy.10), calls=%async_computation | async-start | bytes 2097152 | tf_op jit(solution)/shard_map/all_to_all | solution.py:102
  28.2 5.5 %collective-permute-start = (f32[1,2,16,1,512]{4,3,2,1,0:T(1,128)S(1)}, f32[1,2,16,1,512]{4,3,2,1,0:T(1,128)S(1)}, u32[]{:S(2)}, u32[]{:S(2)}) collective-permute-start(f32[1,2,16,1,512]{4,3,2,1,0:T(1,128)S(1)} %get-tuple-element.53), channel_id=1, source_target_pairs={{0,16},{16,32},{32,48},{48,64},{64,80},{80,96},{96,112},{112,0},{1... | collective-permute-start | bytes 196616 | tf_op jit(solution)/shard_map/ppermute | solution.py:31
  32.3 3.7 %collective-permute-start.1 = (f32[1,2,16,1,512]{4,3,2,1,0:T(1,128)S(1)}, f32[1,2,16,1,512]{4,3,2,1,0:T(1,128)S(1)}, u32[]{:S(2)}, u32[]{:S(2)}) collective-permute-start(f32[1,2,16,1,512]{4,3,2,1,0:T(1,128)S(1)} %get-tuple-element.54), channel_id=1, source_target_pairs={{16,0},{32,16},{48,32},{64,48},{80,64},{96,80},{112,96},{0,112},{1... | collective-permute-start | bytes 196616 | tf_op jit(solution)/shard_map/ppermute | solution.py:34
  32.4 70.0 %copy-start.5 = (f32[8,512]{1,0:T(8,128)}, f32[8,512]{1,0:T(8,128)S(1)}, u32[]{:S(2)}) copy-start(f32[8,512]{1,0:T(8,128)S(1)} %get-tuple-element.66) | copy-start | bytes 49156
  36.2 11.6 %collective-permute-start.2 = (f32[1,2,16,10,1]{4,3,2,1,0:T(8,128)S(1)}, f32[1,2,16,10,1]{4,3,2,1,0:T(8,128)S(1)}, u32[]{:S(2)}, u32[]{:S(2)}) collective-permute-start(f32[1,2,16,10,1]{4,3,2,1,0:T(8,128)S(1)} %get-tuple-element.47), channel_id=1, source_target_pairs={{0,1},{1,2},{2,3},{3,4},{4,5},{5,6},{6,7},{7,8},{8,9},{9,10},{10,1... | collective-permute-start | bytes 3848 | tf_op jit(solution)/shard_map/ppermute | solution.py:31
  36.3 11.5 %collective-permute-start.3 = (f32[1,2,16,10,1]{4,3,2,1,0:T(8,128)S(1)}, f32[1,2,16,10,1]{4,3,2,1,0:T(8,128)S(1)}, u32[]{:S(2)}, u32[]{:S(2)}) collective-permute-start(f32[1,2,16,10,1]{4,3,2,1,0:T(8,128)S(1)} %get-tuple-element.48), channel_id=1, source_target_pairs={{1,0},{2,1},{3,2},{4,3},{5,4},{6,5},{7,6},{8,7},{9,8},{10,9},{11,1... | collective-permute-start | bytes 3848 | tf_op jit(solution)/shard_map/ppermute | solution.py:34
  50.1 2.0 %collective-permute-start.4 = (f32[2,2,16,1,512]{4,3,2,1,0:T(1,128)S(1)}, f32[2,2,16,1,512]{4,3,2,1,0:T(1,128)S(1)}, u32[]{:S(2)}, u32[]{:S(2)}) collective-permute-start(f32[2,2,16,1,512]{4,3,2,1,0:T(1,128)S(1)} %get-tuple-element.45), channel_id=1, source_target_pairs={{0,16},{16,32},{32,48},{48,64},{64,80},{80,96},{96,112},{112,0},{1... | collective-permute-start | bytes 393224 | tf_op jit(solution)/shard_map/ppermute | solution.py:31
  50.1 4.7 %collective-permute-start.5 = (f32[2,2,16,1,512]{4,3,2,1,0:T(1,128)S(1)}, f32[2,2,16,1,512]{4,3,2,1,0:T(1,128)S(1)}, u32[]{:S(2)}, u32[]{:S(2)}) collective-permute-start(f32[2,2,16,1,512]{4,3,2,1,0:T(1,128)S(1)} %get-tuple-element.46), channel_id=1, source_target_pairs={{16,0},{32,16},{48,32},{64,48},{80,64},{96,80},{112,96},{0,112},{1... | collective-permute-start | bytes 393224 | tf_op jit(solution)/shard_map/ppermute | solution.py:34
  55.2 16.4 %collective-permute-start.6 = (f32[2,2,16,10,1]{4,3,2,1,0:T(8,128)S(1)}, f32[2,2,16,10,1]{4,3,2,1,0:T(8,128)S(1)}, u32[]{:S(2)}, u32[]{:S(2)}) collective-permute-start(f32[2,2,16,10,1]{4,3,2,1,0:T(8,128)S(1)} %get-tuple-element.32), channel_id=1, source_target_pairs={{0,1},{1,2},{2,3},{3,4},{4,5},{5,6},{6,7},{7,8},{8,9},{9,10},{10,1... | collective-permute-start | bytes 7688 | tf_op jit(solution)/shard_map/ppermute | solution.py:31
  55.3 16.3 %collective-permute-start.7 = (f32[2,2,16,10,1]{4,3,2,1,0:T(8,128)S(1)}, f32[2,2,16,10,1]{4,3,2,1,0:T(8,128)S(1)}, u32[]{:S(2)}, u32[]{:S(2)}) collective-permute-start(f32[2,2,16,10,1]{4,3,2,1,0:T(8,128)S(1)} %get-tuple-element.33), channel_id=1, source_target_pairs={{1,0},{2,1},{3,2},{4,3},{5,4},{6,5},{7,6},{8,7},{9,8},{10,9},{11,1... | collective-permute-start | bytes 7688 | tf_op jit(solution)/shard_map/ppermute | solution.py:34
  77.5 2.7 %collective-permute-start.8 = (f32[2,2,16,1,512]{4,3,2,1,0:T(1,128)S(1)}, f32[2,2,16,1,512]{4,3,2,1,0:T(1,128)S(1)}, u32[]{:S(2)}, u32[]{:S(2)}) collective-permute-start(f32[2,2,16,1,512]{4,3,2,1,0:T(1,128)S(1)} %get-tuple-element.43), channel_id=1, source_target_pairs={{0,16},{16,32},{32,48},{48,64},{64,80},{80,96},{96,112},{112,0},{1... | collective-permute-start | bytes 393224 | tf_op jit(solution)/shard_map/ppermute | solution.py:31
  77.6 4.4 %collective-permute-start.9 = (f32[2,2,16,1,512]{4,3,2,1,0:T(1,128)S(1)}, f32[2,2,16,1,512]{4,3,2,1,0:T(1,128)S(1)}, u32[]{:S(2)}, u32[]{:S(2)}) collective-permute-start(f32[2,2,16,1,512]{4,3,2,1,0:T(1,128)S(1)} %get-tuple-element.44), channel_id=1, source_target_pairs={{16,0},{32,16},{48,32},{64,48},{80,64},{96,80},{112,96},{0,112},{1... | collective-permute-start | bytes 393224 | tf_op jit(solution)/shard_map/ppermute | solution.py:34
  82.4 15.3 %collective-permute-start.10 = (f32[2,2,16,10,1]{4,3,2,1,0:T(8,128)S(1)}, f32[2,2,16,10,1]{4,3,2,1,0:T(8,128)S(1)}, u32[]{:S(2)}, u32[]{:S(2)}) collective-permute-start(f32[2,2,16,10,1]{4,3,2,1,0:T(8,128)S(1)} %get-tuple-element.30), channel_id=1, source_target_pairs={{0,1},{1,2},{2,3},{3,4},{4,5},{5,6},{6,7},{7,8},{8,9},{9,10},{10,1... | collective-permute-start | bytes 7688 | tf_op jit(solution)/shard_map/ppermute | solution.py:31
  82.5 15.2 %collective-permute-start.11 = (f32[2,2,16,10,1]{4,3,2,1,0:T(8,128)S(1)}, f32[2,2,16,10,1]{4,3,2,1,0:T(8,128)S(1)}, u32[]{:S(2)}, u32[]{:S(2)}) collective-permute-start(f32[2,2,16,10,1]{4,3,2,1,0:T(8,128)S(1)} %get-tuple-element.31), channel_id=1, source_target_pairs={{1,0},{2,1},{3,2},{4,3},{5,4},{6,5},{7,6},{8,7},{9,8},{10,9},{11,1... | collective-permute-start | bytes 7688 | tf_op jit(solution)/shard_map/ppermute | solution.py:34
  103.2 4.2 %copy-start.6 = (f32[2,8,4,128]{3,1,2,0:T(8,128)S(1)}, f32[2,8,4,128]{3,1,2,0:T(8,128)}, u32[]{:S(2)}) copy-start(f32[2,8,4,128]{3,1,2,0:T(8,128)} %get-tuple-element.55) | copy-start | bytes 98308
  104.3 6.4 %collective-permute-start.12 = (f32[2,2,16,1,512]{4,3,2,1,0:T(1,128)}, f32[2,2,16,1,512]{4,3,2,1,0:T(1,128)}, u32[]{:S(2)}, u32[]{:S(2)}) collective-permute-start(f32[2,2,16,1,512]{4,3,2,1,0:T(1,128)} %get-tuple-element.41), channel_id=1, source_target_pairs={{0,16},{16,32},{32,48},{48,64},{64,80},{80,96},{96,112},{112,0},{1... | collective-permute-start | bytes 393224 | tf_op jit(solution)/shard_map/ppermute | solution.py:31
  105.0 5.7 %collective-permute-start.13 = (f32[2,2,16,1,512]{4,3,2,1,0:T(1,128)}, f32[2,2,16,1,512]{4,3,2,1,0:T(1,128)}, u32[]{:S(2)}, u32[]{:S(2)}) collective-permute-start(f32[2,2,16,1,512]{4,3,2,1,0:T(1,128)} %get-tuple-element.42), channel_id=1, source_target_pairs={{16,0},{32,16},{48,32},{64,48},{80,64},{96,80},{112,96},{0,112},{1... | collective-permute-start | bytes 393224 | tf_op jit(solution)/shard_map/ppermute | solution.py:34
  109.7 8.3 %copy-start.4 = (f32[1,16,8,4,128]{4,3,2,1,0:T(4,128)S(1)}, f32[1,16,8,4,128]{4,3,2,1,0:T(4,128)}, u32[]{:S(2)}) copy-start(f32[1,16,8,4,128]{4,3,2,1,0:T(4,128)} %stack.135) | copy-start | bytes 786436
  112.8 14.7 %collective-permute-start.14 = (f32[2,2,16,10,1]{4,3,2,1,0:T(8,128)}, f32[2,2,16,10,1]{4,3,2,1,0:T(8,128)}, u32[]{:S(2)}, u32[]{:S(2)}) collective-permute-start(f32[2,2,16,10,1]{4,3,2,1,0:T(8,128)} %get-tuple-element.28), channel_id=1, source_target_pairs={{0,1},{1,2},{2,3},{3,4},{4,5},{5,6},{6,7},{7,8},{8,9},{9,10},{10,1... | collective-permute-start | bytes 7688 | tf_op jit(solution)/shard_map/ppermute | solution.py:31
  112.8 14.7 %collective-permute-start.15 = (f32[2,2,16,10,1]{4,3,2,1,0:T(8,128)}, f32[2,2,16,10,1]{4,3,2,1,0:T(8,128)}, u32[]{:S(2)}, u32[]{:S(2)}) collective-permute-start(f32[2,2,16,10,1]{4,3,2,1,0:T(8,128)} %get-tuple-element.29), channel_id=1, source_target_pairs={{1,0},{2,1},{3,2},{4,3},{5,4},{6,5},{7,6},{8,7},{9,8},{10,9},{11,1... | collective-permute-start | bytes 7688 | tf_op jit(solution)/shard_map/ppermute | solution.py:34
  118.0 9.6 %copy-start.1 = (f32[2,16,8,4,128]{4,3,2,1,0:T(4,128)}, f32[2,16,8,4,128]{4,3,2,1,0:T(4,128)S(1)}, u32[]{:S(2)}) copy-start(f32[2,16,8,4,128]{4,3,2,1,0:T(4,128)S(1)} %constant_dynamic-update-slice_fusion) | copy-start | bytes 1572868
  132.5 3.4 %copy-start.2 = (f32[2,16,8,4,128]{4,3,2,1,0:T(4,128)S(1)}, f32[2,16,8,4,128]{4,3,2,1,0:T(4,128)}, u32[]{:S(2)}) copy-start(f32[2,16,8,4,128]{4,3,2,1,0:T(4,128)} %copy-done.1) | copy-start | bytes 1572868
  132.5 3.4 %copy-start.3 = (f32[1,16,8,4,128]{4,3,2,1,0:T(4,128)S(1)}, f32[1,16,8,4,128]{4,3,2,1,0:T(4,128)}, u32[]{:S(2)}) copy-start(f32[1,16,8,4,128]{4,3,2,1,0:T(4,128)} %stack.146) | copy-start | bytes 786436
where the time goes:
time: 178 us; the launch traced here: 174 us
  waiting for transfers between devices  58.9 us (33%)
  starting transfers between devices  38.9 us (22%)
  blocking collectives  34.2 us (19%)
  other arithmetic  29.2 us (16%)
  local copies, waits for them, and re-layouts  10.7 us (6%)
    ppermute x8, waiting for transfers between devices, extended(): lax.ppermute(lax.slice_in_dim(block, block.shape[dim] - width, None, axis...  36.7 us
    psum x4, blocking collectives, one_axis_at_a_time(): array = lax.psum(array, axis)  34.2 us
    ppermute x8, starting transfers between devices, extended(): lax.ppermute(lax.slice_in_dim(block, 0, width, axis=dim), axis, backward)  26.1 us
    all_to_all x1, waiting for transfers between devices, local(): lax.all_to_all(outgoing, GY, split_axis=0, concat_axis=0, tiled=True)  15.3 us
    concatenate x4, other arithmetic, extended(): block = jnp.concatenate([low, block, high], axis=dim)  7.79 us
    all_to_all x1, starting transfers between devices, local(): lax.all_to_all(outgoing, GY, split_axis=0, concat_axis=0, tiled=True)  7.72 us
    mul x8, other arithmetic, hamilton(): out_real.append(result_real * factor)  7.04 us
    ppermute x8, waiting for transfers between devices, extended(): lax.ppermute(lax.slice_in_dim(block, 0, width, axis=dim), axis, backward)  6.92 us
  transfers between devices with their start and end apart: 17, of which 11 were waited for; matrix products, arithmetic and copies ran while one was open for 4% of the time, Pallas kernels for 0%

commit v1 on v0

v1 whole, which is shorter than its diff:
```python
import functools

import jax
import jax.numpy as jnp
from jax import lax
from jax.experimental import pallas as pl
from jax.experimental.pallas import tpu as pltpu
from jax.sharding import PartitionSpec as P

BLOCK = 128
R = 16
TERMS = 4
HALO = 4
BLOCKS = 4
LANES = BLOCK * (BLOCKS + 1)
OWN = BLOCK * BLOCKS
WIDTH_X = 8
ROWS_X = WIDTH_X + 2 * HALO
SLOT = 2 * WIDTH_X * R
EDGE = SLOT
SITE_EDGE = SLOT + 16
SLOT_ROWS = SLOT + 32
HALF = 2 * HALO * R
PLANES = HALF + 16
MESSAGE = HALF + 16 + 4 * 2 * HALO

HOP_NEXT = 0.3
TWIST_COS = 0.4535961214255773
TWIST_SIN = 0.8912073600614354
SPREAD = 6.5
COS = HOP_NEXT * TWIST_COS
SIN = HOP_NEXT * TWIST_SIN
F32 = jnp.float32
BF16 = jnp.bfloat16


def site_planes(onsite, keep):
    high = onsite.astype(BF16).astype(F32)
    rest = onsite - high
    middle = rest.astype(BF16).astype(F32)
    low = (rest - middle).astype(BF16).astype(F32)
    return high, middle, low, keep


def lane_index(rows, lanes):
    return lax.broadcasted_iota(jnp.int32, (rows, lanes), 1)


def pack_kernel(columns, plan, stored, disorder, vacancy, out, turned, where_to):
    me = lax.axis_index("gy")
    first = me * BLOCKS

    def find(k, carry):
        held = plan[k] - first
        spot = jnp.where((held >= 0) & (held < BLOCKS), held, BLOCKS)
        where_to[spot] = k
        return carry

    lax.fori_loop(0, BLOCKS * columns, find, 0, unroll=8)

    for b in range(BLOCKS):
        block = stored[:, :, :, b * BLOCK : (b + 1) * BLOCK]
        turned[b] = block.reshape(2 * R * WIDTH_X, BLOCK).astype(F32)
    lane = lane_index(8, BLOCK)
    edges = [[jnp.zeros((8, BLOCK), F32) for _ in range(2)] for _ in range(BLOCKS)]
    slots = [where_to[b] // BLOCKS for b in range(BLOCKS)]
    for s in range(2):
        for x in range(WIDTH_X):
            q = s * WIDTH_X + x
            for b in range(BLOCKS):
                parts = []
                for h in range(2):
                    base = s * R * WIDTH_X + h * 8 * WIDTH_X + x
                    rows = turned[b, pl.ds(base, 8, stride=WIDTH_X), :]
                    parts.append(rows)
                    moved = pltpu.roll(rows, (8 * q + 4) % BLOCK, 1)
                    edges[b][h] = jnp.where(lane // 8 == q, moved, edges[b][h])
                both = jnp.concatenate(parts, axis=0).astype(BF16)
                out[slots[b], q * R : (q + 1) * R, :] = both
    last_half = lane_index(R, BLOCK) % 8 < 4
    for b in range(BLOCKS):
        spot = where_to[b]
        edge = jnp.concatenate(edges[b], axis=0)

        @pl.when(spot % BLOCKS == BLOCKS - 1)
        def _():
            slot = ((spot + 1) // BLOCKS) % columns
            old = out[slot, EDGE : EDGE + R, :].astype(F32)
            out[slot, EDGE : EDGE + R, :] = jnp.where(last_half, edge, old).astype(BF16)

        @pl.when(spot % BLOCKS == 0)
        def _():
            slot = (spot // BLOCKS + columns - 1) % columns
            old = out[slot, EDGE : EDGE + R, :].astype(F32)
            out[slot, EDGE : EDGE + R, :] = jnp.where(last_half, old, edge).astype(BF16)

    lane16 = lane_index(R, BLOCK)
    ends = []
    for ref in (disorder, vacancy):
        low = ref[:, :, 0:BLOCK].reshape(R, BLOCK).astype(F32)
        high = ref[:, :, OWN - BLOCK : OWN].reshape(R, BLOCK).astype(F32)
        ends.append(jnp.where(lane16 < BLOCK // 2, low, high))
    sites = jnp.zeros((R, BLOCK), F32)
    for p, plane in enumerate(site_planes(ends[0], ends[1])):
        sites = jnp.where(lane16 // 8 == p, pltpu.roll(plane, 8 * p + 4, 1), sites)
    sites = sites.astype(BF16)
    out[(me + 1) % columns, SITE_EDGE : SITE_EDGE + R, :] = sites
    out[(me + columns - 1) % columns, SITE_EDGE : SITE_EDGE + R, :] = sites


def edge_tiles(columns, plan, received):
    me = lax.axis_index("gy")
    total = BLOCKS * columns
    left = plan[(me * BLOCKS + total - 1) % total] // BLOCKS
    right = plan[(me * BLOCKS + BLOCKS) % total] // BLOCKS
    last_half = lane_index(R, BLOCK) % 8 < 4
    tile = jnp.where(
        last_half,
        received[left, EDGE : EDGE + R, :].astype(F32),
        received[right, EDGE : EDGE + R, :].astype(F32),
    )
    low = (me + columns - 1) % columns
    high = (me + 1) % columns
    sites = jnp.where(
        last_half,
        received[low, SITE_EDGE : SITE_EDGE + R, :].astype(F32),
        received[high, SITE_EDGE : SITE_EDGE + R, :].astype(F32),
    )
    return tile, sites


def arrange_kernel(columns, plan, received, disorder, vacancy, low_out, high_out, rows):
    me = lax.axis_index("gy")
    for b in range(BLOCKS):
        slot = plan[me * BLOCKS + b] // BLOCKS
        lanes = slice(b * BLOCK, (b + 1) * BLOCK)
        for s in range(2):
            base = s * WIDTH_X * R
            size = HALO * R
            low_out[s * size : (s + 1) * size, lanes] = received[slot, base : base + size, :]
            high_out[s * size : (s + 1) * size, lanes] = received[
                slot, base + (WIDTH_X - HALO) * R : base + WIDTH_X * R, :
            ]
    tile, sites = edge_tiles(columns, plan, received)
    for out in (low_out, high_out):
        out[HALF : HALF + R, 0:BLOCK] = tile.astype(BF16)
        out[HALF : HALF + R, BLOCK : 2 * BLOCK] = sites.astype(BF16)
        out[HALF : HALF + R, 2 * BLOCK : OWN] = jnp.zeros((R, OWN - 2 * BLOCK), BF16)
    for s in range(2):
        for p, plane in enumerate(site_planes(disorder[s], vacancy[s].astype(F32))):
            rows[0, p * 8 + s * HALO : p * 8 + (s + 1) * HALO, :] = plane[0:HALO]
            rows[1, p * 8 + s * HALO : p * 8 + (s + 1) * HALO, :] = plane[WIDTH_X - HALO :]
    low_out[PLANES:MESSAGE, :] = rows[0].astype(BF16)
    high_out[PLANES:MESSAGE, :] = rows[1].astype(BF16)


def shift_up(field):
    return pltpu.roll(field, LANES - 1, 1)


def shift_down(field):
    return pltpu.roll(field, 1, 1)


def chebyshev_kernel(
    columns, plan, received, below, above, disorder, vacancy,
    local_out, trace_out,
    level, keep, factor, start, real1, imag1, real2, imag2, real3, imag3, sums,
):
    me = lax.axis_index("gy")
    tile, sites = edge_tiles(columns, plan, received)
    lane8 = lane_index(8, BLOCK)
    in_halo = (lane8 < HALO) | (lane8 >= BLOCK - HALO)

    def unpack_sites(s, rows, onsite, kept, source, x_of):
        side_level = jnp.zeros((8, BLOCK), F32)
        for p in range(3):
            side_level = side_level + pltpu.roll(source, BLOCK - 4 - 8 * p, 1)
        side_keep = pltpu.roll(source, BLOCK - 4 - 8 * 3, 1)
        side_level = jnp.where(in_halo, side_level, 0.0)
        side_keep = jnp.where(in_halo, side_keep, 0.0)
        for i, row in enumerate(rows):
            j = x_of(i)
            lev = jnp.concatenate([onsite[i : i + 1], side_level[j : j + 1]], axis=1)
            kep = jnp.concatenate([kept[i : i + 1], side_keep[j : j + 1]], axis=1)
            level[s, row] = jnp.broadcast_to(lev, (8, LANES))
            kep = jnp.broadcast_to(kep, (8, LANES))
            keep[s, row] = kep
            factor[s, row] = kep * (1.0 / SPREAD)

    for s in range(2):
        unpack_sites(
            s, range(HALO, HALO + WIDTH_X), disorder[s], vacancy[s].astype(F32),
            sites[s * 8 : (s + 1) * 8], lambda i: i,
        )
    for ref, rows, shift in (
        (below, range(0, HALO), WIDTH_X - HALO),
        (above, range(HALO + WIDTH_X, ROWS_X), 0),
    ):
        planes = [ref[PLANES + p * 8 : PLANES + (p + 1) * 8, :].astype(F32) for p in range(4)]
        onsite = planes[0] + planes[1] + planes[2]
        far = ref[HALF : HALF + R, BLOCK : 2 * BLOCK].astype(F32)
        for s in range(2):
            part = slice(s * HALO, (s + 1) * HALO)
            unpack_sites(
                s, rows, onsite[part], planes[3][part], far[s * 8 : (s + 1) * 8],
                lambda i, shift=shift: i + shift,
            )

    def put_start(s, row, lanes, value):
        for h in range(2):
            start[s, row, h * 8 : (h + 1) * 8, lanes] = (
                value[h * 8 : (h + 1) * 8] * keep[s, row, :, lanes]
            )

    side = slice(OWN, LANES)
    for b in range(BLOCKS):
        slot = plan[me * BLOCKS + b] // BLOCKS
        for s in range(2):
            for x in range(WIDTH_X):
                q = s * WIDTH_X + x
                value = received[slot, q * R : (q + 1) * R, :].astype(F32)
                put_start(s, HALO + x, slice(b * BLOCK, (b + 1) * BLOCK), value)
    for s in range(2):
        for x in range(WIDTH_X):
            q = s * WIDTH_X + x
            put_start(s, HALO + x, side, pltpu.roll(tile, (BLOCK - 4 - 8 * q) % BLOCK, 1))
    for ref, base, shift in ((below, 0, WIDTH_X - HALO), (above, HALO + WIDTH_X, 0)):
        far = ref[HALF : HALF + R, 0:BLOCK].astype(F32)
        for s in range(2):
            for i in range(HALO):
                row = base + i
                index = (s * HALO + i) * R
                put_start(s, row, slice(0, OWN), ref[index : index + R, :].astype(F32))
                q = s * WIDTH_X + shift + i
                put_start(s, row, side, pltpu.roll(far, (BLOCK - 4 - 8 * q) % BLOCK, 1))

    def hamilton(real, imag, s, row, h, want_imag):
        part = slice(h * 8, (h + 1) * 8)
        sine = SIN if s == 0 else -SIN

        def get(ref, sub, r):
            return ref[sub, r, part, :]

        r_m, r_0, r_p = (get(real, s, row + d) for d in (-1, 0, 1))
        o_0 = get(real, 1 - s, row)
        o_s = get(real, 1 - s, row - 1 if s == 0 else row + 1)
        lev = level[s, row]
        if imag is None:
            out_r = COS * (r_p + r_m) + lev * r_0 - (o_0 + o_s)
            g0 = COS * (r_m + r_0)
            g1 = COS * (r_0 + r_p)
        else:
            i_m, i_0, i_p = (get(imag, s, row + d) for d in (-1, 0, 1))
            out_r = COS * (r_p + r_m) - sine * (i_p - i_m) + lev * r_0 - (o_0 + o_s)
            g0 = COS * (r_m + r_0) - sine * (i_m - i_0)
            g1 = COS * (r_0 + r_p) - sine * (i_0 - i_p)
        if s == 0:
            g1 = g1 - o_0
        else:
            g0 = g0 - o_0
        out_r = out_r + shift_up(g0) + shift_down(g1)
        if not want_imag:
            return out_r, None
        out_i = sine * (r_p - r_m)
        g0 = sine * (r_m - r_0)
        g1 = sine * (r_0 - r_p)
        if imag is not None:
            o_0 = get(imag, 1 - s, row)
            o_s = get(imag, 1 - s, row - 1 if s == 0 else row + 1)
            out_i = out_i + COS * (i_p + i_m) + lev * i_0 - (o_0 + o_s)
            g0 = g0 + COS * (i_m + i_0)
            g1 = g1 + COS * (i_0 + i_p)
            if s == 0:
                g1 = g1 - o_0
            else:
                g0 = g0 - o_0
        out_i = out_i + shift_up(g0) + shift_down(g1)
        return out_r, out_i

    fields = [(start, None), (real1, imag1), (real2, imag2), (real3, imag3)]

    for term in range(1, TERMS):
        real, imag = fields[term - 1]
        to_real, to_imag = fields[term]

        def body(row, carry, term=term, real=real, imag=imag, to_real=to_real, to_imag=to_imag):
            for h in range(2):
                part = slice(h * 8, (h + 1) * 8)
                for s in range(2):
                    out_r, out_i = hamilton(real, imag, s, row, h, True)
                    scale = factor[s, row]
                    if term == 1:
                        out_r, out_i = out_r * scale, out_i * scale
                    else:
                        scale = scale + scale
                        old_r, old_i = fields[term - 2]
                        out_r = out_r * scale - old_r[s, row, part, :]
                        out_i = out_i * scale
                        if old_i is not None:
                            out_i = out_i - old_i[s, row, part, :]
                    to_real[s, row, part, :] = out_r
                    to_imag[s, row, part, :] = out_i
            return carry

        lax.fori_loop(term, ROWS_X - term, body, 0)

    sums[...] = jnp.zeros_like(sums)

    def finish(x, carry):
        row = x + HALO
        own = slice(0, OWN)
        for s in range(2):
            totals = [None] * TERMS
            for h in range(2):
                part = slice(h * 8, (h + 1) * 8)
                v0 = start[s, row, part, own]
                out_r, _ = hamilton(real3, imag3, s, row, h, False)
                scale = factor[s, row]
                v4 = out_r * (scale + scale) - real2[s, row, part, :]
                values = [ref[s, row, part, own] for ref in (real1, real2, real3)]
                values.append(v4[:, own])
                for n, value in enumerate(values):
                    product = v0 * value
                    totals[n] = product if h == 0 else totals[n] + product
                    lanes = product[:, 0:BLOCK]
                    for b in range(1, BLOCKS):
                        lanes = lanes + product[:, b * BLOCK : (b + 1) * BLOCK]
                    sums[n * R + h * 8 : n * R + (h + 1) * 8, :] += lanes
            for n in range(TERMS):
                local_out[n, s, pl.ds(x, 1), :] = (
                    jnp.sum(totals[n], axis=0, keepdims=True) * (1.0 / R)
                )
        return carry

    lax.fori_loop(0, WIDTH_X, finish, 0)
    trace_out[...] = lax.dot_general(
        jnp.ones(trace_out.shape[:1] + (BLOCK,), F32), sums[...],
        (((1,), (1,)), ((), ())),
        precision=lax.Precision.HIGHEST, preferred_element_type=F32,
    )


def local(stored_vectors, disorder, vacancy, plan):
    columns = lax.axis_size("gy")
    rows = lax.axis_size("gx")
    devices = rows * columns
    smem = pl.BlockSpec(memory_space=pltpu.SMEM)
    vmem = pl.BlockSpec(memory_space=pltpu.VMEM)
    params = pltpu.CompilerParams(vmem_limit_bytes=48 * 1024 * 1024)

    outgoing = pl.pallas_call(
        functools.partial(pack_kernel, columns),
        out_shape=jax.ShapeDtypeStruct((columns, SLOT_ROWS, BLOCK), BF16),
        in_specs=[smem, vmem, vmem, vmem],
        out_specs=vmem,
        scratch_shapes=[
            pltpu.VMEM((BLOCKS, 2 * R * WIDTH_X, BLOCK), F32),
            pltpu.SMEM((BLOCKS + 1,), jnp.int32),
        ],
        compiler_params=params,
        name="pack",
    )(plan, stored_vectors, disorder, vacancy)
    received = lax.all_to_all(outgoing, "gy", split_axis=0, concat_axis=0, tiled=True)

    message = jax.ShapeDtypeStruct((MESSAGE, OWN), BF16)
    low_rows, high_rows = pl.pallas_call(
        functools.partial(arrange_kernel, columns),
        out_shape=(message, message),
        in_specs=[smem, vmem, vmem, vmem],
        out_specs=(vmem, vmem),
        scratch_shapes=[pltpu.VMEM((2, 4 * 2 * HALO, OWN), F32)],
        compiler_params=params,
        name="arrange",
    )(plan, received, disorder, vacancy)
    up = [(i, (i + 1) % rows) for i in range(rows)]
    down = [(target, source) for source, target in up]
    below = lax.ppermute(high_rows, "gx", up)
    above = lax.ppermute(low_rows, "gx", down)

    site = pltpu.VMEM((2, ROWS_X, 8, LANES), F32)
    field = pltpu.VMEM((2, ROWS_X, R, LANES), F32)
    local_moments, partial = pl.pallas_call(
        functools.partial(chebyshev_kernel, columns),
        out_shape=(
            jax.ShapeDtypeStruct((TERMS, 2, WIDTH_X, OWN), F32),
            jax.ShapeDtypeStruct((devices, TERMS * R), F32),
        ),
        in_specs=[smem, vmem, vmem, vmem, vmem, vmem],
        out_specs=(vmem, vmem),
        scratch_shapes=[site, site, site] + [field] * 7 + [pltpu.VMEM((TERMS * R, BLOCK), F32)],
        compiler_params=params,
        name="chebyshev",
    )(plan, received, below, above, disorder, vacancy)

    shared = lax.all_to_all(partial, ("gx", "gy"), split_axis=0, concat_axis=0, tiled=True)
    sites = 2 * WIDTH_X * rows * OWN * columns
    trace = jnp.sum(shared, axis=0).reshape(TERMS, R) * (1.0 / sites)
    return local_moments, trace


def solution(mesh):
    placed = (P(None, None, "gx", "gy"), P(None, "gx", "gy"), P(None, "gx", "gy"), P())
    return jax.shard_map(
        local, mesh=mesh, in_specs=placed,
        out_specs=(P(None, None, "gx", "gy"), P()), check_vma=False,
    )
```

time: 178 us -> 63.8 us (0.36); the launches traced: 174 us -> 63.4 us
  waiting for transfers between devices: 58.9 us -> 4.92 us
  starting transfers between devices: 38.9 us -> 3.63 us
  other arithmetic: 29.2 us -> 0.16 us
  Pallas kernels: 0 us -> 10.2 us
  local copies, waits for them, and re-layouts: 10.7 us -> 3.78 us
  blocking collectives: 34.2 us -> 40.1 us
    all_to_all x0 -> x2, blocking collectives: none -> 40.1 us  [the longest x1 24.8 us: local(): lax.all_to_all(outgoing, 'gy', split_axis=0, concat_axis=0, tiled=True)]
    ppermute x16 -> x2, waiting for transfers between devices: 43.6 us -> 4.92 us  [the longest x1 2.48 us: local(): above = lax.ppermute(low_rows, 'gx', down)]
    psum x4 -> x0, blocking collectives: 34.2 us -> none  [one_axis_at_a_time(): array = lax.psum(array, axis)]
    ppermute x16 -> x2, starting transfers between devices: 31.2 us -> 3.63 us  [the longest x1 3.63 us: local(): below = lax.ppermute(high_rows, 'gx', up)]
    all_to_all x1 -> x0, waiting for transfers between devices: 15.3 us -> none  [local(): lax.all_to_all(outgoing, GY, split_axis=0, concat_axis=0, tiled=True)]
    pallas_call x0 -> x3, Pallas kernels: none -> 10.2 us  [the longest x1 8.44 us: local(): pl.pallas_call(functools.partial(chebyshev_kernel, columns), out_shape=(j...]
    concatenate x4 -> x0, other arithmetic: 7.79 us -> none  [extended(): block = jnp.concatenate([low, block, high], axis=dim)]
    mul x12 -> x1, other arithmetic: 7.75 us -> 0.01 us  [local(): trace = jnp.sum(shared, axis=0).reshape(TERMS, R) * (1.0 / sites)]
  transfers between devices with their start and end apart: 17 -> 2, of which waited for: 11 -> 2; matrix products, arithmetic and copies ran while one was open for 4% -> 0% of each run, Pallas kernels for 0% -> 0%
where the time goes in v1:
time: 63.8 us; the launch traced here: 63.4 us
  blocking collectives  40.1 us (63%)
  Pallas kernels  10.2 us (16%)
  waiting for transfers between devices  4.92 us (8%)
  local copies, waits for them, and re-layouts  3.78 us (6%)
  starting transfers between devices  3.63 us (6%)
  between operations  0.65 us (1%)
    all_to_all x1, blocking collectives, local(): lax.all_to_all(outgoing, 'gy', split_axis=0, concat_axis=0, tiled=True)  24.8 us
    all_to_all x1, blocking collectives, local(): lax.all_to_all(partial, ('gx', 'gy'), split_axis=0, concat_axis=0, tiled=...  15.3 us
    pallas_call x1, Pallas kernels, local(): pl.pallas_call(functools.partial(chebyshev_kernel, columns), out_shape=(j...  8.44 us
    ppermute x1, starting transfers between devices, local(): below = lax.ppermute(high_rows, 'gx', up)  3.63 us
    unnamed x8, local copies, waits for them, and re-layouts  3.11 us
    ppermute x1, waiting for transfers between devices, local(): above = lax.ppermute(low_rows, 'gx', down)  2.48 us
    ppermute x1, waiting for transfers between devices, local(): below = lax.ppermute(high_rows, 'gx', up)  2.44 us
  transfers between devices with their start and end apart: 2, of which 2 were waited for; matrix products, arithmetic and copies ran while one was open for 0% of the time, Pallas kernels for 0%

profile of v1, /device:TPU:1, one launch (start us, length us, event | category | flops | bytes accessed | tf_op | source)
XLA Modules:
  0.0 63.4 jit_solution(8286968349183874404)
XLA Ops:
  0.6 0.0 copy-start
  0.6 0.7 %copy-done = f32[2,8,512]{2,1,0:T(8,128)S(1)} copy-done((f32[2,8,512]{2,1,0:T(8,128)S(1)}, f32[2,8,512]{2,1,0:T(8,128)}, u32[]{:S(2)}) %copy-start) | copy-done | bytes 32792
  1.4 0.0 copy-start.1
  1.4 0.8 %copy-done.1 = s32[2,8,512]{2,1,0:T(8,128)S(1)} copy-done((s32[2,8,512]{2,1,0:T(8,128)S(1)}, s32[2,8,512]{2,1,0:T(8,128)}, u32[]{:S(2)}) %copy-start.1) | copy-done | bytes 32792
  2.1 0.0 copy-start.2
  2.1 0.9 %copy-done.2 = bf16[2,16,8,512]{3,2,1,0:T(8,128)(2,1)S(1)} copy-done((bf16[2,16,8,512]{3,2,1,0:T(8,128)(2,1)S(1)}, bf16[2,16,8,512]{3,2,1,0:T(8,128)(2,1)}, u32[]{:S(2)}) %copy-start.2) | copy-done | bytes 262168
  3.1 0.0 copy-start.3
  3.1 0.7 %copy-done.3 = s32[64]{0:T(128)S(1)} copy-done((s32[64]{0:T(128)S(1)}, s32[64]{0:T(128)}, u32[]{:S(2)}) %copy-start.3) | copy-done | bytes 280
  3.8 1.1 %pack.1 = bf16[16,288,128]{2,1,0:T(8,128)(2,1)S(1)} custom-call(s32[64]{0:T(128)S(1)} %copy-done.3, bf16[2,16,8,512]{3,2,1,0:T(8,128)(2,1)S(1)} %copy-done.2, f32[2,8,512]{2,1,0:T(8,128)S(1)} %copy-done, s32[2,8,512]{2,1,0:T(8,128)S(1)} %copy-done.1), custom_call_target="tpu_custom_call" | custom-call | tf_op jit(solution)/shard_map/pack/pallas_call | solution.py:352
  4.9 24.8 %all_to_all.14.received = bf16[16,288,128]{2,1,0:T(8,128)(2,1)S(1)} all-to-all(bf16[16,288,128]{2,1,0:T(8,128)(2,1)S(1)} %pack.1), channel_id=1, replica_groups=mesh['gx'=8,'gy'=16] {'gy'}, dimensions={0} | all-to-all | bytes 2359296 | tf_op jit(solution)/shard_map/all_to_all | solution.py:364
  29.7 0.6 %arrange.1 = (bf16[176,512]{1,0:T(8,128)(2,1)S(1)}, bf16[176,512]{1,0:T(8,128)(2,1)S(1)}) custom-call(s32[64]{0:T(128)S(1)} %copy-done.3, bf16[16,288,128]{2,1,0:T(8,128)(2,1)S(1)} %all_to_all.14.received, f32[2,8,512]{2,1,0:T(8,128)S(1)} %copy-done, s32[2,8,512]{2,1,0:T(8,128)S(1)} %copy-done.1), custom_call_target="tpu_custom_call" | custom-call | tf_op jit(solution)/shard_map/arrange/pallas_call | solution.py:367
  30.3 3.6 %collective-permute-start = (bf16[176,512]{1,0:T(8,128)(2,1)S(1)}, bf16[176,512]{1,0:T(8,128)(2,1)S(1)}, u32[]{:S(2)}, u32[]{:S(2)}) collective-permute-start(bf16[176,512]{1,0:T(8,128)(2,1)S(1)} %get-tuple-element.6), channel_id=1, source_target_pairs={{0,16},{16,32},{32,48},{48,64},{64,80},{80,96},{96,112},{112,0},{1... | collective-permute-start | bytes 540680 | tf_op jit(solution)/shard_map/ppermute | solution.py:378
  34.0 0.0 collective-permute-start.1
  34.0 2.4 %collective-permute-done.below = bf16[176,512]{1,0:T(8,128)(2,1)S(1)} collective-permute-done((bf16[176,512]{1,0:T(8,128)(2,1)S(1)}, bf16[176,512]{1,0:T(8,128)(2,1)S(1)}, u32[]{:S(2)}, u32[]{:S(2)}) %collective-permute-start) | collective-permute-done | bytes 180256 | tf_op jit(solution)/shard_map/ppermute | solution.py:378
  36.4 2.5 %collective-permute-done.1.above = bf16[176,512]{1,0:T(8,128)(2,1)S(1)} collective-permute-done((bf16[176,512]{1,0:T(8,128)(2,1)S(1)}, bf16[176,512]{1,0:T(8,128)(2,1)S(1)}, u32[]{:S(2)}, u32[]{:S(2)}) %collective-permute-start.1) | collective-permute-done | bytes 180256 | tf_op jit(solution)/shard_map/ppermute | solution.py:379
  38.9 8.4 %chebyshev.1 = (f32[4,2,8,512]{3,2,1,0:T(8,128)}, f32[128,64]{1,0:T(8,128)S(1)}) custom-call(s32[64]{0:T(128)S(1)} %copy-done.3, bf16[16,288,128]{2,1,0:T(8,128)(2,1)S(1)} %all_to_all.14.received, bf16[176,512]{1,0:T(8,128)(2,1)S(1)} %collective-permute-done.below, bf16[176,512]{1,0:T(8,128)(2,1)S(1)} %collective-permute-done.1.above, ...), custom_call_target="tpu_custom_call" | custom-call | tf_op jit(solution)/shard_map/chebyshev/pallas_call | solution.py:383
  47.3 15.3 %all_to_all.15 = f32[128,1,64]{2,1,0:T(1,128)S(1)} all-to-all(f32[128,1,64]{2,1,0:T(1,128)S(1)} %bitcast.3), channel_id=1, replica_groups=mesh['gx'=8,'gy'=16] {'gx','gy'}, dimensions={0} | all-to-all | bytes 65536 | tf_op jit(solution)/shard_map/all_to_all | solution.py:396
  62.6 0.2 reduce_sum.9
  62.8 0.7 %mul.11 = f32[4,16]{1,0:T(4,128)} reshape(f32[64]{0:T(128)S(1)} %broadcast_multiply_fusion) | data formatting | bytes 512 | tf_op jit(solution)/shard_map/mul | solution.py:398
  (1 shorter events, 0.0 us)
Async XLA Ops:
  0.6 0.8 %copy-start = (f32[2,8,512]{2,1,0:T(8,128)S(1)}, f32[2,8,512]{2,1,0:T(8,128)}, u32[]{:S(2)}) copy-start(f32[2,8,512]{2,1,0:T(8,128)} %disorder.5) | copy-start | bytes 98308
  1.4 0.8 %copy-start.1 = (s32[2,8,512]{2,1,0:T(8,128)S(1)}, s32[2,8,512]{2,1,0:T(8,128)}, u32[]{:S(2)}) copy-start(s32[2,8,512]{2,1,0:T(8,128)} %vacancy.5) | copy-start | bytes 98308
  2.1 0.9 %copy-start.2 = (bf16[2,16,8,512]{3,2,1,0:T(8,128)(2,1)S(1)}, bf16[2,16,8,512]{3,2,1,0:T(8,128)(2,1)}, u32[]{:S(2)}) copy-start(bf16[2,16,8,512]{3,2,1,0:T(8,128)(2,1)} %stored.1) | copy-start | bytes 786436
  3.1 0.7 %copy-start.3 = (s32[64]{0:T(128)S(1)}, s32[64]{0:T(128)}, u32[]{:S(2)}) copy-start(s32[64]{0:T(128)} %plan.5) | copy-start | bytes 772
  30.3 6.1 %collective-permute-start = (bf16[176,512]{1,0:T(8,128)(2,1)S(1)}, bf16[176,512]{1,0:T(8,128)(2,1)S(1)}, u32[]{:S(2)}, u32[]{:S(2)}) collective-permute-start(bf16[176,512]{1,0:T(8,128)(2,1)S(1)} %get-tuple-element.6), channel_id=1, source_target_pairs={{0,16},{16,32},{32,48},{48,64},{64,80},{80,96},{96,112},{112,0},{1... | collective-permute-start | bytes 540680 | tf_op jit(solution)/shard_map/ppermute | solution.py:378
  34.0 4.9 %collective-permute-start.1 = (bf16[176,512]{1,0:T(8,128)(2,1)S(1)}, bf16[176,512]{1,0:T(8,128)(2,1)S(1)}, u32[]{:S(2)}, u32[]{:S(2)}) collective-permute-start(bf16[176,512]{1,0:T(8,128)(2,1)S(1)} %get-tuple-element.7), channel_id=1, source_target_pairs={{16,0},{32,16},{48,32},{64,48},{80,64},{96,80},{112,96},{0,112},{1... | collective-permute-start | bytes 540680 | tf_op jit(solution)/shard_map/ppermute | solution.py:379

commit v2 on v1

v2 whole, which is shorter than its diff:
```python
import functools

import jax
import jax.numpy as jnp
from jax import lax
from jax.experimental import pallas as pl
from jax.experimental.pallas import tpu as pltpu
from jax.sharding import PartitionSpec as P

BLOCK = 128
R = 16
TERMS = 4
HALO = 4
BLOCKS = 4
LANES = BLOCK * (BLOCKS + 1)
OWN = BLOCK * BLOCKS
WIDTH_X = 8
ROWS_X = WIDTH_X + 2 * HALO
SLOT = 2 * WIDTH_X * R
EDGE = SLOT
SITE_EDGE = SLOT + 16
SLOT_ROWS = SLOT + 32
HALF = 2 * HALO * R
PLANES = HALF + 16
MESSAGE = HALF + 16 + 4 * 2 * HALO

HOP_NEXT = 0.3
TWIST_COS = 0.4535961214255773
TWIST_SIN = 0.8912073600614354
SPREAD = 6.5
COS = HOP_NEXT * TWIST_COS
SIN = HOP_NEXT * TWIST_SIN
F32 = jnp.float32
BF16 = jnp.bfloat16


def site_planes(onsite, keep):
    high = onsite.astype(BF16).astype(F32)
    rest = onsite - high
    middle = rest.astype(BF16).astype(F32)
    low = (rest - middle).astype(BF16).astype(F32)
    return high, middle, low, keep


def lane_index(rows, lanes):
    return lax.broadcasted_iota(jnp.int32, (rows, lanes), 1)


def pack_kernel(
    columns, plan_hbm, stored_hbm, disorder_hbm, vacancy_hbm, out,
    plan, stored, disorder, vacancy, turned, where_to, arrived,
):
    copies = [
        pltpu.make_async_copy(source, target, arrived.at[i])
        for i, (source, target) in enumerate(
            ((plan_hbm, plan), (stored_hbm, stored), (disorder_hbm, disorder), (vacancy_hbm, vacancy))
        )
    ]
    for copy in copies:
        copy.start()
    me = lax.axis_index("gy")
    first = me * BLOCKS
    copies[0].wait()

    def find(k, carry):
        held = plan[k] - first
        spot = jnp.where((held >= 0) & (held < BLOCKS), held, BLOCKS)
        where_to[spot] = k
        return carry

    lax.fori_loop(0, BLOCKS * columns, find, 0, unroll=8)

    copies[1].wait()
    for b in range(BLOCKS):
        block = stored[:, :, :, b * BLOCK : (b + 1) * BLOCK]
        turned[b] = block.reshape(2 * R * WIDTH_X, BLOCK).astype(F32)
    lane = lane_index(8, BLOCK)
    edges = [[jnp.zeros((8, BLOCK), F32) for _ in range(2)] for _ in range(BLOCKS)]
    slots = [where_to[b] // BLOCKS for b in range(BLOCKS)]
    for s in range(2):
        for x in range(WIDTH_X):
            q = s * WIDTH_X + x
            for b in range(BLOCKS):
                parts = []
                for h in range(2):
                    base = s * R * WIDTH_X + h * 8 * WIDTH_X + x
                    rows = turned[b, pl.ds(base, 8, stride=WIDTH_X), :]
                    parts.append(rows)
                    moved = pltpu.roll(rows, (8 * q + 4) % BLOCK, 1)
                    edges[b][h] = jnp.where(lane // 8 == q, moved, edges[b][h])
                both = jnp.concatenate(parts, axis=0).astype(BF16)
                out[slots[b], q * R : (q + 1) * R, :] = both
    last_half = lane_index(R, BLOCK) % 8 < 4
    for b in range(BLOCKS):
        spot = where_to[b]
        edge = jnp.concatenate(edges[b], axis=0)

        @pl.when(spot % BLOCKS == BLOCKS - 1)
        def _():
            slot = ((spot + 1) // BLOCKS) % columns
            old = out[slot, EDGE : EDGE + R, :].astype(F32)
            out[slot, EDGE : EDGE + R, :] = jnp.where(last_half, edge, old).astype(BF16)

        @pl.when(spot % BLOCKS == 0)
        def _():
            slot = (spot // BLOCKS + columns - 1) % columns
            old = out[slot, EDGE : EDGE + R, :].astype(F32)
            out[slot, EDGE : EDGE + R, :] = jnp.where(last_half, old, edge).astype(BF16)

    copies[2].wait()
    copies[3].wait()
    lane16 = lane_index(R, BLOCK)
    ends = []
    for ref in (disorder, vacancy):
        low = ref[:, :, 0:BLOCK].reshape(R, BLOCK).astype(F32)
        high = ref[:, :, OWN - BLOCK : OWN].reshape(R, BLOCK).astype(F32)
        ends.append(jnp.where(lane16 < BLOCK // 2, low, high))
    sites = jnp.zeros((R, BLOCK), F32)
    for p, plane in enumerate(site_planes(ends[0], ends[1])):
        sites = jnp.where(lane16 // 8 == p, pltpu.roll(plane, 8 * p + 4, 1), sites)
    sites = sites.astype(BF16)
    out[(me + 1) % columns, SITE_EDGE : SITE_EDGE + R, :] = sites
    out[(me + columns - 1) % columns, SITE_EDGE : SITE_EDGE + R, :] = sites


def edge_tiles(columns, plan, received):
    me = lax.axis_index("gy")
    total = BLOCKS * columns
    left = plan[(me * BLOCKS + total - 1) % total] // BLOCKS
    right = plan[(me * BLOCKS + BLOCKS) % total] // BLOCKS
    last_half = lane_index(R, BLOCK) % 8 < 4
    tile = jnp.where(
        last_half,
        received[left, EDGE : EDGE + R, :].astype(F32),
        received[right, EDGE : EDGE + R, :].astype(F32),
    )
    low = (me + columns - 1) % columns
    high = (me + 1) % columns
    sites = jnp.where(
        last_half,
        received[low, SITE_EDGE : SITE_EDGE + R, :].astype(F32),
        received[high, SITE_EDGE : SITE_EDGE + R, :].astype(F32),
    )
    return tile, sites


def arrange_kernel(columns, plan, received, disorder, vacancy, low_out, high_out, rows):
    me = lax.axis_index("gy")
    for b in range(BLOCKS):
        slot = plan[me * BLOCKS + b] // BLOCKS
        lanes = slice(b * BLOCK, (b + 1) * BLOCK)
        for s in range(2):
            base = s * WIDTH_X * R
            size = HALO * R
            low_out[s * size : (s + 1) * size, lanes] = received[slot, base : base + size, :]
            high_out[s * size : (s + 1) * size, lanes] = received[
                slot, base + (WIDTH_X - HALO) * R : base + WIDTH_X * R, :
            ]
    tile, sites = edge_tiles(columns, plan, received)
    for out in (low_out, high_out):
        out[HALF : HALF + R, 0:BLOCK] = tile.astype(BF16)
        out[HALF : HALF + R, BLOCK : 2 * BLOCK] = sites.astype(BF16)
        out[HALF : HALF + R, 2 * BLOCK : OWN] = jnp.zeros((R, OWN - 2 * BLOCK), BF16)
    for s in range(2):
        for p, plane in enumerate(site_planes(disorder[s], vacancy[s].astype(F32))):
            rows[0, p * 8 + s * HALO : p * 8 + (s + 1) * HALO, :] = plane[0:HALO]
            rows[1, p * 8 + s * HALO : p * 8 + (s + 1) * HALO, :] = plane[WIDTH_X - HALO :]
    low_out[PLANES:MESSAGE, :] = rows[0].astype(BF16)
    high_out[PLANES:MESSAGE, :] = rows[1].astype(BF16)


def fill_sites(level, factor, s, rows, onsite, kept, source, first):
    lane = lane_index(8, BLOCK)
    in_halo = (lane < HALO) | (lane >= BLOCK - HALO)
    side_level = jnp.zeros((8, BLOCK), F32)
    for p in range(3):
        side_level = side_level + pltpu.roll(source, BLOCK - 4 - 8 * p, 1)
    side_keep = pltpu.roll(source, BLOCK - 4 - 8 * 3, 1)
    side_level = jnp.where(in_halo, side_level, 0.0)
    side_keep = jnp.where(in_halo, side_keep, 0.0)
    kept_rows = []
    for i, row in enumerate(rows):
        j = first + i
        lev = jnp.concatenate([onsite[i : i + 1], side_level[j : j + 1]], axis=1)
        kep = jnp.concatenate([kept[i : i + 1], side_keep[j : j + 1]], axis=1)
        level[s, row] = jnp.broadcast_to(lev, (8, LANES))
        kep = jnp.broadcast_to(kep, (8, LANES))
        factor[s, row] = kep * (1.0 / SPREAD)
        kept_rows.append(kep)
    return kept_rows


def hamilton(level, real, imag, s, row, h, want_imag):
    part = slice(h * 8, (h + 1) * 8)
    sine = SIN if s == 0 else -SIN
    aside = row - 1 if s == 0 else row + 1
    r_m, r_0, r_p = (real[s, row + d, part, :] for d in (-1, 0, 1))
    o_0 = real[1 - s, row, part, :]
    near = o_0 + real[1 - s, aside, part, :]
    lev = level[s, row]
    out_r = COS * (r_p + r_m) + lev * r_0 - near
    g0 = COS * (r_m + r_0)
    g1 = COS * (r_0 + r_p)
    if imag is not None:
        i_m, i_0, i_p = (imag[s, row + d, part, :] for d in (-1, 0, 1))
        out_r = out_r - sine * (i_p - i_m)
        g0 = g0 - sine * (i_m - i_0)
        g1 = g1 - sine * (i_0 - i_p)
    if s == 0:
        g1 = g1 - o_0
    else:
        g0 = g0 - o_0
    out_r = out_r + pltpu.roll(g0, LANES - 1, 1) + pltpu.roll(g1, 1, 1)
    if not want_imag:
        return out_r, None
    out_i = sine * (r_p - r_m)
    g0 = sine * (r_m - r_0)
    g1 = sine * (r_0 - r_p)
    if imag is not None:
        o_0 = imag[1 - s, row, part, :]
        near = o_0 + imag[1 - s, aside, part, :]
        out_i = out_i + COS * (i_p + i_m) + lev * i_0 - near
        g0 = g0 + COS * (i_m + i_0)
        g1 = g1 + COS * (i_0 + i_p)
        if s == 0:
            g1 = g1 - o_0
        else:
            g0 = g0 - o_0
    out_i = out_i + pltpu.roll(g0, LANES - 1, 1) + pltpu.roll(g1, 1, 1)
    return out_r, out_i


def advance(term, level, factor, old, now, new, row):
    for h in range(2):
        part = slice(h * 8, (h + 1) * 8)
        for s in range(2):
            out_r, out_i = hamilton(level, now[0], now[1], s, row, h, True)
            scale = factor[s, row]
            if term == 1:
                out_r, out_i = out_r * scale, out_i * scale
            else:
                scale = scale + scale
                out_r = out_r * scale - old[0][s, row, part, :]
                out_i = out_i * scale
                if old[1] is not None:
                    out_i = out_i - old[1][s, row, part, :]
            new[0][s, row, part, :] = out_r
            new[1][s, row, part, :] = out_i


def fold(product):
    lanes = product[:, 0:BLOCK]
    for b in range(1, BLOCKS):
        lanes = lanes + product[:, b * BLOCK : (b + 1) * BLOCK]
    return lanes


def trace_row(start, first, second, row, sums):
    own = slice(0, OWN)
    sums = list(sums)
    for h in range(2):
        part = slice(h * 8, (h + 1) * 8)
        for s in range(2):
            v0 = start[s, row, part, own]
            r1 = first[0][s, row, part, own]
            i1 = first[1][s, row, part, own]
            r2 = second[0][s, row, part, own]
            i2 = second[1][s, row, part, own]
            terms = (v0 * v0, v0 * r1, v0 * r2, r1 * r2 + i1 * i2, r2 * r2 + i2 * i2)
            for n, term in enumerate(terms):
                sums[n * 2 + h] = sums[n * 2 + h] + fold(term)
    return tuple(sums)


SUMS = 5


class Rows:
    def __init__(self, ref, first):
        self.ref = ref
        self.first = first

    def __getitem__(self, index):
        s, row, part, lanes = index
        return self.ref[s, row - self.first, part, lanes]

    def __setitem__(self, index, value):
        s, row, part, lanes = index
        self.ref[s, row - self.first, part, lanes] = value


def interior_kernel(
    columns, plan, received, disorder, vacancy,
    level, factor, start, real1, imag1, real2, imag2, sums,
):
    real2, imag2 = Rows(real2, 2), Rows(imag2, 2)
    me = lax.axis_index("gy")
    tile, sites = edge_tiles(columns, plan, received)
    slots = [plan[me * BLOCKS + b] // BLOCKS for b in range(BLOCKS)]
    for s in range(2):
        kept = fill_sites(
            level, factor, s, range(HALO, HALO + WIDTH_X), disorder[s],
            vacancy[s].astype(F32), sites[s * 8 : (s + 1) * 8], 0,
        )
        for x in range(WIDTH_X):
            q = s * WIDTH_X + x
            pieces = [received[slots[b], q * R : (q + 1) * R, :].astype(F32) for b in range(BLOCKS)]
            pieces.append(pltpu.roll(tile, (BLOCK - 4 - 8 * q) % BLOCK, 1))
            value = jnp.concatenate(pieces, axis=1)
            for h in range(2):
                part = slice(h * 8, (h + 1) * 8)
                start[s, HALO + x, part, :] = value[part] * kept[x]

    def one(row, carry):
        advance(1, level, factor, None, (start, None), (real1, imag1), row)
        return carry

    lax.fori_loop(HALO + 1, HALO + WIDTH_X - 1, one, 0)

    def two(row, carry):
        advance(2, level, factor, (start, None), (real1, imag1), (real2, imag2), row)
        return trace_row(start, (real1, imag1), (real2, imag2), row, carry)

    zero = jnp.zeros((8, BLOCK), F32)
    totals = lax.fori_loop(HALO + 2, HALO + WIDTH_X - 2, two, (zero,) * (2 * SUMS))
    for i, total in enumerate(totals):
        sums[i * 8 : (i + 1) * 8, :] = total


def border_kernel(
    below, above, level_in, factor_in, start_in, real1_in, imag1_in, real2_in, imag2_in, sums_in,
    level, factor, start, real1, imag1, real2, imag2, trace_out, sites_out, start_out,
):
    real2, imag2 = Rows(real2, 2), Rows(imag2, 2)
    for ref, base, shift in ((below, 0, WIDTH_X - HALO), (above, HALO + WIDTH_X, 0)):
        planes = [ref[PLANES + p * 8 : PLANES + (p + 1) * 8, :].astype(F32) for p in range(4)]
        onsite = planes[0] + planes[1] + planes[2]
        sites = ref[HALF : HALF + R, BLOCK : 2 * BLOCK].astype(F32)
        far = ref[HALF : HALF + R, 0:BLOCK].astype(F32)
        for s in range(2):
            some = slice(s * HALO, (s + 1) * HALO)
            kept = fill_sites(
                level, factor, s, range(base, base + HALO), onsite[some], planes[3][some],
                sites[s * 8 : (s + 1) * 8], shift,
            )
            for i in range(HALO):
                index = (s * HALO + i) * R
                q = s * WIDTH_X + shift + i
                side = pltpu.roll(far, (BLOCK - 4 - 8 * q) % BLOCK, 1)
                value = jnp.concatenate([ref[index : index + R, :].astype(F32), side], axis=1)
                for h in range(2):
                    part = slice(h * 8, (h + 1) * 8)
                    start[s, base + i, part, :] = value[part] * kept[i]

    def one(i, carry):
        for row in (i + 1, i + HALO + WIDTH_X - 1):
            advance(1, level, factor, None, (start, None), (real1, imag1), row)
        return carry

    lax.fori_loop(0, HALO, one, 0)

    def two(i, carry):
        for row in (i + 2, i + HALO + WIDTH_X - 2):
            advance(2, level, factor, (start, None), (real1, imag1), (real2, imag2), row)
        return carry

    lax.fori_loop(0, HALO, two, 0)
    for s in range(2):
        for row in range(ROWS_X):
            sites_out[0, s, row : row + 1, :] = level[s, row, 0:1, :]
            sites_out[1, s, row : row + 1, :] = factor[s, row, 0:1, :]
            start_out[s, row] = start[s, row].astype(BF16)
    totals = tuple(sums_in[i * 8 : (i + 1) * 8, :] for i in range(2 * SUMS))

    def trace(i, carry):
        for row in (i + HALO, i + HALO + WIDTH_X - 2):
            carry = trace_row(start, (real1, imag1), (real2, imag2), row, carry)
        return carry

    totals = lax.fori_loop(0, 2, trace, totals)
    norm, one_one, one_two, both, second = (
        jnp.concatenate(totals[2 * n : 2 * n + 2], axis=0) for n in range(SUMS)
    )
    moments = jnp.concatenate(
        [one_one, one_two, 2.0 * both - one_one, 2.0 * second - norm], axis=0
    )
    trace_out[...] = lax.dot_general(
        jnp.ones(trace_out.shape[:1] + (BLOCK,), F32), moments,
        (((1,), (1,)), ((), ())),
        precision=lax.Precision.HIGHEST, preferred_element_type=F32,
    )


def local_kernel(
    sites, kept_start, real2, imag2,
    local_out, level, factor, start, real1, imag1, real3, imag3,
):
    real2, imag2 = Rows(real2, 2), Rows(imag2, 2)
    for s in range(2):
        for row in range(2, ROWS_X - 2):
            level[s, row] = jnp.broadcast_to(sites[0, s, row : row + 1, :], (8, LANES))
            factor[s, row] = jnp.broadcast_to(sites[1, s, row : row + 1, :], (8, LANES))
            start[s, row] = kept_start[s, row].astype(F32)

    def one(row, carry):
        advance(1, level, factor, None, (start, None), (real1, imag1), row)
        return carry

    lax.fori_loop(3, ROWS_X - 3, one, 0)

    def three(row, carry):
        advance(3, level, factor, (real1, imag1), (real2, imag2), (real3, imag3), row)
        return carry

    lax.fori_loop(3, ROWS_X - 3, three, 0)

    def finish(x, carry):
        row = x + HALO
        own = slice(0, OWN)
        for s in range(2):
            totals = [None] * TERMS
            for h in range(2):
                part = slice(h * 8, (h + 1) * 8)
                v0 = start[s, row, part, own]
                out_r, _ = hamilton(level, real3, imag3, s, row, h, False)
                scale = factor[s, row]
                v4 = out_r * (scale + scale) - real2[s, row, part, :]
                values = [ref[s, row, part, own] for ref in (real1, real2, real3)]
                values.append(v4[:, own])
                for n, value in enumerate(values):
                    product = v0 * value
                    totals[n] = product if h == 0 else totals[n] + product
            for n in range(TERMS):
                local_out[n, s, pl.ds(x, 1), :] = (
                    jnp.sum(totals[n], axis=0, keepdims=True) * (1.0 / R)
                )
        return carry

    lax.fori_loop(0, WIDTH_X, finish, 0)


def total_kernel(sites, shared, out):
    total = jnp.sum(shared[...], axis=0, keepdims=True) * (1.0 / sites)
    for n in range(TERMS):
        out[n : n + 1, :] = total[:, n * R : (n + 1) * R]


def local(stored_vectors, disorder, vacancy, plan):
    columns = lax.axis_size("gy")
    rows = lax.axis_size("gx")
    devices = rows * columns
    smem = pl.BlockSpec(memory_space=pltpu.SMEM)
    vmem = pl.BlockSpec(memory_space=pltpu.VMEM)
    params = pltpu.CompilerParams(vmem_limit_bytes=8 * 1024 * 1024)

    hbm = pl.BlockSpec(memory_space=pltpu.HBM)
    outgoing = pl.pallas_call(
        functools.partial(pack_kernel, columns),
        out_shape=jax.ShapeDtypeStruct((columns, SLOT_ROWS, BLOCK), BF16),
        in_specs=[hbm] * 4,
        out_specs=vmem,
        scratch_shapes=[
            pltpu.SMEM(plan.shape, plan.dtype),
            pltpu.VMEM(stored_vectors.shape, stored_vectors.dtype),
            pltpu.VMEM(disorder.shape, disorder.dtype),
            pltpu.VMEM(vacancy.shape, vacancy.dtype),
            pltpu.VMEM((BLOCKS, 2 * R * WIDTH_X, BLOCK), F32),
            pltpu.SMEM((BLOCKS + 1,), jnp.int32),
            pltpu.SemaphoreType.DMA((4,)),
        ],
        compiler_params=pltpu.CompilerParams(vmem_limit_bytes=60 * 1024 * 1024),
        name="pack",
    )(plan, stored_vectors, disorder, vacancy)
    received = lax.all_to_all(outgoing, "gy", split_axis=0, concat_axis=0, tiled=True)

    message = jax.ShapeDtypeStruct((MESSAGE, OWN), BF16)
    low_rows, high_rows = pl.pallas_call(
        functools.partial(arrange_kernel, columns),
        out_shape=(message, message),
        in_specs=[smem, vmem, vmem, vmem],
        out_specs=(vmem, vmem),
        scratch_shapes=[pltpu.VMEM((2, 4 * 2 * HALO, OWN), F32)],
        compiler_params=params,
        name="arrange",
    )(plan, received, disorder, vacancy)
    up = [(i, (i + 1) % rows) for i in range(rows)]
    down = [(target, source) for source, target in up]
    below = lax.ppermute(high_rows, "gx", up)
    above = lax.ppermute(low_rows, "gx", down)

    site = jax.ShapeDtypeStruct((2, ROWS_X, 8, LANES), F32)
    field = jax.ShapeDtypeStruct((2, ROWS_X, R, LANES), F32)
    narrow = jax.ShapeDtypeStruct((2, ROWS_X - 4, R, LANES), F32)
    state = (site, site) + (field,) * 3 + (narrow,) * 2
    inner = pl.pallas_call(
        functools.partial(interior_kernel, columns),
        out_shape=state + (jax.ShapeDtypeStruct((2 * SUMS * 8, BLOCK), F32),),
        in_specs=[smem, vmem, vmem, vmem],
        out_specs=(vmem,) * 8,
        compiler_params=params,
        cost_estimate=pl.CostEstimate(flops=10**7, bytes_accessed=8 * 10**6, transcendentals=0),
        name="interior",
    )(plan, received, disorder, vacancy)
    outputs = pl.pallas_call(
        border_kernel,
        out_shape=state + (
            jax.ShapeDtypeStruct((devices, TERMS * R), F32),
            jax.ShapeDtypeStruct((2, 2, ROWS_X, LANES), F32),
            jax.ShapeDtypeStruct(field.shape, BF16),
        ),
        in_specs=[vmem] * 10,
        out_specs=(vmem,) * 10,
        input_output_aliases={2 + i: i for i in range(7)},
        compiler_params=params,
        name="border",
    )(below, above, *inner)
    real2, imag2, partial, sites, start = outputs[5:]
    shared = lax.all_to_all(partial, ("gx", "gy"), split_axis=0, concat_axis=0, tiled=True)
    local_moments = pl.pallas_call(
        local_kernel,
        out_shape=jax.ShapeDtypeStruct((TERMS, 2, WIDTH_X, OWN), F32),
        in_specs=[vmem] * 4,
        out_specs=vmem,
        scratch_shapes=[pltpu.VMEM(site.shape, F32)] * 2 + [pltpu.VMEM(field.shape, F32)] * 5,
        compiler_params=pltpu.CompilerParams(vmem_limit_bytes=16 * 1024 * 1024),
        cost_estimate=pl.CostEstimate(flops=10**7, bytes_accessed=8 * 10**6, transcendentals=0),
        name="local_moments",
    )(sites, start, real2, imag2)
    trace = pl.pallas_call(
        functools.partial(total_kernel, 2 * WIDTH_X * rows * OWN * columns),
        out_shape=jax.ShapeDtypeStruct((TERMS, R), F32),
        in_specs=[vmem],
        out_specs=vmem,
        compiler_params=params,
        name="total",
    )(shared)
    return local_moments, trace


def solution(mesh):
    placed = (P(None, None, "gx", "gy"), P(None, "gx", "gy"), P(None, "gx", "gy"), P())
    return jax.shard_map(
        local, mesh=mesh, in_specs=placed,
        out_specs=(P(None, None, "gx", "gy"), P()), check_vma=False,
    )
```

time: 63.8 us -> 57.3 us (0.90)
  blocking collectives: 40.1 us -> 25.1 us
  starting transfers between devices: 3.63 us -> 9.52 us
  Pallas kernels: 10.2 us -> 14.7 us
  local copies, waits for them, and re-layouts: 3.78 us -> 0.02 us
  waiting for transfers between devices: 4.92 us -> 6.93 us
    all_to_all x1 -> x0, blocking collectives: 15.3 us -> none  [local(): lax.all_to_all(partial, ('gx', 'gy'), split_axis=0, concat_axis=0, tiled=...]
    all_to_all x0 -> x1, starting transfers between devices: none -> 5.89 us  [local(): lax.all_to_all(partial, ('gx', 'gy'), split_axis=0, concat_axis=0, tiled=...]
    all_to_all x0 -> x1, waiting for transfers between devices: none -> 4.4 us  [local(): lax.all_to_all(partial, ('gx', 'gy'), split_axis=0, concat_axis=0, tiled=...]
    pallas_call x1 -> x4, Pallas kernels: 8.44 us -> 11.6 us  [the longest x1 5.16 us: local(): pl.pallas_call(local_kernel, out_shape=jax.ShapeDtypeStruct((TERMS, 2, WI...]
    unnamed x8 -> x6, local copies, waits for them, and re-layouts: 3.11 us -> 0.02 us
    ppermute x1, waiting for transfers between devices: 2.44 us -> 0.04 us  [local(): below = lax.ppermute(high_rows, 'gx', up)]
    pallas_call x1, Pallas kernels: 1.14 us -> 2.42 us  [local(): pl.pallas_call(functools.partial(pack_kernel, columns), out_shape=jax.Sha...]
    mul x1 -> x0, local copies, waits for them, and re-layouts: 0.66 us -> none  [local(): trace = jnp.sum(shared, axis=0).reshape(TERMS, R) * (1.0 / sites)]
  transfers between devices with their start and end apart: 2 -> 3, of which waited for: 2 -> 2; matrix products, arithmetic and copies ran while one was open for 0% -> 0% of each run, Pallas kernels for 0% -> 13%
where the time goes in v2:
time: 57.3 us; the launch traced here: 57 us
  blocking collectives  25.1 us (44%)
  Pallas kernels  14.7 us (26%)
  starting transfers between devices  9.52 us (17%)
  waiting for transfers between devices  6.93 us (12%)
  between operations  0.69 us (1%)
    all_to_all x1, blocking collectives, local(): lax.all_to_all(outgoing, 'gy', split_axis=0, concat_axis=0, tiled=True)  25.1 us
    all_to_all x1, starting transfers between devices, local(): lax.all_to_all(partial, ('gx', 'gy'), split_axis=0, concat_axis=0, tiled=...  5.89 us
    pallas_call x1, Pallas kernels, local(): pl.pallas_call(local_kernel, out_shape=jax.ShapeDtypeStruct((TERMS, 2, WI...  5.16 us
    all_to_all x1, waiting for transfers between devices, local(): lax.all_to_all(partial, ('gx', 'gy'), split_axis=0, concat_axis=0, tiled=...  4.4 us
    ppermute x1, starting transfers between devices, local(): below = lax.ppermute(high_rows, 'gx', up)  3.63 us
    pallas_call x1, Pallas kernels, local(): pl.pallas_call(border_kernel, out_shape=state + (jax.ShapeDtypeStruct((de...  3.41 us
    ppermute x1, waiting for transfers between devices, local(): above = lax.ppermute(low_rows, 'gx', down)  2.48 us
    pallas_call x1, Pallas kernels, local(): pl.pallas_call(functools.partial(pack_kernel, columns), out_shape=jax.Sha...  2.42 us
  transfers between devices with their start and end apart: 3, of which 2 were waited for; matrix products, arithmetic and copies ran while one was open for 0% of the time, Pallas kernels for 13%

profile of v2, /device:TPU:1, one launch (start us, length us, event | category | flops | bytes accessed | tf_op | source)
XLA Modules:
  0.0 57.0 jit_solution(8780572229780718570)
XLA Ops:
  0.6 2.4 %pack.1 = bf16[16,288,128]{2,1,0:T(8,128)(2,1)} custom-call(s32[64]{0:T(128)} %plan.3, bf16[2,16,8,512]{3,2,1,0:T(8,128)(2,1)} %stored_hbm.1, f32[2,8,512]{2,1,0:T(8,128)} %disorder.3, s32[2,8,512]{2,1,0:T(8,128)} %vacancy.3), custom_call_target="tpu_custom_call" | custom-call | tf_op jit(solution)/shard_map/pack/pallas_call | solution.py:457
  3.1 0.0 copy-start
  3.1 0.0 copy-start.1
  3.1 0.0 copy-start.2
  3.1 25.1 %all_to_all.16.received = bf16[16,288,128]{2,1,0:T(8,128)(2,1)S(1)} all-to-all(bf16[16,288,128]{2,1,0:T(8,128)(2,1)} %pack.1), channel_id=1, replica_groups=mesh['gx'=8,'gy'=16] {'gy'}, dimensions={0} | all-to-all | bytes 2359296 | tf_op jit(solution)/shard_map/all_to_all | solution.py:474
  28.2 0.0 copy-done
  28.2 0.0 copy-done.1
  28.2 0.0 copy-done.2
  28.3 0.6 %arrange.1 = (bf16[176,512]{1,0:T(8,128)(2,1)S(1)}, bf16[176,512]{1,0:T(8,128)(2,1)S(1)}) custom-call(s32[64]{0:T(128)S(1)} %copy-done.2, bf16[16,288,128]{2,1,0:T(8,128)(2,1)S(1)} %all_to_all.16.received, f32[2,8,512]{2,1,0:T(8,128)S(1)} %copy-done, s32[2,8,512]{2,1,0:T(8,128)S(1)} %copy-done.1), custom_call_target="tpu_custom_call" | custom-call | tf_op jit(solution)/shard_map/arrange/pallas_call | solution.py:477
  28.9 3.6 %collective-permute-start = (bf16[176,512]{1,0:T(8,128)(2,1)S(1)}, bf16[176,512]{1,0:T(8,128)(2,1)S(1)}, u32[]{:S(2)}, u32[]{:S(2)}) collective-permute-start(bf16[176,512]{1,0:T(8,128)(2,1)S(1)} %get-tuple-element.17), channel_id=1, source_target_pairs={{0,16},{16,32},{32,48},{48,64},{64,80},{80,96},{96,112},{112,0},{1... | collective-permute-start | bytes 540680 | tf_op jit(solution)/shard_map/ppermute | solution.py:488
  32.5 0.0 collective-permute-start.1
  32.5 2.4 %interior.1 = (f32[2,16,8,640]{3,2,1,0:T(8,128)S(1)}, f32[2,16,8,640]{3,2,1,0:T(8,128)S(1)}, f32[2,16,16,640]{3,2,1,0:T(8,128)S(1)}, f32[2,16,16,640]{3,2,1,0:T(...) custom-call(s32[64]{0:T(128)S(1)} %copy-done.2, ...), custom_call_target="tpu_custom_call" | custom-call | flops 10000000 | bytes 8000000 | tf_op jit(solution)/shard_map/interior/pallas_call | solution.py:495
  34.9 0.0 collective-permute-done.below
  35.0 2.5 %collective-permute-done.1.above = bf16[176,512]{1,0:T(8,128)(2,1)S(1)} collective-permute-done((bf16[176,512]{1,0:T(8,128)(2,1)S(1)}, bf16[176,512]{1,0:T(8,128)(2,1)S(1)}, u32[]{:S(2)}, u32[]{:S(2)}) %collective-permute-start.1) | collective-permute-done | bytes 180256 | tf_op jit(solution)/shard_map/ppermute | solution.py:489
  37.4 3.4 %border.1 = (f32[2,16,8,640]{3,2,1,0:T(8,128)S(1)}, f32[2,16,8,640]{3,2,1,0:T(8,128)S(1)}, f32[2,16,16,640]{3,2,1,0:T(8,128)S(1)}, f32[2,16,16,640]{3,2,1,0:T(8,...) custom-call(bf16[176,512]{1,0:T(8,128)(2,1)S(1)} %collective-permute, ...), custom_call_target="tpu_custom_call", output_to_operand_aliasing={{0}: (2, {}), {1}: (3, {}), {2}: (4, {}), {3}: (5, {}), {4}... | custom-call | tf_op jit(solution)/shard_map/border/pallas_call | solution.py:504
  40.9 5.9 %all-to-all-start.1 = ((f32[128,1,64]{2,1,0:T(1,128)}), f32[128,1,64]{2,1,0:T(1,128)S(1)}, u32[]{:S(2)}, u32[]{:S(2)}) async-start(f32[128,1,64]{2,1,0:T(1,128)} %bitcast.1), calls=%async_computation.1 | async-start | bytes 131072 | tf_op jit(solution)/shard_map/all_to_all | solution.py:518
  46.8 5.2 %local_moments.1 = f32[4,2,8,512]{3,2,1,0:T(8,128)} custom-call(f32[2,2,16,640]{3,2,1,0:T(8,128)S(1)} %get-tuple-element.27.sites, bf16[2,16,16,640]{3,2,1,0:T(8,128)(2,1)S(1)} %get-tuple-element.28.kept_start, f32[2,12,16,640]{3,2,1,0:T(8,128)S(1)} %get-tuple-element.29.real2, f32[2,12,16,640]{3,2,1,0:T(8,128)S(1)} %get-tuple-element.30.imag2), custom_call_target="tpu_custom_call" | custom-call | flops 10000000 | bytes 8000000 | tf_op jit(solution)/shard_map/local_moments/pallas_call | solution.py:519
  51.9 4.4 %all-to-all-done.1 = f32[128,1,64]{2,1,0:T(1,128)S(1)} async-done(((f32[128,1,64]{2,1,0:T(1,128)}), f32[128,1,64]{2,1,0:T(1,128)S(1)}, u32[]{:S(2)}, u32[]{:S(2)}) %all-to-all-start.1) | async-done | bytes 32800 | tf_op jit(solution)/shard_map/all_to_all | solution.py:518
  56.3 0.7 %total.1 = f32[4,16]{1,0:T(4,128)} custom-call(f32[128,64]{1,0:T(8,128)S(1)} %bitcast.4), custom_call_target="tpu_custom_call" | custom-call | tf_op jit(solution)/shard_map/total/pallas_call | solution.py:529
Async XLA Ops:
  3.1 25.2 %copy-start = (f32[2,8,512]{2,1,0:T(8,128)S(1)}, f32[2,8,512]{2,1,0:T(8,128)}, u32[]{:S(2)}) copy-start(f32[2,8,512]{2,1,0:T(8,128)} %disorder.3) | copy-start | bytes 98308
  3.1 25.2 %copy-start.1 = (s32[2,8,512]{2,1,0:T(8,128)S(1)}, s32[2,8,512]{2,1,0:T(8,128)}, u32[]{:S(2)}) copy-start(s32[2,8,512]{2,1,0:T(8,128)} %vacancy.3) | copy-start | bytes 98308
  3.1 25.2 %copy-start.2 = (s32[64]{0:T(128)S(1)}, s32[64]{0:T(128)}, u32[]{:S(2)}) copy-start(s32[64]{0:T(128)} %plan.3) | copy-start | bytes 772
  28.9 6.1 %collective-permute-start = (bf16[176,512]{1,0:T(8,128)(2,1)S(1)}, bf16[176,512]{1,0:T(8,128)(2,1)S(1)}, u32[]{:S(2)}, u32[]{:S(2)}) collective-permute-start(bf16[176,512]{1,0:T(8,128)(2,1)S(1)} %get-tuple-element.17), channel_id=1, source_target_pairs={{0,16},{16,32},{32,48},{48,64},{64,80},{80,96},{96,112},{112,0},{1... | collective-permute-start | bytes 540680 | tf_op jit(solution)/shard_map/ppermute | solution.py:488
  32.5 4.9 %collective-permute-start.1 = (bf16[176,512]{1,0:T(8,128)(2,1)S(1)}, bf16[176,512]{1,0:T(8,128)(2,1)S(1)}, u32[]{:S(2)}, u32[]{:S(2)}) collective-permute-start(bf16[176,512]{1,0:T(8,128)(2,1)S(1)} %get-tuple-element.18), channel_id=1, source_target_pairs={{16,0},{32,16},{48,32},{64,48},{80,64},{96,80},{112,96},{0,112},{1... | collective-permute-start | bytes 540680 | tf_op jit(solution)/shard_map/ppermute | solution.py:489
  40.9 15.5 %all-to-all-start.1 = ((f32[128,1,64]{2,1,0:T(1,128)}), f32[128,1,64]{2,1,0:T(1,128)S(1)}, u32[]{:S(2)}, u32[]{:S(2)}) async-start(f32[128,1,64]{2,1,0:T(1,128)} %bitcast.1), calls=%async_computation.1 | async-start | bytes 131072 | tf_op jit(solution)/shard_map/all_to_all | solution.py:518

commit v3 on v2

--- a/solution.py
+++ b/solution.py
@@ -183,69 +183,62 @@
         j = first + i
         lev = jnp.concatenate([onsite[i : i + 1], side_level[j : j + 1]], axis=1)
         kep = jnp.concatenate([kept[i : i + 1], side_keep[j : j + 1]], axis=1)
-        level[s, row] = jnp.broadcast_to(lev, (8, LANES))
+        level[s, row] = jnp.broadcast_to(lev * (1.0 / COS), (8, LANES))
         kep = jnp.broadcast_to(kep, (8, LANES))
-        factor[s, row] = kep * (1.0 / SPREAD)
+        factor[s, row] = kep * (2.0 * COS / SPREAD)
         kept_rows.append(kep)
     return kept_rows
 
 
-def hamilton(level, real, imag, s, row, h, want_imag):
-    part = slice(h * 8, (h + 1) * 8)
-    sine = SIN if s == 0 else -SIN
-    aside = row - 1 if s == 0 else row + 1
-    r_m, r_0, r_p = (real[s, row + d, part, :] for d in (-1, 0, 1))
-    o_0 = real[1 - s, row, part, :]
-    near = o_0 + real[1 - s, aside, part, :]
-    lev = level[s, row]
-    out_r = COS * (r_p + r_m) + lev * r_0 - near
-    g0 = COS * (r_m + r_0)
-    g1 = COS * (r_0 + r_p)
-    if imag is not None:
-        i_m, i_0, i_p = (imag[s, row + d, part, :] for d in (-1, 0, 1))
-        out_r = out_r - sine * (i_p - i_m)
-        g0 = g0 - sine * (i_m - i_0)
-        g1 = g1 - sine * (i_0 - i_p)
-    if s == 0:
-        g1 = g1 - o_0
-    else:
-        g0 = g0 - o_0
-    out_r = out_r + pltpu.roll(g0, LANES - 1, 1) + pltpu.roll(g1, 1, 1)
-    if not want_imag:
-        return out_r, None
-    out_i = sine * (r_p - r_m)
-    g0 = sine * (r_m - r_0)
-    g1 = sine * (r_0 - r_p)
-    if imag is not None:
-        o_0 = imag[1 - s, row, part, :]
-        near = o_0 + imag[1 - s, aside, part, :]
-        out_i = out_i + COS * (i_p + i_m) + lev * i_0 - near
-        g0 = g0 + COS * (i_m + i_0)
-        g1 = g1 + COS * (i_0 + i_p)
-        if s == 0:
-            g1 = g1 - o_0
-        else:
-            g0 = g0 - o_0
-    out_i = out_i + pltpu.roll(g0, LANES - 1, 1) + pltpu.roll(g1, 1, 1)
-    return out_r, out_i
-
-
-def advance(term, level, factor, old, now, new, row):
+def span(level, factor, term, old, now, new, row, count=2):
     for h in range(2):
         part = slice(h * 8, (h + 1) * 8)
+        near_rows = range(-1, count + 1)
+        real = [{d: now[0][s, row + d, part, :] for d in near_rows} for s in range(2)]
+        fields = [real]
+        if now[1] is not None:
+            fields.append([{d: now[1][s, row + d, part, :] for d in near_rows} for s in range(2)])
+        others = [
+            [{d: f[s][d] * (1.0 / COS) for d in near_rows} for s in range(2)] for f in fields
+        ]
         for s in range(2):
-            out_r, out_i = hamilton(level, now[0], now[1], s, row, h, True)
-            scale = factor[s, row]
-            if term == 1:
-                out_r, out_i = out_r * scale, out_i * scale
+            ratio = SIN / COS if s == 0 else -SIN / COS
+            turn = [{d: f[s][d] * ratio for d in near_rows} for f in fields]
+            if len(fields) == 1:
+                ahead = [real[s], turn[0]]
+                back = [real[s], {d: -turn[0][d] for d in near_rows}]
             else:
-                scale = scale + scale
-                out_r = out_r * scale - old[0][s, row, part, :]
-                out_i = out_i * scale
-                if old[1] is not None:
-                    out_i = out_i - old[1][s, row, part, :]
-            new[0][s, row, part, :] = out_r
-            new[1][s, row, part, :] = out_i
+                imag = fields[1][s]
+                ahead = [
+                    {d: real[s][d] - turn[1][d] for d in near_rows},
+                    {d: imag[d] + turn[0][d] for d in near_rows},
+                ]
+                back = [
+                    {d: real[s][d] + turn[1][d] for d in near_rows},
+                    {d: imag[d] - turn[0][d] for d in near_rows},
+                ]
+            for c in range(2):
+                if new[c] is None:
+                    continue
+                joint = {d: ahead[c][d - 1] + back[c][d] for d in range(count + 1)}
+                for d in range(count):
+                    out = ahead[c][d + 1] + back[c][d - 1]
+                    up, down = joint[d], joint[d + 1]
+                    if c < len(fields):
+                        other = others[c][1 - s]
+                        aside = d - 1 if s == 0 else d + 1
+                        out = out + level[s, row + d] * fields[c][s][d]
+                        out = out - (other[d] + other[aside])
+                        if s == 0:
+                            down = down - other[d]
+                        else:
+                            up = up - other[d]
+                    out = out + pltpu.roll(up, LANES - 1, 1) + pltpu.roll(down, 1, 1)
+                    scale = factor[s, row + d]
+                    out = out * (scale * 0.5 if term == 1 else scale)
+                    if term > 1 and old[c] is not None:
+                        out = out - old[c][s, row + d, part, :]
+                    new[c][s, row + d, part, :] = out
 
 
 def fold(product):
@@ -293,7 +286,7 @@
     columns, plan, received, disorder, vacancy,
     level, factor, start, real1, imag1, real2, imag2, sums,
 ):
-    real2, imag2 = Rows(real2, 2), Rows(imag2, 2)
+    real2, imag2 = Rows(real2, HALO), Rows(imag2, HALO)
     me = lax.axis_index("gy")
     tile, sites = edge_tiles(columns, plan, received)
     slots = [plan[me * BLOCKS + b] // BLOCKS for b in range(BLOCKS)]
@@ -311,18 +304,22 @@
                 part = slice(h * 8, (h + 1) * 8)
                 start[s, HALO + x, part, :] = value[part] * kept[x]
 
-    def one(row, carry):
-        advance(1, level, factor, None, (start, None), (real1, imag1), row)
+    def one(i, carry):
+        row = HALO + 1 + 2 * i
+        span(level, factor, 1, None, (start, None), (real1, imag1), row)
         return carry
 
-    lax.fori_loop(HALO + 1, HALO + WIDTH_X - 1, one, 0)
-
-    def two(row, carry):
-        advance(2, level, factor, (start, None), (real1, imag1), (real2, imag2), row)
-        return trace_row(start, (real1, imag1), (real2, imag2), row, carry)
+    lax.fori_loop(0, 3, one, 0)
+
+    def two(i, carry):
+        row = HALO + 2 + 2 * i
+        span(level, factor, 2, (start, None), (real1, imag1), (real2, imag2), row)
+        for d in range(2):
+            carry = trace_row(start, (real1, imag1), (real2, imag2), row + d, carry)
+        return carry
 
     zero = jnp.zeros((8, BLOCK), F32)
-    totals = lax.fori_loop(HALO + 2, HALO + WIDTH_X - 2, two, (zero,) * (2 * SUMS))
+    totals = lax.fori_loop(0, 2, two, (zero,) * (2 * SUMS))
     for i, total in enumerate(totals):
         sums[i * 8 : (i + 1) * 8, :] = total
 
@@ -331,7 +328,7 @@
     below, above, level_in, factor_in, start_in, real1_in, imag1_in, real2_in, imag2_in, sums_in,
     level, factor, start, real1, imag1, real2, imag2, trace_out, sites_out, start_out,
 ):
-    real2, imag2 = Rows(real2, 2), Rows(imag2, 2)
+    real2, imag2 = Rows(real2, HALO), Rows(imag2, HALO)
     for ref, base, shift in ((below, 0, WIDTH_X - HALO), (above, HALO + WIDTH_X, 0)):
         planes = [ref[PLANES + p * 8 : PLANES + (p + 1) * 8, :].astype(F32) for p in range(4)]
         onsite = planes[0] + planes[1] + planes[2]
@@ -352,32 +349,13 @@
                     part = slice(h * 8, (h + 1) * 8)
                     start[s, base + i, part, :] = value[part] * kept[i]
 
-    def one(i, carry):
-        for row in (i + 1, i + HALO + WIDTH_X - 1):
-            advance(1, level, factor, None, (start, None), (real1, imag1), row)
-        return carry
-
-    lax.fori_loop(0, HALO, one, 0)
-
-    def two(i, carry):
-        for row in (i + 2, i + HALO + WIDTH_X - 2):
-            advance(2, level, factor, (start, None), (real1, imag1), (real2, imag2), row)
-        return carry
-
-    lax.fori_loop(0, HALO, two, 0)
-    for s in range(2):
-        for row in range(ROWS_X):
-            sites_out[0, s, row : row + 1, :] = level[s, row, 0:1, :]
-            sites_out[1, s, row : row + 1, :] = factor[s, row, 0:1, :]
-            start_out[s, row] = start[s, row].astype(BF16)
+    for row in (HALO - 1, HALO + WIDTH_X - 1):
+        span(level, factor, 1, None, (start, None), (real1, imag1), row)
     totals = tuple(sums_in[i * 8 : (i + 1) * 8, :] for i in range(2 * SUMS))
-
-    def trace(i, carry):
-        for row in (i + HALO, i + HALO + WIDTH_X - 2):
-            carry = trace_row(start, (real1, imag1), (real2, imag2), row, carry)
-        return carry
-
-    totals = lax.fori_loop(0, 2, trace, totals)
+    for row in (HALO, HALO + WIDTH_X - 2):
+        span(level, factor, 2, (start, None), (real1, imag1), (real2, imag2), row)
+        for d in range(2):
+            totals = trace_row(start, (real1, imag1), (real2, imag2), row + d, totals)
     norm, one_one, one_two, both, second = (
         jnp.concatenate(totals[2 * n : 2 * n + 2], axis=0) for n in range(SUMS)
     )
@@ -389,54 +367,66 @@
         (((1,), (1,)), ((), ())),
         precision=lax.Precision.HIGHEST, preferred_element_type=F32,
     )
+    for s in range(2):
+        for row in range(ROWS_X):
+            sites_out[0, s, row : row + 1, :] = level[s, row, 0:1, :]
+            sites_out[1, s, row : row + 1, :] = factor[s, row, 0:1, :]
+            start_out[s, row] = start[s, row].astype(BF16)
 
 
 def local_kernel(
-    sites, kept_start, real2, imag2,
-    local_out, level, factor, start, real1, imag1, real3, imag3,
+    sites, kept_start, real2_in, imag2_in,
+    local_out, level, factor, start, real1, imag1, real2, imag2, real3, imag3, real4, products,
 ):
-    real2, imag2 = Rows(real2, 2), Rows(imag2, 2)
+    real2_in, imag2_in, real4 = Rows(real2_in, HALO), Rows(imag2_in, HALO), Rows(real4, HALO)
     for s in range(2):
-        for row in range(2, ROWS_X - 2):
+        for row in range(ROWS_X):
             level[s, row] = jnp.broadcast_to(sites[0, s, row : row + 1, :], (8, LANES))
             factor[s, row] = jnp.broadcast_to(sites[1, s, row : row + 1, :], (8, LANES))
             start[s, row] = kept_start[s, row].astype(F32)
-
-    def one(row, carry):
-        advance(1, level, factor, None, (start, None), (real1, imag1), row)
+        for row in range(HALO, HALO + WIDTH_X):
+            real2[s, row] = real2_in[s, row, :, :]
+            imag2[s, row] = imag2_in[s, row, :, :]
+
+    def one(i, carry):
+        span(level, factor, 1, None, (start, None), (real1, imag1), 2 * i + 1)
         return carry
 
-    lax.fori_loop(3, ROWS_X - 3, one, 0)
-
-    def three(row, carry):
-        advance(3, level, factor, (real1, imag1), (real2, imag2), (real3, imag3), row)
+    lax.fori_loop(0, 7, one, 0)
+    for row in (2, ROWS_X - 4):
+        span(level, factor, 2, (start, None), (real1, imag1), (real2, imag2), row)
+
+    def three(i, carry):
+        span(level, factor, 3, (real1, imag1), (real2, imag2), (real3, imag3), 2 * i + 3)
         return carry
 
-    lax.fori_loop(3, ROWS_X - 3, three, 0)
-
-    def finish(x, carry):
-        row = x + HALO
-        own = slice(0, OWN)
+    lax.fori_loop(0, 5, three, 0)
+
+    def four(i, carry):
+        row = 2 * i + HALO
+        span(level, factor, 4, (real2, imag2), (real3, imag3), (real4, None), row)
+        for d in range(2):
+            for s in range(2):
+                for n, ref in enumerate((real1, real2, real3, real4)):
+                    total = None
+                    for h in range(2):
+                        index = (s, row + d, slice(h * 8, (h + 1) * 8), slice(0, OWN))
+                        product = start[index] * ref[index]
+                        total = product if h == 0 else total + product
+                    for b in range(BLOCKS):
+                        products[n, s, b, pl.ds(8 * (2 * i + d), 8), :] = (
+                            total[:, b * BLOCK : (b + 1) * BLOCK]
+                        )
+        return carry
+
+    lax.fori_loop(0, WIDTH_X // 2, four, 0)
+    for n in range(TERMS):
         for s in range(2):
-            totals = [None] * TERMS
-            for h in range(2):
-                part = slice(h * 8, (h + 1) * 8)
-                v0 = start[s, row, part, own]
-                out_r, _ = hamilton(level, real3, imag3, s, row, h, False)
-                scale = factor[s, row]
-                v4 = out_r * (scale + scale) - real2[s, row, part, :]
-                values = [ref[s, row, part, own] for ref in (real1, real2, real3)]
-                values.append(v4[:, own])
-                for n, value in enumerate(values):
-                    product = v0 * value
-                    totals[n] = product if h == 0 else totals[n] + product
-            for n in range(TERMS):
-                local_out[n, s, pl.ds(x, 1), :] = (
-                    jnp.sum(totals[n], axis=0, keepdims=True) * (1.0 / R)
-                )
-        return carry
-
-    lax.fori_loop(0, WIDTH_X, finish, 0)
+            for b in range(BLOCKS):
+                total = products[n, s, b, pl.ds(0, WIDTH_X, stride=8), :]
+                for r in range(1, 8):
+                    total = total + products[n, s, b, pl.ds(r, WIDTH_X, stride=8), :]
+                local_out[n, s, :, b * BLOCK : (b + 1) * BLOCK] = total * (1.0 / R)
 
 
 def total_kernel(sites, shared, out):
@@ -490,7 +480,7 @@
 
     site = jax.ShapeDtypeStruct((2, ROWS_X, 8, LANES), F32)
     field = jax.ShapeDtypeStruct((2, ROWS_X, R, LANES), F32)
-    narrow = jax.ShapeDtypeStruct((2, ROWS_X - 4, R, LANES), F32)
+    narrow = jax.ShapeDtypeStruct((2, WIDTH_X, R, LANES), F32)
     state = (site, site) + (field,) * 3 + (narrow,) * 2
     inner = pl.pallas_call(
         functools.partial(interior_kernel, columns),
@@ -521,7 +511,12 @@
         out_shape=jax.ShapeDtypeStruct((TERMS, 2, WIDTH_X, OWN), F32),
         in_specs=[vmem] * 4,
         out_specs=vmem,
-        scratch_shapes=[pltpu.VMEM(site.shape, F32)] * 2 + [pltpu.VMEM(field.shape, F32)] * 5,
+        scratch_shapes=[pltpu.VMEM(site.shape, F32)] * 2
+        + [pltpu.VMEM(field.shape, F32)] * 7
+        + [
+            pltpu.VMEM(narrow.shape, F32),
+            pltpu.VMEM((TERMS, 2, BLOCKS, 8 * WIDTH_X, BLOCK), F32),
+        ],
         compiler_params=pltpu.CompilerParams(vmem_limit_bytes=16 * 1024 * 1024),
         cost_estimate=pl.CostEstimate(flops=10**7, bytes_accessed=8 * 10**6, transcendentals=0),
         name="local_moments",

time: 57.3 us -> 56 us (0.977)
  Pallas kernels: 14.7 us -> 13.4 us
    pallas_call x1, Pallas kernels: 3.41 us -> 2.13 us  [local(): pl.pallas_call(border_kernel, out_shape=state + (jax.ShapeDtypeStruct((de...]
  transfers between devices with their start and end apart: 3 -> 3, of which waited for: 2 -> 3; matrix products, arithmetic and copies ran while one was open for 0% -> 0% of each run, Pallas kernels for 13% -> 14%
where the time goes in v3:
time: 56 us; the launch traced here: 55.7 us
  blocking collectives  25.1 us (45%)
  Pallas kernels  13.4 us (24%)
  starting transfers between devices  9.52 us (17%)
  waiting for transfers between devices  6.95 us (12%)
  between operations  0.69 us (1%)
    all_to_all x1, blocking collectives, local(): lax.all_to_all(outgoing, 'gy', split_axis=0, concat_axis=0, tiled=True)  25.1 us
    all_to_all x1, starting transfers between devices, local(): lax.all_to_all(partial, ('gx', 'gy'), split_axis=0, concat_axis=0, tiled=...  5.89 us
    pallas_call x1, Pallas kernels, local(): pl.pallas_call(local_kernel, out_shape=jax.ShapeDtypeStruct((TERMS, 2, WI...  5.44 us
    all_to_all x1, waiting for transfers between devices, local(): lax.all_to_all(partial, ('gx', 'gy'), split_axis=0, concat_axis=0, tiled=...  4.12 us
    ppermute x1, starting transfers between devices, local(): below = lax.ppermute(high_rows, 'gx', up)  3.63 us
    ppermute x1, waiting for transfers between devices, local(): above = lax.ppermute(low_rows, 'gx', down)  2.48 us
    pallas_call x1, Pallas kernels, local(): pl.pallas_call(functools.partial(pack_kernel, columns), out_shape=jax.Sha...  2.42 us
    pallas_call x1, Pallas kernels, local(): pl.pallas_call(border_kernel, out_shape=state + (jax.ShapeDtypeStruct((de...  2.13 us
  transfers between devices with their start and end apart: 3, of which 3 were waited for; matrix products, arithmetic and copies ran while one was open for 0% of the time, Pallas kernels for 14%

profile of v3, /device:TPU:1, one launch (start us, length us, event | category | flops | bytes accessed | tf_op | source)
XLA Modules:
  0.0 55.7 jit_solution(3557384033983565526)
XLA Ops:
  0.6 2.4 %pack.1 = bf16[16,288,128]{2,1,0:T(8,128)(2,1)} custom-call(s32[64]{0:T(128)} %plan.3, bf16[2,16,8,512]{3,2,1,0:T(8,128)(2,1)} %stored_hbm.1, f32[2,8,512]{2,1,0:T(8,128)} %disorder.3, s32[2,8,512]{2,1,0:T(8,128)} %vacancy.3), custom_call_target="tpu_custom_call" | custom-call | tf_op jit(solution)/shard_map/pack/pallas_call | solution.py:447
  3.1 0.0 copy-start
  3.1 0.0 copy-start.1
  3.1 0.0 copy-start.2
  3.1 25.1 %all_to_all.16.received = bf16[16,288,128]{2,1,0:T(8,128)(2,1)S(1)} all-to-all(bf16[16,288,128]{2,1,0:T(8,128)(2,1)} %pack.1), channel_id=1, replica_groups=mesh['gx'=8,'gy'=16] {'gy'}, dimensions={0} | all-to-all | bytes 2359296 | tf_op jit(solution)/shard_map/all_to_all | solution.py:464
  28.2 0.0 copy-done
  28.2 0.0 copy-done.1
  28.2 0.0 copy-done.2
  28.3 0.6 %arrange.1 = (bf16[176,512]{1,0:T(8,128)(2,1)S(1)}, bf16[176,512]{1,0:T(8,128)(2,1)S(1)}) custom-call(s32[64]{0:T(128)S(1)} %copy-done.2, bf16[16,288,128]{2,1,0:T(8,128)(2,1)S(1)} %all_to_all.16.received, f32[2,8,512]{2,1,0:T(8,128)S(1)} %copy-done, s32[2,8,512]{2,1,0:T(8,128)S(1)} %copy-done.1), custom_call_target="tpu_custom_call" | custom-call | tf_op jit(solution)/shard_map/arrange/pallas_call | solution.py:467
  28.9 3.6 %collective-permute-start = (bf16[176,512]{1,0:T(8,128)(2,1)S(1)}, bf16[176,512]{1,0:T(8,128)(2,1)S(1)}, u32[]{:S(2)}, u32[]{:S(2)}) collective-permute-start(bf16[176,512]{1,0:T(8,128)(2,1)S(1)} %get-tuple-element.17), channel_id=1, source_target_pairs={{0,16},{16,32},{32,48},{48,64},{64,80},{80,96},{96,112},{112,0},{1... | collective-permute-start | bytes 540680 | tf_op jit(solution)/shard_map/ppermute | solution.py:478
  32.5 0.0 collective-permute-start.1
  32.5 2.1 %interior.1 = (f32[2,16,8,640]{3,2,1,0:T(8,128)S(1)}, f32[2,16,8,640]{3,2,1,0:T(8,128)S(1)}, f32[2,16,16,640]{3,2,1,0:T(8,128)S(1)}, f32[2,16,16,640]{3,2,1,0:T(...) custom-call(s32[64]{0:T(128)S(1)} %copy-done.2, ...), custom_call_target="tpu_custom_call" | custom-call | flops 10000000 | bytes 8000000 | tf_op jit(solution)/shard_map/interior/pallas_call | solution.py:485
  34.6 0.3 collective-permute-done.below
  35.0 2.5 %collective-permute-done.1.above = bf16[176,512]{1,0:T(8,128)(2,1)S(1)} collective-permute-done((bf16[176,512]{1,0:T(8,128)(2,1)S(1)}, bf16[176,512]{1,0:T(8,128)(2,1)S(1)}, u32[]{:S(2)}, u32[]{:S(2)}) %collective-permute-start.1) | collective-permute-done | bytes 180256 | tf_op jit(solution)/shard_map/ppermute | solution.py:479
  37.4 2.1 %border.1 = (f32[2,16,8,640]{3,2,1,0:T(8,128)S(1)}, f32[2,16,8,640]{3,2,1,0:T(8,128)S(1)}, f32[2,16,16,640]{3,2,1,0:T(8,128)S(1)}, f32[2,16,16,640]{3,2,1,0:T(8,...) custom-call(bf16[176,512]{1,0:T(8,128)(2,1)S(1)} %collective-permute, ...), custom_call_target="tpu_custom_call", output_to_operand_aliasing={{0}: (2, {}), {1}: (3, {}), {2}: (4, {}), {3}: (5, {}), {4}... | custom-call | tf_op jit(solution)/shard_map/border/pallas_call | solution.py:494
  39.6 5.9 %all-to-all-start.1 = ((f32[128,1,64]{2,1,0:T(1,128)}), f32[128,1,64]{2,1,0:T(1,128)S(1)}, u32[]{:S(2)}, u32[]{:S(2)}) async-start(f32[128,1,64]{2,1,0:T(1,128)} %bitcast.1), calls=%async_computation.1 | async-start | bytes 131072 | tf_op jit(solution)/shard_map/all_to_all | solution.py:508
  45.5 5.4 %local_moments.1 = f32[4,2,8,512]{3,2,1,0:T(8,128)} custom-call(f32[2,2,16,640]{3,2,1,0:T(8,128)S(1)} %get-tuple-element.27.sites, bf16[2,16,16,640]{3,2,1,0:T(8,128)(2,1)S(1)} %get-tuple-element.28.kept_start, f32[2,8,16,640]{3,2,1,0:T(8,128)S(1)} %get-tuple-element.29.real2_in, f32[2,8,16,640]{3,2,1,0:T(8,128)S(1)} %get-tuple-element.30.imag2_in), custom_call_target="tpu_custom_call" | custom-call | flops 10000000 | bytes 8000000 | tf_op jit(solution)/shard_map/local_moments/pallas_call | solution.py:509
  50.9 4.1 %all-to-all-done.1 = f32[128,1,64]{2,1,0:T(1,128)S(1)} async-done(((f32[128,1,64]{2,1,0:T(1,128)}), f32[128,1,64]{2,1,0:T(1,128)S(1)}, u32[]{:S(2)}, u32[]{:S(2)}) %all-to-all-start.1) | async-done | bytes 32800 | tf_op jit(solution)/shard_map/all_to_all | solution.py:508
  55.0 0.7 %total.1 = f32[4,16]{1,0:T(4,128)} custom-call(f32[128,64]{1,0:T(8,128)S(1)} %bitcast.4), custom_call_target="tpu_custom_call" | custom-call | tf_op jit(solution)/shard_map/total/pallas_call | solution.py:524
Async XLA Ops:
  3.1 25.2 %copy-start = (f32[2,8,512]{2,1,0:T(8,128)S(1)}, f32[2,8,512]{2,1,0:T(8,128)}, u32[]{:S(2)}) copy-start(f32[2,8,512]{2,1,0:T(8,128)} %disorder.3) | copy-start | bytes 98308
  3.1 25.2 %copy-start.1 = (s32[2,8,512]{2,1,0:T(8,128)S(1)}, s32[2,8,512]{2,1,0:T(8,128)}, u32[]{:S(2)}) copy-start(s32[2,8,512]{2,1,0:T(8,128)} %vacancy.3) | copy-start | bytes 98308
  3.1 25.2 %copy-start.2 = (s32[64]{0:T(128)S(1)}, s32[64]{0:T(128)}, u32[]{:S(2)}) copy-start(s32[64]{0:T(128)} %plan.3) | copy-start | bytes 772
  28.9 6.1 %collective-permute-start = (bf16[176,512]{1,0:T(8,128)(2,1)S(1)}, bf16[176,512]{1,0:T(8,128)(2,1)S(1)}, u32[]{:S(2)}, u32[]{:S(2)}) collective-permute-start(bf16[176,512]{1,0:T(8,128)(2,1)S(1)} %get-tuple-element.17), channel_id=1, source_target_pairs={{0,16},{16,32},{32,48},{48,64},{64,80},{80,96},{96,112},{112,0},{1... | collective-permute-start | bytes 540680 | tf_op jit(solution)/shard_map/ppermute | solution.py:478
  32.5 4.9 %collective-permute-start.1 = (bf16[176,512]{1,0:T(8,128)(2,1)S(1)}, bf16[176,512]{1,0:T(8,128)(2,1)S(1)}, u32[]{:S(2)}, u32[]{:S(2)}) collective-permute-start(bf16[176,512]{1,0:T(8,128)(2,1)S(1)} %get-tuple-element.18), channel_id=1, source_target_pairs={{16,0},{32,16},{48,32},{64,48},{80,64},{96,80},{112,96},{0,112},{1... | collective-permute-start | bytes 540680 | tf_op jit(solution)/shard_map/ppermute | solution.py:479
  39.6 15.5 %all-to-all-start.1 = ((f32[128,1,64]{2,1,0:T(1,128)}), f32[128,1,64]{2,1,0:T(1,128)S(1)}, u32[]{:S(2)}, u32[]{:S(2)}) async-start(f32[128,1,64]{2,1,0:T(1,128)} %bitcast.1), calls=%async_computation.1 | async-start | bytes 131072 | tf_op jit(solution)/shard_map/all_to_all | solution.py:508

commit v4 on v3

--- a/solution.py
+++ b/solution.py
@@ -18,11 +18,14 @@
 ROWS_X = WIDTH_X + 2 * HALO
 SLOT = 2 * WIDTH_X * R
 EDGE = SLOT
-SITE_EDGE = SLOT + 16
-SLOT_ROWS = SLOT + 32
-HALF = 2 * HALO * R
-PLANES = HALF + 16
-MESSAGE = HALF + 16 + 4 * 2 * HALO
+SITE_EDGE = SLOT + R
+SLOT_ROWS = SLOT + R + 8
+NEAR = 2
+PART = 2 * NEAR * R
+PLANES = PART
+SIDES = PLANES + 4 * 2 * NEAR
+NEAR_MESSAGE = SIDES + R
+FAR_MESSAGE = SIDES
 
 HOP_NEXT = 0.3
 TWIST_COS = 0.4535961214255773
@@ -118,9 +121,9 @@
     sites = jnp.zeros((R, BLOCK), F32)
     for p, plane in enumerate(site_planes(ends[0], ends[1])):
         sites = jnp.where(lane16 // 8 == p, pltpu.roll(plane, 8 * p + 4, 1), sites)
-    sites = sites.astype(BF16)
-    out[(me + 1) % columns, SITE_EDGE : SITE_EDGE + R, :] = sites
-    out[(me + columns - 1) % columns, SITE_EDGE : SITE_EDGE + R, :] = sites
+    sites = jnp.where(lane < 32, sites[0:8], pltpu.roll(sites[8:16], 32, 1)).astype(BF16)
+    out[(me + 1) % columns, SITE_EDGE : SITE_EDGE + 8, :] = sites
+    out[(me + columns - 1) % columns, SITE_EDGE : SITE_EDGE + 8, :] = sites
 
 
 def edge_tiles(columns, plan, received):
@@ -137,36 +140,39 @@
     low = (me + columns - 1) % columns
     high = (me + 1) % columns
     sites = jnp.where(
-        last_half,
-        received[low, SITE_EDGE : SITE_EDGE + R, :].astype(F32),
-        received[high, SITE_EDGE : SITE_EDGE + R, :].astype(F32),
+        last_half[0:8],
+        received[low, SITE_EDGE : SITE_EDGE + 8, :].astype(F32),
+        received[high, SITE_EDGE : SITE_EDGE + 8, :].astype(F32),
     )
     return tile, sites
 
 
-def arrange_kernel(columns, plan, received, disorder, vacancy, low_out, high_out, rows):
+def arrange_kernel(
+    columns, plan, received, disorder, vacancy, low_near, high_near, low_far, high_far, planes
+):
     me = lax.axis_index("gy")
+    outs = ((low_near, 0), (high_near, WIDTH_X - NEAR), (low_far, NEAR), (high_far, NEAR + NEAR))
+    size = NEAR * R
     for b in range(BLOCKS):
         slot = plan[me * BLOCKS + b] // BLOCKS
         lanes = slice(b * BLOCK, (b + 1) * BLOCK)
         for s in range(2):
-            base = s * WIDTH_X * R
-            size = HALO * R
-            low_out[s * size : (s + 1) * size, lanes] = received[slot, base : base + size, :]
-            high_out[s * size : (s + 1) * size, lanes] = received[
-                slot, base + (WIDTH_X - HALO) * R : base + WIDTH_X * R, :
-            ]
+            for out, x in outs:
+                base = (s * WIDTH_X + x) * R
+                out[s * size : (s + 1) * size, lanes] = received[slot, base : base + size, :]
     tile, sites = edge_tiles(columns, plan, received)
-    for out in (low_out, high_out):
-        out[HALF : HALF + R, 0:BLOCK] = tile.astype(BF16)
-        out[HALF : HALF + R, BLOCK : 2 * BLOCK] = sites.astype(BF16)
-        out[HALF : HALF + R, 2 * BLOCK : OWN] = jnp.zeros((R, OWN - 2 * BLOCK), BF16)
+    for out in (low_near, high_near):
+        out[SIDES : SIDES + R, 0:BLOCK] = tile.astype(BF16)
+        out[SIDES : SIDES + 8, BLOCK : 2 * BLOCK] = sites.astype(BF16)
+        out[SIDES + 8 : SIDES + R, BLOCK : 2 * BLOCK] = jnp.zeros((8, BLOCK), BF16)
+        out[SIDES : SIDES + R, 2 * BLOCK : OWN] = jnp.zeros((R, OWN - 2 * BLOCK), BF16)
     for s in range(2):
         for p, plane in enumerate(site_planes(disorder[s], vacancy[s].astype(F32))):
-            rows[0, p * 8 + s * HALO : p * 8 + (s + 1) * HALO, :] = plane[0:HALO]
-            rows[1, p * 8 + s * HALO : p * 8 + (s + 1) * HALO, :] = plane[WIDTH_X - HALO :]
-    low_out[PLANES:MESSAGE, :] = rows[0].astype(BF16)
-    high_out[PLANES:MESSAGE, :] = rows[1].astype(BF16)
+            row = p * 2 * NEAR + s * NEAR
+            for i, (_, x) in enumerate(outs):
+                planes[i, row : row + NEAR, :] = plane[x : x + NEAR]
+    for i, (out, _) in enumerate(outs):
+        out[PLANES:SIDES, :] = planes[i].astype(BF16)
 
 
 def fill_sites(level, factor, s, rows, onsite, kept, source, first):
@@ -174,8 +180,8 @@
     in_halo = (lane < HALO) | (lane >= BLOCK - HALO)
     side_level = jnp.zeros((8, BLOCK), F32)
     for p in range(3):
-        side_level = side_level + pltpu.roll(source, BLOCK - 4 - 8 * p, 1)
-    side_keep = pltpu.roll(source, BLOCK - 4 - 8 * 3, 1)
+        side_level = side_level + pltpu.roll(source, BLOCK - 4 - 8 * p - 32 * s, 1)
+    side_keep = pltpu.roll(source, BLOCK - 4 - 8 * 3 - 32 * s, 1)
     side_level = jnp.where(in_halo, side_level, 0.0)
     side_keep = jnp.where(in_halo, side_keep, 0.0)
     kept_rows = []
@@ -188,6 +194,28 @@
         factor[s, row] = kep * (2.0 * COS / SPREAD)
         kept_rows.append(kep)
     return kept_rows
+
+
+def unpack_rows(message, near, level, factor, start, base, x):
+    planes = message[PLANES:SIDES, :].astype(F32)
+    tile = near[SIDES : SIDES + R, 0:BLOCK].astype(F32)
+    sites = near[SIDES : SIDES + 8, BLOCK : 2 * BLOCK].astype(F32)
+    step = 2 * NEAR
+    onsite = planes[0:step] + planes[step : 2 * step] + planes[2 * step : 3 * step]
+    keep = planes[3 * step : 4 * step]
+    for s in range(2):
+        some = slice(s * NEAR, (s + 1) * NEAR)
+        kept = fill_sites(
+            level, factor, s, range(base, base + NEAR), onsite[some], keep[some], sites, x
+        )
+        for i in range(NEAR):
+            index = (s * NEAR + i) * R
+            q = s * WIDTH_X + x + i
+            side = pltpu.roll(tile, (BLOCK - 4 - 8 * q) % BLOCK, 1)
+            value = jnp.concatenate([message[index : index + R, :].astype(F32), side], axis=1)
+            for h in range(2):
+                part = slice(h * 8, (h + 1) * 8)
+                start[s, base + i, part, :] = value[part] * kept[i]
 
 
 def span(level, factor, term, old, now, new, row, count=2):
@@ -284,7 +312,7 @@
 
 def interior_kernel(
     columns, plan, received, disorder, vacancy,
-    level, factor, start, real1, imag1, real2, imag2, sums,
+    level, factor, start, real1, imag1, real2, imag2, sums, own_sites, own_start,
 ):
     real2, imag2 = Rows(real2, HALO), Rows(imag2, HALO)
     me = lax.axis_index("gy")
@@ -293,16 +321,18 @@
     for s in range(2):
         kept = fill_sites(
             level, factor, s, range(HALO, HALO + WIDTH_X), disorder[s],
-            vacancy[s].astype(F32), sites[s * 8 : (s + 1) * 8], 0,
+            vacancy[s].astype(F32), sites, 0,
         )
         for x in range(WIDTH_X):
             q = s * WIDTH_X + x
             pieces = [received[slots[b], q * R : (q + 1) * R, :].astype(F32) for b in range(BLOCKS)]
             pieces.append(pltpu.roll(tile, (BLOCK - 4 - 8 * q) % BLOCK, 1))
             value = jnp.concatenate(pieces, axis=1)
-            for h in range(2):
-                part = slice(h * 8, (h + 1) * 8)
-                start[s, HALO + x, part, :] = value[part] * kept[x]
+            value = value * jnp.concatenate([kept[x], kept[x]], axis=0)
+            start[s, HALO + x] = value
+            own_start[s, x] = value.astype(BF16)
+            own_sites[0, s, x : x + 1, :] = level[s, HALO + x, 0:1, :]
+            own_sites[1, s, x : x + 1, :] = factor[s, HALO + x, 0:1, :]
 
     def one(i, carry):
         row = HALO + 1 + 2 * i
@@ -326,29 +356,11 @@
 
 def border_kernel(
     below, above, level_in, factor_in, start_in, real1_in, imag1_in, real2_in, imag2_in, sums_in,
-    level, factor, start, real1, imag1, real2, imag2, trace_out, sites_out, start_out,
+    level, factor, start, real1, imag1, real2, imag2, trace_out,
 ):
     real2, imag2 = Rows(real2, HALO), Rows(imag2, HALO)
-    for ref, base, shift in ((below, 0, WIDTH_X - HALO), (above, HALO + WIDTH_X, 0)):
-        planes = [ref[PLANES + p * 8 : PLANES + (p + 1) * 8, :].astype(F32) for p in range(4)]
-        onsite = planes[0] + planes[1] + planes[2]
-        sites = ref[HALF : HALF + R, BLOCK : 2 * BLOCK].astype(F32)
-        far = ref[HALF : HALF + R, 0:BLOCK].astype(F32)
-        for s in range(2):
-            some = slice(s * HALO, (s + 1) * HALO)
-            kept = fill_sites(
-                level, factor, s, range(base, base + HALO), onsite[some], planes[3][some],
-                sites[s * 8 : (s + 1) * 8], shift,
-            )
-            for i in range(HALO):
-                index = (s * HALO + i) * R
-                q = s * WIDTH_X + shift + i
-                side = pltpu.roll(far, (BLOCK - 4 - 8 * q) % BLOCK, 1)
-                value = jnp.concatenate([ref[index : index + R, :].astype(F32), side], axis=1)
-                for h in range(2):
-                    part = slice(h * 8, (h + 1) * 8)
-                    start[s, base + i, part, :] = value[part] * kept[i]
-
+    unpack_rows(below, below, level, factor, start, HALO - NEAR, WIDTH_X - NEAR)
+    unpack_rows(above, above, level, factor, start, HALO + WIDTH_X, 0)
     for row in (HALO - 1, HALO + WIDTH_X - 1):
         span(level, factor, 1, None, (start, None), (real1, imag1), row)
     totals = tuple(sums_in[i * 8 : (i + 1) * 8, :] for i in range(2 * SUMS))
@@ -367,26 +379,25 @@
         (((1,), (1,)), ((), ())),
         precision=lax.Precision.HIGHEST, preferred_element_type=F32,
     )
-    for s in range(2):
-        for row in range(ROWS_X):
-            sites_out[0, s, row : row + 1, :] = level[s, row, 0:1, :]
-            sites_out[1, s, row : row + 1, :] = factor[s, row, 0:1, :]
-            start_out[s, row] = start[s, row].astype(BF16)
 
 
 def local_kernel(
-    sites, kept_start, real2_in, imag2_in,
+    below, above, below_far, above_far, own_sites, own_start, real2_in, imag2_in,
     local_out, level, factor, start, real1, imag1, real2, imag2, real3, imag3, real4, products,
 ):
-    real2_in, imag2_in, real4 = Rows(real2_in, HALO), Rows(imag2_in, HALO), Rows(real4, HALO)
+    real4 = Rows(real4, HALO)
     for s in range(2):
-        for row in range(ROWS_X):
-            level[s, row] = jnp.broadcast_to(sites[0, s, row : row + 1, :], (8, LANES))
-            factor[s, row] = jnp.broadcast_to(sites[1, s, row : row + 1, :], (8, LANES))
-            start[s, row] = kept_start[s, row].astype(F32)
-        for row in range(HALO, HALO + WIDTH_X):
-            real2[s, row] = real2_in[s, row, :, :]
-            imag2[s, row] = imag2_in[s, row, :, :]
+        for x in range(WIDTH_X):
+            row = HALO + x
+            level[s, row] = jnp.broadcast_to(own_sites[0, s, x : x + 1, :], (8, LANES))
+            factor[s, row] = jnp.broadcast_to(own_sites[1, s, x : x + 1, :], (8, LANES))
+            start[s, row] = own_start[s, x].astype(F32)
+            real2[s, row] = real2_in[s, x]
+            imag2[s, row] = imag2_in[s, x]
+    unpack_rows(below_far, below, level, factor, start, 0, WIDTH_X - HALO)
+    unpack_rows(below, below, level, factor, start, NEAR, WIDTH_X - NEAR)
+    unpack_rows(above, above, level, factor, start, HALO + WIDTH_X, 0)
+    unpack_rows(above_far, above, level, factor, start, HALO + WIDTH_X + NEAR, NEAR)
 
     def one(i, carry):
         span(level, factor, 1, None, (start, None), (real1, imag1), 2 * i + 1)
@@ -458,58 +469,64 @@
             pltpu.SMEM((BLOCKS + 1,), jnp.int32),
             pltpu.SemaphoreType.DMA((4,)),
         ],
-        compiler_params=pltpu.CompilerParams(vmem_limit_bytes=60 * 1024 * 1024),
+        compiler_params=pltpu.CompilerParams(vmem_limit_bytes=16 * 1024 * 1024),
         name="pack",
-    )(plan, stored_vectors, disorder, vacancy)
+    )(*(
+        pltpu.with_memory_space_constraint(x, pltpu.HBM)
+        for x in (plan, stored_vectors, disorder, vacancy)
+    ))
     received = lax.all_to_all(outgoing, "gy", split_axis=0, concat_axis=0, tiled=True)
 
-    message = jax.ShapeDtypeStruct((MESSAGE, OWN), BF16)
-    low_rows, high_rows = pl.pallas_call(
+    near_message = jax.ShapeDtypeStruct((NEAR_MESSAGE, OWN), BF16)
+    far_message = jax.ShapeDtypeStruct((FAR_MESSAGE, OWN), BF16)
+    low_near, high_near, low_far, high_far = pl.pallas_call(
         functools.partial(arrange_kernel, columns),
-        out_shape=(message, message),
+        out_shape=(near_message, near_message, far_message, far_message),
         in_specs=[smem, vmem, vmem, vmem],
-        out_specs=(vmem, vmem),
-        scratch_shapes=[pltpu.VMEM((2, 4 * 2 * HALO, OWN), F32)],
+        out_specs=(vmem,) * 4,
+        scratch_shapes=[pltpu.VMEM((4, 4 * 2 * NEAR, OWN), F32)],
         compiler_params=params,
         name="arrange",
     )(plan, received, disorder, vacancy)
     up = [(i, (i + 1) % rows) for i in range(rows)]
     down = [(target, source) for source, target in up]
-    below = lax.ppermute(high_rows, "gx", up)
-    above = lax.ppermute(low_rows, "gx", down)
+    below = lax.ppermute(high_near, "gx", up)
+    above = lax.ppermute(low_near, "gx", down)
+    below_far = lax.ppermute(high_far, "gx", up)
+    above_far = lax.ppermute(low_far, "gx", down)
 
     site = jax.ShapeDtypeStruct((2, ROWS_X, 8, LANES), F32)
     field = jax.ShapeDtypeStruct((2, ROWS_X, R, LANES), F32)
     narrow = jax.ShapeDtypeStruct((2, WIDTH_X, R, LANES), F32)
     state = (site, site) + (field,) * 3 + (narrow,) * 2
-    inner = pl.pallas_call(
+    *inner, own_sites, own_start = pl.pallas_call(
         functools.partial(interior_kernel, columns),
-        out_shape=state + (jax.ShapeDtypeStruct((2 * SUMS * 8, BLOCK), F32),),
+        out_shape=state + (
+            jax.ShapeDtypeStruct((2 * SUMS * 8, BLOCK), F32),
+            jax.ShapeDtypeStruct((2, 2, WIDTH_X, LANES), F32),
+            jax.ShapeDtypeStruct((2, WIDTH_X, R, LANES), BF16),
+        ),
         in_specs=[smem, vmem, vmem, vmem],
-        out_specs=(vmem,) * 8,
+        out_specs=(vmem,) * 10,
         compiler_params=params,
         cost_estimate=pl.CostEstimate(flops=10**7, bytes_accessed=8 * 10**6, transcendentals=0),
         name="interior",
     )(plan, received, disorder, vacancy)
     outputs = pl.pallas_call(
         border_kernel,
-        out_shape=state + (
-            jax.ShapeDtypeStruct((devices, TERMS * R), F32),
-            jax.ShapeDtypeStruct((2, 2, ROWS_X, LANES), F32),
-            jax.ShapeDtypeStruct(field.shape, BF16),
-        ),
+        out_shape=state + (jax.ShapeDtypeStruct((devices, TERMS * R), F32),),
         in_specs=[vmem] * 10,
-        out_specs=(vmem,) * 10,
+        out_specs=(vmem,) * 8,
         input_output_aliases={2 + i: i for i in range(7)},
         compiler_params=params,
         name="border",
     )(below, above, *inner)
-    real2, imag2, partial, sites, start = outputs[5:]
+    real2, imag2, partial = outputs[5:]
     shared = lax.all_to_all(partial, ("gx", "gy"), split_axis=0, concat_axis=0, tiled=True)
     local_moments = pl.pallas_call(
         local_kernel,
         out_shape=jax.ShapeDtypeStruct((TERMS, 2, WIDTH_X, OWN), F32),
-        in_specs=[vmem] * 4,
+        in_specs=[vmem] * 8,
         out_specs=vmem,
         scratch_shapes=[pltpu.VMEM(site.shape, F32)] * 2
         + [pltpu.VMEM(field.shape, F32)] * 7
@@ -520,7 +537,7 @@
         compiler_params=pltpu.CompilerParams(vmem_limit_bytes=16 * 1024 * 1024),
         cost_estimate=pl.CostEstimate(flops=10**7, bytes_accessed=8 * 10**6, transcendentals=0),
         name="local_moments",
-    )(sites, start, real2, imag2)
+    )(below, above, below_far, above_far, own_sites, own_start, real2, imag2)
     trace = pl.pallas_call(
         functools.partial(total_kernel, 2 * WIDTH_X * rows * OWN * columns),
         out_shape=jax.ShapeDtypeStruct((TERMS, R), F32),

time: 56 us -> 54.3 us (0.970)
  waiting for transfers between devices: 6.95 us -> 4.15 us
  starting transfers between devices: 9.52 us -> 11.8 us
  Pallas kernels: 13.4 us -> 12.7 us
    ppermute x2 -> x4, waiting for transfers between devices: 2.82 us -> 0.04 us  [the longest x1 0.04 us: local(): above = lax.ppermute(low_near, 'gx', down)]
    ppermute x2 -> x4, starting transfers between devices: 3.63 us -> 5.35 us  [the longest x1 3.6 us: local(): below = lax.ppermute(high_near, 'gx', up)]
    pallas_call x1, Pallas kernels: 2.42 us -> 1.46 us  [local(): pl.pallas_call(functools.partial(pack_kernel, columns), out_shape=jax.Sha...]
    all_to_all x1, starting transfers between devices: 5.89 us -> 6.48 us  [local(): lax.all_to_all(partial, ('gx', 'gy'), split_axis=0, concat_axis=0, tiled=...]
  transfers between devices with their start and end apart: 3 -> 5, of which waited for: 3 -> 1; matrix products, arithmetic and copies ran while one was open for 0% -> 0% of each run, Pallas kernels for 14% -> 18%
where the time goes in v4:
time: 54.3 us; the launch traced here: 54.1 us
  blocking collectives  24.6 us (45%)
  Pallas kernels  12.7 us (23%)
  starting transfers between devices  11.8 us (22%)
  waiting for transfers between devices  4.15 us (8%)
  between operations  0.72 us (1%)
    all_to_all x1, blocking collectives, local(): lax.all_to_all(outgoing, 'gy', split_axis=0, concat_axis=0, tiled=True)  24.6 us
    all_to_all x1, starting transfers between devices, local(): lax.all_to_all(partial, ('gx', 'gy'), split_axis=0, concat_axis=0, tiled=...  6.48 us
    pallas_call x1, Pallas kernels, local(): pl.pallas_call(local_kernel, out_shape=jax.ShapeDtypeStruct((TERMS, 2, WI...  5.46 us
    all_to_all x1, waiting for transfers between devices, local(): lax.all_to_all(partial, ('gx', 'gy'), split_axis=0, concat_axis=0, tiled=...  4.1 us
    ppermute x1, starting transfers between devices, local(): below = lax.ppermute(high_near, 'gx', up)  3.6 us
    pallas_call x1, Pallas kernels, local(): pl.pallas_call(border_kernel, out_shape=state + (jax.ShapeDtypeStruct((de...  2.26 us
    pallas_call x1, Pallas kernels, local(): pl.pallas_call(functools.partial(interior_kernel, columns), out_shape=sta...  2.24 us
    ppermute x1, starting transfers between devices, local(): below_far = lax.ppermute(high_far, 'gx', up)  1.74 us
  transfers between devices with their start and end apart: 5, of which 1 were waited for; matrix products, arithmetic and copies ran while one was open for 0% of the time, Pallas kernels for 18%

profile of v4, /device:TPU:1, one launch (start us, length us, event | category | flops | bytes accessed | tf_op | source)
XLA Modules:
  0.0 54.1 jit_solution(6282617569578398964)
XLA Ops:
  0.6 1.5 %pack.1 = bf16[16,280,128]{2,1,0:T(8,128)(2,1)S(1)} custom-call(s32[64]{0:T(128)} %plan.3, bf16[2,16,8,512]{3,2,1,0:T(8,128)(2,1)} %stored_hbm.1, f32[2,8,512]{2,1,0:T(8,128)} %disorder.3, s32[2,8,512]{2,1,0:T(8,128)} %vacancy.3), custom_call_target="tpu_custom_call" | custom-call | tf_op jit(solution)/shard_map/pack/pallas_call | solution.py:458
  2.1 0.0 copy-start
  2.1 0.0 copy-start.1
  2.1 0.0 copy-start.2
  2.1 24.6 %all_to_all.16.received = bf16[16,280,128]{2,1,0:T(8,128)(2,1)S(1)} all-to-all(bf16[16,280,128]{2,1,0:T(8,128)(2,1)S(1)} %pack.1), channel_id=1, replica_groups=mesh['gx'=8,'gy'=16] {'gy'}, dimensions={0} | all-to-all | bytes 2293760 | tf_op jit(solution)/shard_map/all_to_all | solution.py:478
  26.7 0.0 copy-done
  26.7 0.0 copy-done.1
  26.8 0.0 copy-done.2
  26.8 0.7 %arrange.1 = (bf16[96,512]{1,0:T(8,128)(2,1)S(1)}, bf16[96,512]{1,0:T(8,128)(2,1)S(1)}, bf16[80,512]{1,0:T(8,128)(2,1)S(1)}, bf16[80,512]{1,0:T(8,128)(2,1)S(1)}) custom-call(s32[64]{0:T(128)S(1)} %copy-done.2, bf16[16,280,128]{2,1,0:T(8,128)(2,1)S(1)} %all_to_all.16.received, f32[2,8,512]{2,1,0:T(8,128)S(1)} %copy-done, s32[2,8,512]{2,1,0:T(8,128)S(1)} %copy-done.1), custom_call_target="tpu_custom_call" | custom-call | tf_op jit(solution)/shard_map/arrange/pallas_call | solution.py:482
  27.4 3.6 %collective-permute-start = (bf16[96,512]{1,0:T(8,128)(2,1)S(1)}, bf16[96,512]{1,0:T(8,128)(2,1)S(1)}, u32[]{:S(2)}, u32[]{:S(2)}) collective-permute-start(bf16[96,512]{1,0:T(8,128)(2,1)S(1)} %get-tuple-element.19), channel_id=1, source_target_pairs={{0,16},{16,32},{32,48},{48,64},{64,80},{80,96},{96,112},{112,0},{1... | collective-permute-start | bytes 294920 | tf_op jit(solution)/shard_map/ppermute | solution.py:493
  31.0 0.0 collective-permute-start.1
  31.0 1.7 %collective-permute-start.2 = (bf16[80,512]{1,0:T(8,128)(2,1)S(1)}, bf16[80,512]{1,0:T(8,128)(2,1)S(1)}, u32[]{:S(2)}, u32[]{:S(2)}) collective-permute-start(bf16[80,512]{1,0:T(8,128)(2,1)S(1)} %get-tuple-element.21), channel_id=1, source_target_pairs={{0,16},{16,32},{32,48},{48,64},{64,80},{80,96},{96,112},{112,0},{1... | collective-permute-start | bytes 245768 | tf_op jit(solution)/shard_map/ppermute | solution.py:495
  32.8 0.0 collective-permute-start.3
  32.8 2.2 %interior.1 = (f32[2,16,8,640]{3,2,1,0:T(8,128)S(1)}, f32[2,16,8,640]{3,2,1,0:T(8,128)S(1)}, f32[2,16,16,640]{3,2,1,0:T(8,128)S(1)}, f32[2,16,16,640]{3,2,1,0:T(...) custom-call(s32[64]{0:T(128)S(1)} %copy-done.2, ...), custom_call_target="tpu_custom_call" | custom-call | flops 10000000 | bytes 8000000 | tf_op jit(solution)/shard_map/interior/pallas_call | solution.py:502
  35.0 0.0 collective-permute-done.below
  35.0 0.0 collective-permute-done.1.above
  35.1 2.3 %border.1 = (f32[2,16,8,640]{3,2,1,0:T(8,128)S(1)}, f32[2,16,8,640]{3,2,1,0:T(8,128)S(1)}, f32[2,16,16,640]{3,2,1,0:T(8,128)S(1)}, f32[2,16,16,640]{3,2,1,0:T(8,...) custom-call(bf16[96,512]{1,0:T(8,128)(2,1)S(1)} %collective-permute-, ...), custom_call_target="tpu_custom_call", output_to_operand_aliasing={{0}: (2, {}), {1}: (3, {}), {2}: (4, {}), {3}: (5, {}), {4}... | custom-call | tf_op jit(solution)/shard_map/border/pallas_call | solution.py:515
  37.3 6.5 %all-to-all-start.1 = ((f32[128,1,64]{2,1,0:T(1,128)}), f32[128,1,64]{2,1,0:T(1,128)S(1)}, u32[]{:S(2)}, u32[]{:S(2)}) async-start(f32[128,1,64]{2,1,0:T(1,128)} %bitcast.1), calls=%async_computation.1 | async-start | bytes 131072 | tf_op jit(solution)/shard_map/all_to_all | solution.py:525
  43.8 0.0 collective-permute-done.2.below_far
  43.8 0.0 collective-permute-done.3.above_far
  43.8 5.5 %local_moments.1 = f32[4,2,8,512]{3,2,1,0:T(8,128)} custom-call(bf16[96,512]{1,0:T(8,128)(2,1)S(1)} %collective-permute-done.below, bf16[96,512]{1,0:T(8,128)(2,1)S(1)} %collective-permute-done.1.above, bf16[80,512]{1,0:T(8,128)(2,1)S(1)} %collective-permute-done.2.below_far, bf16[80,512]{1,0:T(8,128)(2,1)S(1)} %collective-permute-done.3.above_far, ...), custom_call_target="tpu_custom_call" | custom-call | flops 10000000 | bytes 8000000 | tf_op jit(solution)/shard_map/local_moments/pallas_call | solution.py:526
  49.3 4.1 %all-to-all-done.1 = f32[128,1,64]{2,1,0:T(1,128)S(1)} async-done(((f32[128,1,64]{2,1,0:T(1,128)}), f32[128,1,64]{2,1,0:T(1,128)S(1)}, u32[]{:S(2)}, u32[]{:S(2)}) %all-to-all-start.1) | async-done | bytes 32800 | tf_op jit(solution)/shard_map/all_to_all | solution.py:525
  53.4 0.7 %total.1 = f32[4,16]{1,0:T(4,128)} custom-call(f32[128,64]{1,0:T(8,128)S(1)} %bitcast.4), custom_call_target="tpu_custom_call" | custom-call | tf_op jit(solution)/shard_map/total/pallas_call | solution.py:541
Async XLA Ops:
  2.1 24.7 %copy-start = (f32[2,8,512]{2,1,0:T(8,128)S(1)}, f32[2,8,512]{2,1,0:T(8,128)}, u32[]{:S(2)}) copy-start(f32[2,8,512]{2,1,0:T(8,128)} %disorder.3) | copy-start | bytes 98308
  2.1 24.6 %copy-start.1 = (s32[2,8,512]{2,1,0:T(8,128)S(1)}, s32[2,8,512]{2,1,0:T(8,128)}, u32[]{:S(2)}) copy-start(s32[2,8,512]{2,1,0:T(8,128)} %vacancy.3) | copy-start | bytes 98308
  2.1 24.6 %copy-start.2 = (s32[64]{0:T(128)S(1)}, s32[64]{0:T(128)}, u32[]{:S(2)}) copy-start(s32[64]{0:T(128)} %plan.3) | copy-start | bytes 772
  27.4 7.6 %collective-permute-start = (bf16[96,512]{1,0:T(8,128)(2,1)S(1)}, bf16[96,512]{1,0:T(8,128)(2,1)S(1)}, u32[]{:S(2)}, u32[]{:S(2)}) collective-permute-start(bf16[96,512]{1,0:T(8,128)(2,1)S(1)} %get-tuple-element.19), channel_id=1, source_target_pairs={{0,16},{16,32},{32,48},{48,64},{64,80},{80,96},{96,112},{112,0},{1... | collective-permute-start | bytes 294920 | tf_op jit(solution)/shard_map/ppermute | solution.py:493
  31.0 4.0 %collective-permute-start.1 = (bf16[96,512]{1,0:T(8,128)(2,1)S(1)}, bf16[96,512]{1,0:T(8,128)(2,1)S(1)}, u32[]{:S(2)}, u32[]{:S(2)}) collective-permute-start(bf16[96,512]{1,0:T(8,128)(2,1)S(1)} %get-tuple-element.20), channel_id=1, source_target_pairs={{16,0},{32,16},{48,32},{64,48},{80,64},{96,80},{112,96},{0,112},{1... | collective-permute-start | bytes 294920 | tf_op jit(solution)/shard_map/ppermute | solution.py:494
  31.0 12.8 %collective-permute-start.2 = (bf16[80,512]{1,0:T(8,128)(2,1)S(1)}, bf16[80,512]{1,0:T(8,128)(2,1)S(1)}, u32[]{:S(2)}, u32[]{:S(2)}) collective-permute-start(bf16[80,512]{1,0:T(8,128)(2,1)S(1)} %get-tuple-element.21), channel_id=1, source_target_pairs={{0,16},{16,32},{32,48},{48,64},{64,80},{80,96},{96,112},{112,0},{1... | collective-permute-start | bytes 245768 | tf_op jit(solution)/shard_map/ppermute | solution.py:495
  32.8 11.1 %collective-permute-start.3 = (bf16[80,512]{1,0:T(8,128)(2,1)S(1)}, bf16[80,512]{1,0:T(8,128)(2,1)S(1)}, u32[]{:S(2)}, u32[]{:S(2)}) collective-permute-start(bf16[80,512]{1,0:T(8,128)(2,1)S(1)} %get-tuple-element.22), channel_id=1, source_target_pairs={{16,0},{32,16},{48,32},{64,48},{80,64},{96,80},{112,96},{0,112},{1... | collective-permute-start | bytes 245768 | tf_op jit(solution)/shard_map/ppermute | solution.py:496
  37.3 16.1 %all-to-all-start.1 = ((f32[128,1,64]{2,1,0:T(1,128)}), f32[128,1,64]{2,1,0:T(1,128)S(1)}, u32[]{:S(2)}, u32[]{:S(2)}) async-start(f32[128,1,64]{2,1,0:T(1,128)} %bitcast.1), calls=%async_computation.1 | async-start | bytes 131072 | tf_op jit(solution)/shard_map/all_to_all | solution.py:525

commit v5 on v4

--- a/solution.py
+++ b/solution.py
@@ -50,7 +50,7 @@
 
 
 def pack_kernel(
-    columns, plan_hbm, stored_hbm, disorder_hbm, vacancy_hbm, out,
+    columns, plan_hbm, stored_hbm, disorder_hbm, vacancy_hbm, out, table,
     plan, stored, disorder, vacancy, turned, where_to, arrived,
 ):
     copies = [
@@ -73,6 +73,11 @@
 
     lax.fori_loop(0, BLOCKS * columns, find, 0, unroll=8)
 
+    total = BLOCKS * columns
+    sources = [first + b for b in range(BLOCKS)]
+    sources += [(first + total - 1) % total, (first + BLOCKS) % total]
+    for i, k in enumerate(sources):
+        table[i : i + 1, :] = jnp.full((1, BLOCK), plan[k] // BLOCKS, jnp.int32)
     copies[1].wait()
     for b in range(BLOCKS):
         block = stored[:, :, :, b * BLOCK : (b + 1) * BLOCK]
@@ -126,11 +131,14 @@
     out[(me + columns - 1) % columns, SITE_EDGE : SITE_EDGE + 8, :] = sites
 
 
-def edge_tiles(columns, plan, received):
+def source_of(table, i):
+    return table[i : i + 1, 0:1][0, 0]
+
+
+def edge_tiles(columns, table, received):
     me = lax.axis_index("gy")
-    total = BLOCKS * columns
-    left = plan[(me * BLOCKS + total - 1) % total] // BLOCKS
-    right = plan[(me * BLOCKS + BLOCKS) % total] // BLOCKS
+    left = source_of(table, BLOCKS)
+    right = source_of(table, BLOCKS + 1)
     last_half = lane_index(R, BLOCK) % 8 < 4
     tile = jnp.where(
         last_half,
@@ -148,19 +156,18 @@
 
 
 def arrange_kernel(
-    columns, plan, received, disorder, vacancy, low_near, high_near, low_far, high_far, planes
+    columns, table, received, disorder, vacancy, low_near, high_near, low_far, high_far, planes
 ):
-    me = lax.axis_index("gy")
     outs = ((low_near, 0), (high_near, WIDTH_X - NEAR), (low_far, NEAR), (high_far, NEAR + NEAR))
     size = NEAR * R
     for b in range(BLOCKS):
-        slot = plan[me * BLOCKS + b] // BLOCKS
+        slot = source_of(table, b)
         lanes = slice(b * BLOCK, (b + 1) * BLOCK)
         for s in range(2):
             for out, x in outs:
                 base = (s * WIDTH_X + x) * R
                 out[s * size : (s + 1) * size, lanes] = received[slot, base : base + size, :]
-    tile, sites = edge_tiles(columns, plan, received)
+    tile, sites = edge_tiles(columns, table, received)
     for out in (low_near, high_near):
         out[SIDES : SIDES + R, 0:BLOCK] = tile.astype(BF16)
         out[SIDES : SIDES + 8, BLOCK : 2 * BLOCK] = sites.astype(BF16)
@@ -311,13 +318,12 @@
 
 
 def interior_kernel(
-    columns, plan, received, disorder, vacancy,
+    columns, table, received, disorder, vacancy,
     level, factor, start, real1, imag1, real2, imag2, sums, own_sites, own_start,
 ):
     real2, imag2 = Rows(real2, HALO), Rows(imag2, HALO)
-    me = lax.axis_index("gy")
-    tile, sites = edge_tiles(columns, plan, received)
-    slots = [plan[me * BLOCKS + b] // BLOCKS for b in range(BLOCKS)]
+    tile, sites = edge_tiles(columns, table, received)
+    slots = [source_of(table, b) for b in range(BLOCKS)]
     for s in range(2):
         kept = fill_sites(
             level, factor, s, range(HALO, HALO + WIDTH_X), disorder[s],
@@ -450,16 +456,18 @@
     columns = lax.axis_size("gy")
     rows = lax.axis_size("gx")
     devices = rows * columns
-    smem = pl.BlockSpec(memory_space=pltpu.SMEM)
     vmem = pl.BlockSpec(memory_space=pltpu.VMEM)
     params = pltpu.CompilerParams(vmem_limit_bytes=8 * 1024 * 1024)
 
     hbm = pl.BlockSpec(memory_space=pltpu.HBM)
-    outgoing = pl.pallas_call(
+    outgoing, table = pl.pallas_call(
         functools.partial(pack_kernel, columns),
-        out_shape=jax.ShapeDtypeStruct((columns, SLOT_ROWS, BLOCK), BF16),
+        out_shape=(
+            jax.ShapeDtypeStruct((columns, SLOT_ROWS, BLOCK), BF16),
+            jax.ShapeDtypeStruct((8, BLOCK), jnp.int32),
+        ),
         in_specs=[hbm] * 4,
-        out_specs=vmem,
+        out_specs=(vmem, vmem),
         scratch_shapes=[
             pltpu.SMEM(plan.shape, plan.dtype),
             pltpu.VMEM(stored_vectors.shape, stored_vectors.dtype),
@@ -482,12 +490,12 @@
     low_near, high_near, low_far, high_far = pl.pallas_call(
         functools.partial(arrange_kernel, columns),
         out_shape=(near_message, near_message, far_message, far_message),
-        in_specs=[smem, vmem, vmem, vmem],
+        in_specs=[vmem] * 4,
         out_specs=(vmem,) * 4,
         scratch_shapes=[pltpu.VMEM((4, 4 * 2 * NEAR, OWN), F32)],
         compiler_params=params,
         name="arrange",
-    )(plan, received, disorder, vacancy)
+    )(table, received, disorder, vacancy)
     up = [(i, (i + 1) % rows) for i in range(rows)]
     down = [(target, source) for source, target in up]
     below = lax.ppermute(high_near, "gx", up)
@@ -506,12 +514,12 @@
             jax.ShapeDtypeStruct((2, 2, WIDTH_X, LANES), F32),
             jax.ShapeDtypeStruct((2, WIDTH_X, R, LANES), BF16),
         ),
-        in_specs=[smem, vmem, vmem, vmem],
+        in_specs=[vmem] * 4,
         out_specs=(vmem,) * 10,
         compiler_params=params,
         cost_estimate=pl.CostEstimate(flops=10**7, bytes_accessed=8 * 10**6, transcendentals=0),
         name="interior",
-    )(plan, received, disorder, vacancy)
+    )(table, received, disorder, vacancy)
     outputs = pl.pallas_call(
         border_kernel,
         out_shape=state + (jax.ShapeDtypeStruct((devices, TERMS * R), F32),),

time: 54.3 us -> 53.1 us (0.978)
  Pallas kernels: 12.7 us -> 11.7 us
    pallas_call x1, Pallas kernels: 0.66 us -> 0.1 us  [local(): pl.pallas_call(functools.partial(arrange_kernel, columns), out_shape=(nea...]
  transfers between devices with their start and end apart: 5 -> 5, of which waited for: 1 -> 2; matrix products, arithmetic and copies ran while one was open for 0% -> 0% of each run, Pallas kernels for 18% -> 18%
where the time goes in v5:
time: 53.1 us; the launch traced here: 52.9 us
  blocking collectives  24.5 us (46%)
  Pallas kernels  11.7 us (22%)
  starting transfers between devices  11.3 us (21%)
  waiting for transfers between devices  4.67 us (9%)
  between operations  0.71 us (1%)
    all_to_all x1, blocking collectives, local(): lax.all_to_all(outgoing, 'gy', split_axis=0, concat_axis=0, tiled=True)  24.5 us
    all_to_all x1, starting transfers between devices, local(): lax.all_to_all(partial, ('gx', 'gy'), split_axis=0, concat_axis=0, tiled=...  5.95 us
    pallas_call x1, Pallas kernels, local(): pl.pallas_call(local_kernel, out_shape=jax.ShapeDtypeStruct((TERMS, 2, WI...  5.46 us
    all_to_all x1, waiting for transfers between devices, local(): lax.all_to_all(partial, ('gx', 'gy'), split_axis=0, concat_axis=0, tiled=...  4.1 us
    ppermute x1, starting transfers between devices, local(): below = lax.ppermute(high_near, 'gx', up)  3.6 us
    pallas_call x1, Pallas kernels, local(): pl.pallas_call(border_kernel, out_shape=state + (jax.ShapeDtypeStruct((de...  2.26 us
    ppermute x1, starting transfers between devices, local(): below_far = lax.ppermute(high_far, 'gx', up)  1.74 us
    pallas_call x1, Pallas kernels, local(): pl.pallas_call(functools.partial(interior_kernel, columns), out_shape=sta...  1.71 us
  transfers between devices with their start and end apart: 5, of which 2 were waited for; matrix products, arithmetic and copies ran while one was open for 0% of the time, Pallas kernels for 18%

profile of v5, /device:TPU:1, one launch (start us, length us, event | category | flops | bytes accessed | tf_op | source)
XLA Modules:
  0.0 52.9 jit_solution(6331938388784648762)
XLA Ops:
  0.6 0.0 copy-start.1
  0.6 0.0 copy-start
  0.7 1.5 %pack.1 = (bf16[16,280,128]{2,1,0:T(8,128)(2,1)S(1)}, s32[8,128]{1,0:T(8,128)S(1)}) custom-call(s32[64]{0:T(128)} %plan_hbm.1, bf16[2,16,8,512]{3,2,1,0:T(8,128)(2,1)} %stored_hbm.1, f32[2,8,512]{2,1,0:T(8,128)} %disorder.3, s32[2,8,512]{2,1,0:T(8,128)} %vacancy.3), custom_call_target="tpu_custom_call" | custom-call | tf_op jit(solution)/shard_map/pack/pallas_call | solution.py:463
  2.2 24.5 %all_to_all.16.received = bf16[16,280,128]{2,1,0:T(8,128)(2,1)S(1)} all-to-all(bf16[16,280,128]{2,1,0:T(8,128)(2,1)S(1)} %get-tuple-element.22), channel_id=1, replica_groups=mesh['gx'=8,'gy'=16] {'gy'}, dimensions={0} | all-to-all | bytes 2293760 | tf_op jit(solution)/shard_map/all_to_all | solution.py:486
  26.7 0.0 copy-done.1
  26.7 0.0 copy-done
  26.7 0.1 arrange.1
  26.8 3.6 %collective-permute-start = (bf16[96,512]{1,0:T(8,128)(2,1)S(1)}, bf16[96,512]{1,0:T(8,128)(2,1)S(1)}, u32[]{:S(2)}, u32[]{:S(2)}) collective-permute-start(bf16[96,512]{1,0:T(8,128)(2,1)S(1)} %get-tuple-element.23), channel_id=1, source_target_pairs={{0,16},{16,32},{32,48},{48,64},{64,80},{80,96},{96,112},{112,0},{1... | collective-permute-start | bytes 294920 | tf_op jit(solution)/shard_map/ppermute | solution.py:501
  30.4 0.0 collective-permute-start.1
  30.4 1.7 %collective-permute-start.2 = (bf16[80,512]{1,0:T(8,128)(2,1)S(1)}, bf16[80,512]{1,0:T(8,128)(2,1)S(1)}, u32[]{:S(2)}, u32[]{:S(2)}) collective-permute-start(bf16[80,512]{1,0:T(8,128)(2,1)S(1)} %get-tuple-element.25), channel_id=1, source_target_pairs={{0,16},{16,32},{32,48},{48,64},{64,80},{80,96},{96,112},{112,0},{1... | collective-permute-start | bytes 245768 | tf_op jit(solution)/shard_map/ppermute | solution.py:503
  32.1 0.0 collective-permute-start.3
  32.1 1.7 %interior.1 = (f32[2,16,8,640]{3,2,1,0:T(8,128)S(1)}, f32[2,16,8,640]{3,2,1,0:T(8,128)S(1)}, f32[2,16,16,640]{3,2,1,0:T(8,128)S(1)}, f32[2,16,16,640]{3,2,1,0:T(...) custom-call(s32[8,128]{1,0:T(8,128)S(1)} %get-tuple-element.21.table, ...), custom_call_target="tpu_custom_call" | custom-call | flops 10000000 | bytes 8000000 | tf_op jit(solution)/shard_map/interior/pallas_call | solution.py:510
  33.9 0.0 collective-permute-done.below
  33.9 0.6 %collective-permute-done.1.above = bf16[96,512]{1,0:T(8,128)(2,1)S(1)} collective-permute-done((bf16[96,512]{1,0:T(8,128)(2,1)S(1)}, bf16[96,512]{1,0:T(8,128)(2,1)S(1)}, u32[]{:S(2)}, u32[]{:S(2)}) %collective-permute-start.1) | collective-permute-done | bytes 98336 | tf_op jit(solution)/shard_map/ppermute | solution.py:502
  34.4 2.3 %border.1 = (f32[2,16,8,640]{3,2,1,0:T(8,128)S(1)}, f32[2,16,8,640]{3,2,1,0:T(8,128)S(1)}, f32[2,16,16,640]{3,2,1,0:T(8,128)S(1)}, f32[2,16,16,640]{3,2,1,0:T(8,...) custom-call(bf16[96,512]{1,0:T(8,128)(2,1)S(1)} %collective-permute-, ...), custom_call_target="tpu_custom_call", output_to_operand_aliasing={{0}: (2, {}), {1}: (3, {}), {2}: (4, {}), {3}: (5, {}), {4}... | custom-call | tf_op jit(solution)/shard_map/border/pallas_call | solution.py:523
  36.7 6.0 %all-to-all-start.1 = ((f32[128,1,64]{2,1,0:T(1,128)}), f32[128,1,64]{2,1,0:T(1,128)S(1)}, u32[]{:S(2)}, u32[]{:S(2)}) async-start(f32[128,1,64]{2,1,0:T(1,128)} %bitcast.1), calls=%async_computation.1 | async-start | bytes 131072 | tf_op jit(solution)/shard_map/all_to_all | solution.py:533
  42.6 0.0 collective-permute-done.2.below_far
  42.7 0.0 collective-permute-done.3.above_far
  42.7 5.5 %local_moments.1 = f32[4,2,8,512]{3,2,1,0:T(8,128)} custom-call(bf16[96,512]{1,0:T(8,128)(2,1)S(1)} %collective-permute-done.below, bf16[96,512]{1,0:T(8,128)(2,1)S(1)} %collective-permute-done.1.above, bf16[80,512]{1,0:T(8,128)(2,1)S(1)} %collective-permute-done.2.below_far, bf16[80,512]{1,0:T(8,128)(2,1)S(1)} %collective-permute-done.3.above_far, ...), custom_call_target="tpu_custom_call" | custom-call | flops 10000000 | bytes 8000000 | tf_op jit(solution)/shard_map/local_moments/pallas_call | solution.py:534
  48.1 4.1 %all-to-all-done.1 = f32[128,1,64]{2,1,0:T(1,128)S(1)} async-done(((f32[128,1,64]{2,1,0:T(1,128)}), f32[128,1,64]{2,1,0:T(1,128)S(1)}, u32[]{:S(2)}, u32[]{:S(2)}) %all-to-all-start.1) | async-done | bytes 32800 | tf_op jit(solution)/shard_map/all_to_all | solution.py:533
  52.2 0.7 %total.1 = f32[4,16]{1,0:T(4,128)} custom-call(f32[128,64]{1,0:T(8,128)S(1)} %bitcast.4), custom_call_target="tpu_custom_call" | custom-call | tf_op jit(solution)/shard_map/total/pallas_call | solution.py:549
Async XLA Ops:
  0.6 26.0 %copy-start.1 = (s32[2,8,512]{2,1,0:T(8,128)S(1)}, s32[2,8,512]{2,1,0:T(8,128)}, u32[]{:S(2)}) copy-start(s32[2,8,512]{2,1,0:T(8,128)} %vacancy.3) | copy-start | bytes 98308
  0.6 26.0 %copy-start = (f32[2,8,512]{2,1,0:T(8,128)S(1)}, f32[2,8,512]{2,1,0:T(8,128)}, u32[]{:S(2)}) copy-start(f32[2,8,512]{2,1,0:T(8,128)} %disorder.3) | copy-start | bytes 98308
  26.8 7.1 %collective-permute-start = (bf16[96,512]{1,0:T(8,128)(2,1)S(1)}, bf16[96,512]{1,0:T(8,128)(2,1)S(1)}, u32[]{:S(2)}, u32[]{:S(2)}) collective-permute-start(bf16[96,512]{1,0:T(8,128)(2,1)S(1)} %get-tuple-element.23), channel_id=1, source_target_pairs={{0,16},{16,32},{32,48},{48,64},{64,80},{80,96},{96,112},{112,0},{1... | collective-permute-start | bytes 294920 | tf_op jit(solution)/shard_map/ppermute | solution.py:501
  30.4 4.0 %collective-permute-start.1 = (bf16[96,512]{1,0:T(8,128)(2,1)S(1)}, bf16[96,512]{1,0:T(8,128)(2,1)S(1)}, u32[]{:S(2)}, u32[]{:S(2)}) collective-permute-start(bf16[96,512]{1,0:T(8,128)(2,1)S(1)} %get-tuple-element.24), channel_id=1, source_target_pairs={{16,0},{32,16},{48,32},{64,48},{80,64},{96,80},{112,96},{0,112},{1... | collective-permute-start | bytes 294920 | tf_op jit(solution)/shard_map/ppermute | solution.py:502
  30.4 12.3 %collective-permute-start.2 = (bf16[80,512]{1,0:T(8,128)(2,1)S(1)}, bf16[80,512]{1,0:T(8,128)(2,1)S(1)}, u32[]{:S(2)}, u32[]{:S(2)}) collective-permute-start(bf16[80,512]{1,0:T(8,128)(2,1)S(1)} %get-tuple-element.25), channel_id=1, source_target_pairs={{0,16},{16,32},{32,48},{48,64},{64,80},{80,96},{96,112},{112,0},{1... | collective-permute-start | bytes 245768 | tf_op jit(solution)/shard_map/ppermute | solution.py:503
  32.1 10.5 %collective-permute-start.3 = (bf16[80,512]{1,0:T(8,128)(2,1)S(1)}, bf16[80,512]{1,0:T(8,128)(2,1)S(1)}, u32[]{:S(2)}, u32[]{:S(2)}) collective-permute-start(bf16[80,512]{1,0:T(8,128)(2,1)S(1)} %get-tuple-element.26), channel_id=1, source_target_pairs={{16,0},{32,16},{48,32},{64,48},{80,64},{96,80},{112,96},{0,112},{1... | collective-permute-start | bytes 245768 | tf_op jit(solution)/shard_map/ppermute | solution.py:504
  36.7 15.5 %all-to-all-start.1 = ((f32[128,1,64]{2,1,0:T(1,128)}), f32[128,1,64]{2,1,0:T(1,128)S(1)}, u32[]{:S(2)}, u32[]{:S(2)}) async-start(f32[128,1,64]{2,1,0:T(1,128)} %bitcast.1), calls=%async_computation.1 | async-start | bytes 131072 | tf_op jit(solution)/shard_map/all_to_all | solution.py:533

commit v6 on v5

--- a/solution.py
+++ b/solution.py
@@ -37,12 +37,15 @@
 BF16 = jnp.bfloat16
 
 
+def bfloat16_terms(value):
+    high = value.astype(BF16).astype(F32)
+    rest = value - high
+    middle = rest.astype(BF16).astype(F32)
+    return high, middle, rest - middle
+
+
 def site_planes(onsite, keep):
-    high = onsite.astype(BF16).astype(F32)
-    rest = onsite - high
-    middle = rest.astype(BF16).astype(F32)
-    low = (rest - middle).astype(BF16).astype(F32)
-    return high, middle, low, keep
+    return (*bfloat16_terms(onsite), keep)
 
 
 def lane_index(rows, lanes):
@@ -51,7 +54,7 @@
 
 def pack_kernel(
     columns, plan_hbm, stored_hbm, disorder_hbm, vacancy_hbm, out, table,
-    plan, stored, disorder, vacancy, turned, where_to, arrived,
+    plan, stored, disorder, vacancy, turned, arrived,
 ):
     copies = [
         pltpu.make_async_copy(source, target, arrived.at[i])
@@ -63,28 +66,27 @@
         copy.start()
     me = lax.axis_index("gy")
     first = me * BLOCKS
+    total = BLOCKS * columns
     copies[0].wait()
-
-    def find(k, carry):
-        held = plan[k] - first
-        spot = jnp.where((held >= 0) & (held < BLOCKS), held, BLOCKS)
-        where_to[spot] = k
-        return carry
-
-    lax.fori_loop(0, BLOCKS * columns, find, 0, unroll=8)
-
-    total = BLOCKS * columns
-    sources = [first + b for b in range(BLOCKS)]
-    sources += [(first + total - 1) % total, (first + BLOCKS) % total]
-    for i, k in enumerate(sources):
-        table[i : i + 1, :] = jnp.full((1, BLOCK), plan[k] // BLOCKS, jnp.int32)
+    place = lane_index(1, total)
+    listed = plan[...]
+    spots = [
+        jnp.sum(jnp.where(listed == first + b, place, 0), axis=1, keepdims=True)[0, 0]
+        for b in range(BLOCKS)
+    ]
+    source = listed // BLOCKS
+    wanted = [first + b for b in range(BLOCKS)]
+    wanted += [(first + total - 1) % total, (first + BLOCKS) % total]
+    for i, k in enumerate(wanted):
+        row = jnp.sum(jnp.where(place == k, source, 0), axis=1, keepdims=True)
+        table[i : i + 1, :] = jnp.broadcast_to(row, (1, BLOCK))
     copies[1].wait()
     for b in range(BLOCKS):
         block = stored[:, :, :, b * BLOCK : (b + 1) * BLOCK]
         turned[b] = block.reshape(2 * R * WIDTH_X, BLOCK).astype(F32)
     lane = lane_index(8, BLOCK)
     edges = [[jnp.zeros((8, BLOCK), F32) for _ in range(2)] for _ in range(BLOCKS)]
-    slots = [where_to[b] // BLOCKS for b in range(BLOCKS)]
+    slots = [spot // BLOCKS for spot in spots]
     for s in range(2):
         for x in range(WIDTH_X):
             q = s * WIDTH_X + x
@@ -100,7 +102,7 @@
                 out[slots[b], q * R : (q + 1) * R, :] = both
     last_half = lane_index(R, BLOCK) % 8 < 4
     for b in range(BLOCKS):
-        spot = where_to[b]
+        spot = spots[b]
         edge = jnp.concatenate(edges[b], axis=0)
 
         @pl.when(spot % BLOCKS == BLOCKS - 1)
@@ -309,19 +311,45 @@
         self.first = first
 
     def __getitem__(self, index):
-        s, row, part, lanes = index
-        return self.ref[s, row - self.first, part, lanes]
+        s, row, *rest = index
+        return self.ref[(s, row - self.first, *rest)]
 
     def __setitem__(self, index, value):
-        s, row, part, lanes = index
-        self.ref[s, row - self.first, part, lanes] = value
+        s, row, *rest = index
+        self.ref[(s, row - self.first, *rest)] = value
+
+
+class Joined:
+    def __init__(self, *pieces):
+        self.at = {row: (ref, i) for ref, rows in pieces for i, row in enumerate(rows)}
+
+    def __getitem__(self, index):
+        s, row, *rest = index
+        ref, i = self.at[row]
+        return ref[(s, i, *rest)]
+
+    def __setitem__(self, index, value):
+        s, row, *rest = index
+        ref, i = self.at[row]
+        ref[(s, i, *rest)] = value
+
+
+OWN_ROWS = range(HALO, HALO + WIDTH_X)
+NEAR_ROWS = (2, 3, 12, 13)
+FIRST_ROWS = range(5, 11)
+FIRST_BORDER = (3, 4, 11, 12)
+SECOND_ROWS = range(6, 10)
+SECOND_BORDER = (4, 5, 10, 11)
 
 
 def interior_kernel(
     columns, table, received, disorder, vacancy,
     level, factor, start, real1, imag1, real2, imag2, sums, own_sites, own_start,
 ):
-    real2, imag2 = Rows(real2, HALO), Rows(imag2, HALO)
+    own_level, own_factor = level, factor
+    level, factor, start = (Rows(ref, HALO) for ref in (level, factor, start))
+    real1, imag1 = (Rows(ref, FIRST_ROWS[0]) for ref in (real1, imag1))
+    real2, imag2 = (Rows(ref, SECOND_ROWS[0]) for ref in (real2, imag2))
     tile, sites = edge_tiles(columns, table, received)
     slots = [source_of(table, b) for b in range(BLOCKS)]
     for s in range(2):
@@ -337,8 +365,8 @@
             value = value * jnp.concatenate([kept[x], kept[x]], axis=0)
             start[s, HALO + x] = value
             own_start[s, x] = value.astype(BF16)
-            own_sites[0, s, x : x + 1, :] = level[s, HALO + x, 0:1, :]
-            own_sites[1, s, x : x + 1, :] = factor[s, HALO + x, 0:1, :]
+            own_sites[0, s, x : x + 1, :] = own_level[s, x, 0:1, :]
+            own_sites[1, s, x : x + 1, :] = own_factor[s, x, 0:1, :]
 
     def one(i, carry):
         row = HALO + 1 + 2 * i
@@ -361,10 +389,18 @@
 
 
 def border_kernel(
-    below, above, level_in, factor_in, start_in, real1_in, imag1_in, real2_in, imag2_in, sums_in,
-    level, factor, start, real1, imag1, real2, imag2, trace_out,
+    below, above,
+    own_level, own_factor, own_start, own_real1, own_imag1, own_real2, own_imag2, sums_in,
+    border_real2, border_imag2, trace_out,
+    near_level, near_factor, near_start, border_real1, border_imag1,
 ):
-    real2, imag2 = Rows(real2, HALO), Rows(imag2, HALO)
+    level = Joined((own_level, OWN_ROWS), (near_level, NEAR_ROWS))
+    factor = Joined((own_factor, OWN_ROWS), (near_factor, NEAR_ROWS))
+    start = Joined((own_start, OWN_ROWS), (near_start, NEAR_ROWS))
+    real1 = Joined((own_real1, FIRST_ROWS), (border_real1, FIRST_BORDER))
+    imag1 = Joined((own_imag1, FIRST_ROWS), (border_imag1, FIRST_BORDER))
+    real2 = Joined((own_real2, SECOND_ROWS), (border_real2, SECOND_BORDER))
+    imag2 = Joined((own_imag2, SECOND_ROWS), (border_imag2, SECOND_BORDER))
     unpack_rows(below, below, level, factor, start, HALO - NEAR, WIDTH_X - NEAR)
     unpack_rows(above, above, level, factor, start, HALO + WIDTH_X, 0)
     for row in (HALO - 1, HALO + WIDTH_X - 1):
@@ -380,15 +416,19 @@
     moments = jnp.concatenate(
         [one_one, one_two, 2.0 * both - one_one, 2.0 * second - norm], axis=0
     )
-    trace_out[...] = lax.dot_general(
-        jnp.ones(trace_out.shape[:1] + (BLOCK,), F32), moments,
-        (((1,), (1,)), ((), ())),
-        precision=lax.Precision.HIGHEST, preferred_element_type=F32,
-    )
+    ones = jnp.ones((8, BLOCK), BF16)
+    total = jnp.zeros((8, TERMS * R), F32)
+    for term in bfloat16_terms(moments):
+        total = total + lax.dot_general(
+            ones, term.astype(BF16), (((1,), (1,)), ((), ())), preferred_element_type=F32
+        )
+    for i in range(trace_out.shape[0] // 8):
+        trace_out[i * 8 : (i + 1) * 8, :] = total
 
 
 def local_kernel(
-    below, above, below_far, above_far, own_sites, own_start, real2_in, imag2_in,
+    below, above, below_far, above_far, own_sites, own_start,
+    own_real2, own_imag2, border_real2, border_imag2,
     local_out, level, factor, start, real1, imag1, real2, imag2, real3, imag3, real4, products,
 ):
     real4 = Rows(real4, HALO)
@@ -398,8 +438,11 @@
             level[s, row] = jnp.broadcast_to(own_sites[0, s, x : x + 1, :], (8, LANES))
             factor[s, row] = jnp.broadcast_to(own_sites[1, s, x : x + 1, :], (8, LANES))
             start[s, row] = own_start[s, x].astype(F32)
-            real2[s, row] = real2_in[s, x]
-            imag2[s, row] = imag2_in[s, x]
+    for ref, own, border in ((real2, own_real2, border_real2), (imag2, own_imag2, border_imag2)):
+        for s in range(2):
+            for source, rows in ((own, SECOND_ROWS), (border, SECOND_BORDER)):
+                for i, row in enumerate(rows):
+                    ref[s, row] = source[s, i]
     unpack_rows(below_far, below, level, factor, start, 0, WIDTH_X - HALO)
     unpack_rows(below, below, level, factor, start, NEAR, WIDTH_X - NEAR)
     unpack_rows(above, above, level, factor, start, HALO + WIDTH_X, 0)
@@ -469,19 +512,18 @@
         in_specs=[hbm] * 4,
         out_specs=(vmem, vmem),
         scratch_shapes=[
-            pltpu.SMEM(plan.shape, plan.dtype),
+            pltpu.VMEM((1,) + plan.shape, plan.dtype),
             pltpu.VMEM(stored_vectors.shape, stored_vectors.dtype),
             pltpu.VMEM(disorder.shape, disorder.dtype),
             pltpu.VMEM(vacancy.shape, vacancy.dtype),
             pltpu.VMEM((BLOCKS, 2 * R * WIDTH_X, BLOCK), F32),
-            pltpu.SMEM((BLOCKS + 1,), jnp.int32),
             pltpu.SemaphoreType.DMA((4,)),
         ],
         compiler_params=pltpu.CompilerParams(vmem_limit_bytes=16 * 1024 * 1024),
         name="pack",
     )(*(
         pltpu.with_memory_space_constraint(x, pltpu.HBM)
-        for x in (plan, stored_vectors, disorder, vacancy)
+        for x in (plan[None], stored_vectors, disorder, vacancy)
     ))
     received = lax.all_to_all(outgoing, "gy", split_axis=0, concat_axis=0, tiled=True)
 
@@ -503,13 +545,21 @@
     below_far = lax.ppermute(high_far, "gx", up)
     above_far = lax.ppermute(low_far, "gx", down)
 
-    site = jax.ShapeDtypeStruct((2, ROWS_X, 8, LANES), F32)
-    field = jax.ShapeDtypeStruct((2, ROWS_X, R, LANES), F32)
-    narrow = jax.ShapeDtypeStruct((2, WIDTH_X, R, LANES), F32)
-    state = (site, site) + (field,) * 3 + (narrow,) * 2
+    def site(count):
+        return jax.ShapeDtypeStruct((2, count, 8, LANES), F32)
+
+    def field(count):
+        return jax.ShapeDtypeStruct((2, count, R, LANES), F32)
+
+    def scratch(shape):
+        return pltpu.VMEM(shape.shape, shape.dtype)
+
     *inner, own_sites, own_start = pl.pallas_call(
         functools.partial(interior_kernel, columns),
-        out_shape=state + (
+        out_shape=(site(WIDTH_X), site(WIDTH_X), field(WIDTH_X))
+        + (field(len(FIRST_ROWS)),) * 2
+        + (field(len(SECOND_ROWS)),) * 2
+        + (
             jax.ShapeDtypeStruct((2 * SUMS * 8, BLOCK), F32),
             jax.ShapeDtypeStruct((2, 2, WIDTH_X, LANES), F32),
             jax.ShapeDtypeStruct((2, WIDTH_X, R, LANES), BF16),
@@ -520,32 +570,38 @@
         cost_estimate=pl.CostEstimate(flops=10**7, bytes_accessed=8 * 10**6, transcendentals=0),
         name="interior",
     )(table, received, disorder, vacancy)
-    outputs = pl.pallas_call(
+    own_real2, own_imag2 = inner[5:7]
+    border_real2, border_imag2, partial = pl.pallas_call(
         border_kernel,
-        out_shape=state + (jax.ShapeDtypeStruct((devices, TERMS * R), F32),),
+        out_shape=(field(len(SECOND_BORDER)),) * 2
+        + (jax.ShapeDtypeStruct((devices, TERMS * R), F32),),
         in_specs=[vmem] * 10,
-        out_specs=(vmem,) * 8,
-        input_output_aliases={2 + i: i for i in range(7)},
+        out_specs=(vmem,) * 3,
+        scratch_shapes=[scratch(site(len(NEAR_ROWS)))] * 2
+        + [scratch(field(len(NEAR_ROWS)))]
+        + [scratch(field(len(FIRST_BORDER)))] * 2,
         compiler_params=params,
         name="border",
     )(below, above, *inner)
-    real2, imag2, partial = outputs[5:]
     shared = lax.all_to_all(partial, ("gx", "gy"), split_axis=0, concat_axis=0, tiled=True)
     local_moments = pl.pallas_call(
         local_kernel,
         out_shape=jax.ShapeDtypeStruct((TERMS, 2, WIDTH_X, OWN), F32),
-        in_specs=[vmem] * 8,
+        in_specs=[vmem] * 10,
         out_specs=vmem,
-        scratch_shapes=[pltpu.VMEM(site.shape, F32)] * 2
-        + [pltpu.VMEM(field.shape, F32)] * 7
+        scratch_shapes=[scratch(site(ROWS_X))] * 2
+        + [scratch(field(ROWS_X))] * 7
         + [
-            pltpu.VMEM(narrow.shape, F32),
+            scratch(field(WIDTH_X)),
             pltpu.VMEM((TERMS, 2, BLOCKS, 8 * WIDTH_X, BLOCK), F32),
         ],
         compiler_params=pltpu.CompilerParams(vmem_limit_bytes=16 * 1024 * 1024),
         cost_estimate=pl.CostEstimate(flops=10**7, bytes_accessed=8 * 10**6, transcendentals=0),
         name="local_moments",
-    )(below, above, below_far, above_far, own_sites, own_start, real2, imag2)
+    )(
+        below, above, below_far, above_far, own_sites, own_start,
+        own_real2, own_imag2, border_real2, border_imag2,
+    )
     trace = pl.pallas_call(
         functools.partial(total_kernel, 2 * WIDTH_X * rows * OWN * columns),
         out_shape=jax.ShapeDtypeStruct((TERMS, R), F32),

time: 53.1 us -> 52.8 us (level)
  transfers between devices with their start and end apart: 5 -> 5, of which waited for: 2 -> 2; matrix products, arithmetic and copies ran while one was open for 0% -> 0% of each run, Pallas kernels for 18% -> 17%
where the time goes in v6:
time: 52.8 us; the launch traced here: 52.6 us
  blocking collectives  24.5 us (46%)
  Pallas kernels  11.4 us (22%)
  starting transfers between devices  11.3 us (21%)
  waiting for transfers between devices  4.69 us (9%)
  between operations  0.7 us (1%)
    all_to_all x1, blocking collectives, local(): lax.all_to_all(outgoing, 'gy', split_axis=0, concat_axis=0, tiled=True)  24.5 us
    all_to_all x1, starting transfers between devices, local(): lax.all_to_all(partial, ('gx', 'gy'), split_axis=0, concat_axis=0, tiled=...  5.93 us
    pallas_call x1, Pallas kernels, local(): pl.pallas_call(local_kernel, out_shape=jax.ShapeDtypeStruct((TERMS, 2, WI...  5.47 us
    all_to_all x1, waiting for transfers between devices, local(): lax.all_to_all(partial, ('gx', 'gy'), split_axis=0, concat_axis=0, tiled=...  4.09 us
    ppermute x1, starting transfers between devices, local(): below = lax.ppermute(high_near, 'gx', up)  3.6 us
    pallas_call x1, Pallas kernels, local(): pl.pallas_call(border_kernel, out_shape=(field(len(SECOND_BORDER)),) * 2...  2.05 us
    ppermute x1, starting transfers between devices, local(): below_far = lax.ppermute(high_far, 'gx', up)  1.74 us
    pallas_call x1, Pallas kernels, local(): pl.pallas_call(functools.partial(interior_kernel, columns), out_shape=(si...  1.68 us
  transfers between devices with their start and end apart: 5, of which 2 were waited for; matrix products, arithmetic and copies ran while one was open for 0% of the time, Pallas kernels for 17%

profile of v6, /device:TPU:1, one launch (start us, length us, event | category | flops | bytes accessed | tf_op | source)
XLA Modules:
  0.0 52.6 jit_solution(3802612369057788774)
XLA Ops:
  0.6 1.5 %pack.1 = (bf16[16,280,128]{2,1,0:T(8,128)(2,1)S(1)}, s32[8,128]{1,0:T(8,128)S(1)}) custom-call(s32[1,64]{1,0:T(1,128)} %bitcast.6, bf16[2,16,8,512]{3,2,1,0:T(8,128)(2,1)} %stored_hbm.1, f32[2,8,512]{2,1,0:T(8,128)} %disorder.3, s32[2,8,512]{2,1,0:T(8,128)} %vacancy.3), custom_call_target="tpu_custom_call" | custom-call | tf_op jit(solution)/shard_map/pack/pallas_call | solution.py:506
  2.1 0.0 copy-start
  2.1 0.0 copy-start.1
  2.1 24.5 %all_to_all.16.received = bf16[16,280,128]{2,1,0:T(8,128)(2,1)S(1)} all-to-all(bf16[16,280,128]{2,1,0:T(8,128)(2,1)S(1)} %get-tuple-element.22), channel_id=1, replica_groups=mesh['gx'=8,'gy'=16] {'gy'}, dimensions={0} | all-to-all | bytes 2293760 | tf_op jit(solution)/shard_map/all_to_all | solution.py:528
  26.6 0.0 copy-done
  26.6 0.0 copy-done.1
  26.6 0.1 arrange.1
  26.7 3.6 %collective-permute-start = (bf16[96,512]{1,0:T(8,128)(2,1)S(1)}, bf16[96,512]{1,0:T(8,128)(2,1)S(1)}, u32[]{:S(2)}, u32[]{:S(2)}) collective-permute-start(bf16[96,512]{1,0:T(8,128)(2,1)S(1)} %get-tuple-element.23), channel_id=1, source_target_pairs={{0,16},{16,32},{32,48},{48,64},{64,80},{80,96},{96,112},{112,0},{1... | collective-permute-start | bytes 294920 | tf_op jit(solution)/shard_map/ppermute | solution.py:543
  30.3 0.0 collective-permute-start.1
  30.3 1.7 %collective-permute-start.2 = (bf16[80,512]{1,0:T(8,128)(2,1)S(1)}, bf16[80,512]{1,0:T(8,128)(2,1)S(1)}, u32[]{:S(2)}, u32[]{:S(2)}) collective-permute-start(bf16[80,512]{1,0:T(8,128)(2,1)S(1)} %get-tuple-element.25), channel_id=1, source_target_pairs={{0,16},{16,32},{32,48},{48,64},{64,80},{80,96},{96,112},{112,0},{1... | collective-permute-start | bytes 245768 | tf_op jit(solution)/shard_map/ppermute | solution.py:545
  32.1 0.0 collective-permute-start.3
  32.1 1.7 %interior.1 = (f32[2,8,8,640]{3,2,1,0:T(8,128)S(1)}, f32[2,8,8,640]{3,2,1,0:T(8,128)S(1)}, f32[2,8,16,640]{3,2,1,0:T(8,128)S(1)}, f32[2,6,16,640]{3,2,1,0:T(8,12...) custom-call(s32[8,128]{1,0:T(8,128)S(1)} %get-tuple-element.21.table, ...), custom_call_target="tpu_custom_call" | custom-call | flops 10000000 | bytes 8000000 | tf_op jit(solution)/shard_map/interior/pallas_call | solution.py:557
  33.8 0.0 collective-permute-done.below
  33.8 0.6 %collective-permute-done.1.above = bf16[96,512]{1,0:T(8,128)(2,1)S(1)} collective-permute-done((bf16[96,512]{1,0:T(8,128)(2,1)S(1)}, bf16[96,512]{1,0:T(8,128)(2,1)S(1)}, u32[]{:S(2)}, u32[]{:S(2)}) %collective-permute-start.1) | collective-permute-done | bytes 98336 | tf_op jit(solution)/shard_map/ppermute | solution.py:544
  34.4 2.0 %border.1 = (f32[2,4,16,640]{3,2,1,0:T(8,128)S(1)}, f32[2,4,16,640]{3,2,1,0:T(8,128)S(1)}, f32[128,64]{1,0:T(8,128)}) custom-call(bf16[96,512]{1,0:T(8,128)(2,1)S(1)} %collective-permute-done.below, bf16[96,512]{1,0:T(8,128)(2,1)S(1)} %collective-permute-done.1.above, f32[2,8,8,640]{3,2,1,0:T(8,128)S(1)} %get-tuple-element.31.own_level, ...), custom_call_target="tpu_custom_call" | custom-call | tf_op jit(solution)/shard_map/border/pallas_call | solution.py:574
  36.4 5.9 %all-to-all-start.1 = ((f32[128,1,64]{2,1,0:T(1,128)}), f32[128,1,64]{2,1,0:T(1,128)S(1)}, u32[]{:S(2)}, u32[]{:S(2)}) async-start(f32[128,1,64]{2,1,0:T(1,128)} %bitcast.2), calls=%async_computation.1 | async-start | bytes 131072 | tf_op jit(solution)/shard_map/all_to_all | solution.py:586
  42.3 0.0 collective-permute-done.2.below_far
  42.4 0.0 collective-permute-done.3.above_far
  42.4 5.5 %local_moments.1 = f32[4,2,8,512]{3,2,1,0:T(8,128)} custom-call(bf16[96,512]{1,0:T(8,128)(2,1)S(1)} %collective-permute-done.below, bf16[96,512]{1,0:T(8,128)(2,1)S(1)} %collective-permute-done.1.above, bf16[80,512]{1,0:T(8,128)(2,1)S(1)} %collective-permute-done.2.below_far, bf16[80,512]{1,0:T(8,128)(2,1)S(1)} %collective-permute-done.3.above_far, ...), custom_call_target="tpu_custom_call" | custom-call | flops 10000000 | bytes 8000000 | tf_op jit(solution)/shard_map/local_moments/pallas_call | solution.py:587
  47.8 4.1 %all-to-all-done.1 = f32[128,1,64]{2,1,0:T(1,128)S(1)} async-done(((f32[128,1,64]{2,1,0:T(1,128)}), f32[128,1,64]{2,1,0:T(1,128)S(1)}, u32[]{:S(2)}, u32[]{:S(2)}) %all-to-all-start.1) | async-done | bytes 32800 | tf_op jit(solution)/shard_map/all_to_all | solution.py:586
  51.9 0.7 %total.1 = f32[4,16]{1,0:T(4,128)} custom-call(f32[128,64]{1,0:T(8,128)S(1)} %bitcast.5), custom_call_target="tpu_custom_call" | custom-call | tf_op jit(solution)/shard_map/total/pallas_call | solution.py:605
Async XLA Ops:
  2.1 24.5 %copy-start = (f32[2,8,512]{2,1,0:T(8,128)S(1)}, f32[2,8,512]{2,1,0:T(8,128)}, u32[]{:S(2)}) copy-start(f32[2,8,512]{2,1,0:T(8,128)} %disorder.3) | copy-start | bytes 98308
  2.1 24.5 %copy-start.1 = (s32[2,8,512]{2,1,0:T(8,128)S(1)}, s32[2,8,512]{2,1,0:T(8,128)}, u32[]{:S(2)}) copy-start(s32[2,8,512]{2,1,0:T(8,128)} %vacancy.3) | copy-start | bytes 98308
  26.7 7.0 %collective-permute-start = (bf16[96,512]{1,0:T(8,128)(2,1)S(1)}, bf16[96,512]{1,0:T(8,128)(2,1)S(1)}, u32[]{:S(2)}, u32[]{:S(2)}) collective-permute-start(bf16[96,512]{1,0:T(8,128)(2,1)S(1)} %get-tuple-element.23), channel_id=1, source_target_pairs={{0,16},{16,32},{32,48},{48,64},{64,80},{80,96},{96,112},{112,0},{1... | collective-permute-start | bytes 294920 | tf_op jit(solution)/shard_map/ppermute | solution.py:543
  30.3 4.0 %collective-permute-start.1 = (bf16[96,512]{1,0:T(8,128)(2,1)S(1)}, bf16[96,512]{1,0:T(8,128)(2,1)S(1)}, u32[]{:S(2)}, u32[]{:S(2)}) collective-permute-start(bf16[96,512]{1,0:T(8,128)(2,1)S(1)} %get-tuple-element.24), channel_id=1, source_target_pairs={{16,0},{32,16},{48,32},{64,48},{80,64},{96,80},{112,96},{0,112},{1... | collective-permute-start | bytes 294920 | tf_op jit(solution)/shard_map/ppermute | solution.py:544
  30.3 12.0 %collective-permute-start.2 = (bf16[80,512]{1,0:T(8,128)(2,1)S(1)}, bf16[80,512]{1,0:T(8,128)(2,1)S(1)}, u32[]{:S(2)}, u32[]{:S(2)}) collective-permute-start(bf16[80,512]{1,0:T(8,128)(2,1)S(1)} %get-tuple-element.25), channel_id=1, source_target_pairs={{0,16},{16,32},{32,48},{48,64},{64,80},{80,96},{96,112},{112,0},{1... | collective-permute-start | bytes 245768 | tf_op jit(solution)/shard_map/ppermute | solution.py:545
  32.1 10.3 %collective-permute-start.3 = (bf16[80,512]{1,0:T(8,128)(2,1)S(1)}, bf16[80,512]{1,0:T(8,128)(2,1)S(1)}, u32[]{:S(2)}, u32[]{:S(2)}) collective-permute-start(bf16[80,512]{1,0:T(8,128)(2,1)S(1)} %get-tuple-element.26), channel_id=1, source_target_pairs={{16,0},{32,16},{48,32},{64,48},{80,64},{96,80},{112,96},{0,112},{1... | collective-permute-start | bytes 245768 | tf_op jit(solution)/shard_map/ppermute | solution.py:546
  36.4 15.5 %all-to-all-start.1 = ((f32[128,1,64]{2,1,0:T(1,128)}), f32[128,1,64]{2,1,0:T(1,128)S(1)}, u32[]{:S(2)}, u32[]{:S(2)}) async-start(f32[128,1,64]{2,1,0:T(1,128)} %bitcast.2), calls=%async_computation.1 | async-start | bytes 131072 | tf_op jit(solution)/shard_map/all_to_all | solution.py:586

commit v7 on v6

--- a/solution.py
+++ b/solution.py
@@ -24,7 +24,7 @@
 PART = 2 * NEAR * R
 PLANES = PART
 SIDES = PLANES + 4 * 2 * NEAR
-NEAR_MESSAGE = SIDES + R
+NEAR_MESSAGE = SIDES + 8
 FAR_MESSAGE = SIDES
 
 HOP_NEXT = 0.3
@@ -171,10 +171,8 @@
                 out[s * size : (s + 1) * size, lanes] = received[slot, base : base + size, :]
     tile, sites = edge_tiles(columns, table, received)
     for out in (low_near, high_near):
-        out[SIDES : SIDES + R, 0:BLOCK] = tile.astype(BF16)
-        out[SIDES : SIDES + 8, BLOCK : 2 * BLOCK] = sites.astype(BF16)
-        out[SIDES + 8 : SIDES + R, BLOCK : 2 * BLOCK] = jnp.zeros((8, BLOCK), BF16)
-        out[SIDES : SIDES + R, 2 * BLOCK : OWN] = jnp.zeros((R, OWN - 2 * BLOCK), BF16)
+        for i, part in enumerate((tile[0:8], tile[8:16], sites, sites)):
+            out[SIDES : SIDES + 8, i * BLOCK : (i + 1) * BLOCK] = part.astype(BF16)
     for s in range(2):
         for p, plane in enumerate(site_planes(disorder[s], vacancy[s].astype(F32))):
             row = p * 2 * NEAR + s * NEAR
@@ -207,8 +205,9 @@
 
 def unpack_rows(message, near, level, factor, start, base, x):
     planes = message[PLANES:SIDES, :].astype(F32)
-    tile = near[SIDES : SIDES + R, 0:BLOCK].astype(F32)
-    sites = near[SIDES : SIDES + 8, BLOCK : 2 * BLOCK].astype(F32)
+    sides = near[SIDES : SIDES + 8, :].astype(F32)
+    tile = jnp.concatenate([sides[:, 0:BLOCK], sides[:, BLOCK : 2 * BLOCK]], axis=0)
+    sites = sides[:, 2 * BLOCK : 3 * BLOCK]
     step = 2 * NEAR
     onsite = planes[0:step] + planes[step : 2 * step] + planes[2 * step : 3 * step]
     keep = planes[3 * step : 4 * step]
@@ -227,7 +226,8 @@
                 start[s, base + i, part, :] = value[part] * kept[i]
 
 
-def span(level, factor, term, old, now, new, row, count=2):
+def span(level, factor, term, old, now, new, row, count=2, width=LANES):
+    own = slice(0, width)
     for h in range(2):
         part = slice(h * 8, (h + 1) * 8)
         near_rows = range(-1, count + 1)
@@ -259,23 +259,24 @@
                     continue
                 joint = {d: ahead[c][d - 1] + back[c][d] for d in range(count + 1)}
                 for d in range(count):
-                    out = ahead[c][d + 1] + back[c][d - 1]
+                    out = ahead[c][d + 1][:, own] + back[c][d - 1][:, own]
                     up, down = joint[d], joint[d + 1]
                     if c < len(fields):
                         other = others[c][1 - s]
                         aside = d - 1 if s == 0 else d + 1
-                        out = out + level[s, row + d] * fields[c][s][d]
-                        out = out - (other[d] + other[aside])
+                        out = out + level[s, row + d][:, own] * fields[c][s][d][:, own]
+                        out = out - (other[d] + other[aside])[:, own]
                         if s == 0:
                             down = down - other[d]
                         else:
                             up = up - other[d]
-                    out = out + pltpu.roll(up, LANES - 1, 1) + pltpu.roll(down, 1, 1)
-                    scale = factor[s, row + d]
+                    out = out + pltpu.roll(up, LANES - 1, 1)[:, own]
+                    out = out + pltpu.roll(down, 1, 1)[:, own]
+                    scale = factor[s, row + d][:, own]
                     out = out * (scale * 0.5 if term == 1 else scale)
                     if term > 1 and old[c] is not None:
-                        out = out - old[c][s, row + d, part, :]
-                    new[c][s, row + d, part, :] = out
+                        out = out - old[c][s, row + d, part, own]
+                    new[c][s, row + d, part, own] = out
 
 
 def fold(product):
@@ -377,7 +378,7 @@
 
     def two(i, carry):
         row = HALO + 2 + 2 * i
-        span(level, factor, 2, (start, None), (real1, imag1), (real2, imag2), row)
+        span(level, factor, 2, (start, None), (real1, imag1), (real2, imag2), row, width=OWN)
         for d in range(2):
             carry = trace_row(start, (real1, imag1), (real2, imag2), row + d, carry)
         return carry
@@ -391,8 +392,8 @@
 def border_kernel(
     below, above,
     own_level, own_factor, own_start, own_real1, own_imag1, own_real2, own_imag2, sums_in,
-    border_real2, border_imag2, trace_out,
-    near_level, near_factor, near_start, border_real1, border_imag1,
+    trace_out,
+    near_level, near_factor, near_start, border_real1, border_imag1, border_real2, border_imag2,
 ):
     level = Joined((own_level, OWN_ROWS), (near_level, NEAR_ROWS))
     factor = Joined((own_factor, OWN_ROWS), (near_factor, NEAR_ROWS))
@@ -407,7 +408,7 @@
         span(level, factor, 1, None, (start, None), (real1, imag1), row)
     totals = tuple(sums_in[i * 8 : (i + 1) * 8, :] for i in range(2 * SUMS))
     for row in (HALO, HALO + WIDTH_X - 2):
-        span(level, factor, 2, (start, None), (real1, imag1), (real2, imag2), row)
+        span(level, factor, 2, (start, None), (real1, imag1), (real2, imag2), row, width=OWN)
         for d in range(2):
             totals = trace_row(start, (real1, imag1), (real2, imag2), row + d, totals)
     norm, one_one, one_two, both, second = (
@@ -428,7 +429,6 @@
 
 def local_kernel(
     below, above, below_far, above_far, own_sites, own_start,
-    own_real2, own_imag2, border_real2, border_imag2,
     local_out, level, factor, start, real1, imag1, real2, imag2, real3, imag3, real4, products,
 ):
     real4 = Rows(real4, HALO)
@@ -438,11 +438,6 @@
             level[s, row] = jnp.broadcast_to(own_sites[0, s, x : x + 1, :], (8, LANES))
             factor[s, row] = jnp.broadcast_to(own_sites[1, s, x : x + 1, :], (8, LANES))
             start[s, row] = own_start[s, x].astype(F32)
-    for ref, own, border in ((real2, own_real2, border_real2), (imag2, own_imag2, border_imag2)):
-        for s in range(2):
-            for source, rows in ((own, SECOND_ROWS), (border, SECOND_BORDER)):
-                for i, row in enumerate(rows):
-                    ref[s, row] = source[s, i]
     unpack_rows(below_far, below, level, factor, start, 0, WIDTH_X - HALO)
     unpack_rows(below, below, level, factor, start, NEAR, WIDTH_X - NEAR)
     unpack_rows(above, above, level, factor, start, HALO + WIDTH_X, 0)
@@ -453,8 +448,12 @@
         return carry
 
     lax.fori_loop(0, 7, one, 0)
-    for row in (2, ROWS_X - 4):
-        span(level, factor, 2, (start, None), (real1, imag1), (real2, imag2), row)
+
+    def two(i, carry):
+        span(level, factor, 2, (start, None), (real1, imag1), (real2, imag2), 2 * i + 2)
+        return carry
+
+    lax.fori_loop(0, 6, two, 0)
 
     def three(i, carry):
         span(level, factor, 3, (real1, imag1), (real2, imag2), (real3, imag3), 2 * i + 3)
@@ -464,7 +463,7 @@
 
     def four(i, carry):
         row = 2 * i + HALO
-        span(level, factor, 4, (real2, imag2), (real3, imag3), (real4, None), row)
+        span(level, factor, 4, (real2, imag2), (real3, imag3), (real4, None), row, width=OWN)
         for d in range(2):
             for s in range(2):
                 for n, ref in enumerate((real1, real2, real3, real4)):
@@ -570,16 +569,15 @@
         cost_estimate=pl.CostEstimate(flops=10**7, bytes_accessed=8 * 10**6, transcendentals=0),
         name="interior",
     )(table, received, disorder, vacancy)
-    own_real2, own_imag2 = inner[5:7]
-    border_real2, border_imag2, partial = pl.pallas_call(
+    partial = pl.pallas_call(
         border_kernel,
-        out_shape=(field(len(SECOND_BORDER)),) * 2
-        + (jax.ShapeDtypeStruct((devices, TERMS * R), F32),),
+        out_shape=jax.ShapeDtypeStruct((devices, TERMS * R), F32),
         in_specs=[vmem] * 10,
-        out_specs=(vmem,) * 3,
+        out_specs=vmem,
         scratch_shapes=[scratch(site(len(NEAR_ROWS)))] * 2
         + [scratch(field(len(NEAR_ROWS)))]
-        + [scratch(field(len(FIRST_BORDER)))] * 2,
+        + [scratch(field(len(FIRST_BORDER)))] * 2
+        + [scratch(field(len(SECOND_BORDER)))] * 2,
         compiler_params=params,
         name="border",
     )(below, above, *inner)
@@ -587,7 +585,7 @@
     local_moments = pl.pallas_call(
         local_kernel,
         out_shape=jax.ShapeDtypeStruct((TERMS, 2, WIDTH_X, OWN), F32),
-        in_specs=[vmem] * 10,
+        in_specs=[vmem] * 6,
         out_specs=vmem,
         scratch_shapes=[scratch(site(ROWS_X))] * 2
         + [scratch(field(ROWS_X))] * 7
@@ -598,10 +596,7 @@
         compiler_params=pltpu.CompilerParams(vmem_limit_bytes=16 * 1024 * 1024),
         cost_estimate=pl.CostEstimate(flops=10**7, bytes_accessed=8 * 10**6, transcendentals=0),
         name="local_moments",
-    )(
-        below, above, below_far, above_far, own_sites, own_start,
-        own_real2, own_imag2, border_real2, border_imag2,
-    )
+    )(below, above, below_far, above_far, own_sites, own_start)
     trace = pl.pallas_call(
         functools.partial(total_kernel, 2 * WIDTH_X * rows * OWN * columns),
         out_shape=jax.ShapeDtypeStruct((TERMS, R), F32),

time: 52.8 us -> 52.7 us (level)
  waiting for transfers between devices: 4.69 us -> 3.47 us
  Pallas kernels: 11.4 us -> 12.5 us
    all_to_all x1, waiting for transfers between devices: 4.09 us -> 2.9 us  [local(): lax.all_to_all(partial, ('gx', 'gy'), split_axis=0, concat_axis=0, tiled=...]
    pallas_call x1, Pallas kernels: 5.47 us -> 6.65 us  [local(): pl.pallas_call(local_kernel, out_shape=jax.ShapeDtypeStruct((TERMS, 2, WI...]
  transfers between devices with their start and end apart: 5 -> 5, of which waited for: 2 -> 2; matrix products, arithmetic and copies ran while one was open for 0% -> 0% of each run, Pallas kernels for 17% -> 20%
where the time goes in v7:
time: 52.7 us; the launch traced here: 52.5 us
  blocking collectives  24.5 us (46%)
  Pallas kernels  12.5 us (24%)
  starting transfers between devices  11.3 us (21%)
  waiting for transfers between devices  3.47 us (7%)
  between operations  0.7 us (1%)
    all_to_all x1, blocking collectives, local(): lax.all_to_all(outgoing, 'gy', split_axis=0, concat_axis=0, tiled=True)  24.5 us
    pallas_call x1, Pallas kernels, local(): pl.pallas_call(local_kernel, out_shape=jax.ShapeDtypeStruct((TERMS, 2, WI...  6.65 us
    all_to_all x1, starting transfers between devices, local(): lax.all_to_all(partial, ('gx', 'gy'), split_axis=0, concat_axis=0, tiled=...  5.97 us
    ppermute x1, starting transfers between devices, local(): below = lax.ppermute(high_near, 'gx', up)  3.6 us
    all_to_all x1, waiting for transfers between devices, local(): lax.all_to_all(partial, ('gx', 'gy'), split_axis=0, concat_axis=0, tiled=...  2.9 us
    pallas_call x1, Pallas kernels, local(): pl.pallas_call(border_kernel, out_shape=jax.ShapeDtypeStruct((devices, TE...  1.99 us
    ppermute x1, starting transfers between devices, local(): below_far = lax.ppermute(high_far, 'gx', up)  1.74 us
    pallas_call x1, Pallas kernels, local(): pl.pallas_call(functools.partial(interior_kernel, columns), out_shape=(si...  1.62 us
  transfers between devices with their start and end apart: 5, of which 2 were waited for; matrix products, arithmetic and copies ran while one was open for 0% of the time, Pallas kernels for 20%

profile of v7, /device:TPU:1, one launch (start us, length us, event | category | flops | bytes accessed | tf_op | source)
XLA Modules:
  0.0 52.5 jit_solution(3097821779034624126)
XLA Ops:
  0.6 1.5 %pack.1 = (bf16[16,280,128]{2,1,0:T(8,128)(2,1)S(1)}, s32[8,128]{1,0:T(8,128)S(1)}) custom-call(s32[1,64]{1,0:T(1,128)} %bitcast.6, bf16[2,16,8,512]{3,2,1,0:T(8,128)(2,1)} %stored_hbm.1, f32[2,8,512]{2,1,0:T(8,128)} %disorder.3, s32[2,8,512]{2,1,0:T(8,128)} %vacancy.3), custom_call_target="tpu_custom_call" | custom-call | tf_op jit(solution)/shard_map/pack/pallas_call | solution.py:505
  2.1 0.0 copy-start
  2.1 0.0 copy-start.1
  2.1 24.5 %all_to_all.16.received = bf16[16,280,128]{2,1,0:T(8,128)(2,1)S(1)} all-to-all(bf16[16,280,128]{2,1,0:T(8,128)(2,1)S(1)} %get-tuple-element.19), channel_id=1, replica_groups=mesh['gx'=8,'gy'=16] {'gy'}, dimensions={0} | all-to-all | bytes 2293760 | tf_op jit(solution)/shard_map/all_to_all | solution.py:527
  26.6 0.0 copy-done
  26.6 0.0 copy-done.1
  26.6 0.1 arrange.1
  26.7 3.6 %collective-permute-start = (bf16[88,512]{1,0:T(8,128)(2,1)S(1)}, bf16[88,512]{1,0:T(8,128)(2,1)S(1)}, u32[]{:S(2)}, u32[]{:S(2)}) collective-permute-start(bf16[88,512]{1,0:T(8,128)(2,1)S(1)} %get-tuple-element.20), channel_id=1, source_target_pairs={{0,16},{16,32},{32,48},{48,64},{64,80},{80,96},{96,112},{112,0},{1... | collective-permute-start | bytes 270344 | tf_op jit(solution)/shard_map/ppermute | solution.py:542
  30.3 0.0 collective-permute-start.1
  30.3 1.7 %collective-permute-start.2 = (bf16[80,512]{1,0:T(8,128)(2,1)S(1)}, bf16[80,512]{1,0:T(8,128)(2,1)S(1)}, u32[]{:S(2)}, u32[]{:S(2)}) collective-permute-start(bf16[80,512]{1,0:T(8,128)(2,1)S(1)} %get-tuple-element.22), channel_id=1, source_target_pairs={{0,16},{16,32},{32,48},{48,64},{64,80},{80,96},{96,112},{112,0},{1... | collective-permute-start | bytes 245768 | tf_op jit(solution)/shard_map/ppermute | solution.py:544
  32.1 0.0 collective-permute-start.3
  32.1 1.6 %interior.1 = (f32[2,8,8,640]{3,2,1,0:T(8,128)S(1)}, f32[2,8,8,640]{3,2,1,0:T(8,128)S(1)}, f32[2,8,16,640]{3,2,1,0:T(8,128)S(1)}, f32[2,6,16,640]{3,2,1,0:T(8,12...) custom-call(s32[8,128]{1,0:T(8,128)S(1)} %get-tuple-element.18.table, ...), custom_call_target="tpu_custom_call" | custom-call | flops 10000000 | bytes 8000000 | tf_op jit(solution)/shard_map/interior/pallas_call | solution.py:556
  33.7 0.0 collective-permute-done.below
  33.7 0.6 %collective-permute-done.1.above = bf16[88,512]{1,0:T(8,128)(2,1)S(1)} collective-permute-done((bf16[88,512]{1,0:T(8,128)(2,1)S(1)}, bf16[88,512]{1,0:T(8,128)(2,1)S(1)}, u32[]{:S(2)}, u32[]{:S(2)}) %collective-permute-start.1) | collective-permute-done | bytes 90144 | tf_op jit(solution)/shard_map/ppermute | solution.py:543
  34.3 2.0 %border.1 = f32[128,64]{1,0:T(8,128)} custom-call(bf16[88,512]{1,0:T(8,128)(2,1)S(1)} %collective-permute-done.below, bf16[88,512]{1,0:T(8,128)(2,1)S(1)} %collective-permute-done.1.above, f32[2,8,8,640]{3,2,1,0:T(8,128)S(1)} %get-tuple-element.26.own_level, f32[2,8,8,640]{3,2,1,0:T(8,128)S(1)} %get-tuple-element.27.own_factor, ...), custom_call_target="tpu_custom_call" | custom-call | tf_op jit(solution)/shard_map/border/pallas_call | solution.py:572
  36.3 6.0 %all-to-all-start.1 = ((f32[128,1,64]{2,1,0:T(1,128)}), f32[128,1,64]{2,1,0:T(1,128)S(1)}, u32[]{:S(2)}, u32[]{:S(2)}) async-start(f32[128,1,64]{2,1,0:T(1,128)} %bitcast.2), calls=%async_computation.1 | async-start | bytes 131072 | tf_op jit(solution)/shard_map/all_to_all | solution.py:584
  42.2 0.0 collective-permute-done.2.below_far
  42.2 0.0 collective-permute-done.3.above_far
  42.3 6.6 %local_moments.1 = f32[4,2,8,512]{3,2,1,0:T(8,128)} custom-call(bf16[88,512]{1,0:T(8,128)(2,1)S(1)} %collective-permute-done.below, bf16[88,512]{1,0:T(8,128)(2,1)S(1)} %collective-permute-done.1.above, bf16[80,512]{1,0:T(8,128)(2,1)S(1)} %collective-permute-done.2.below_far, bf16[80,512]{1,0:T(8,128)(2,1)S(1)} %collective-permute-done.3.above_far, ...), custom_call_target="tpu_custom_call" | custom-call | flops 10000000 | bytes 8000000 | tf_op jit(solution)/shard_map/local_moments/pallas_call | solution.py:585
  48.9 2.9 %all-to-all-done.1 = f32[128,1,64]{2,1,0:T(1,128)S(1)} async-done(((f32[128,1,64]{2,1,0:T(1,128)}), f32[128,1,64]{2,1,0:T(1,128)S(1)}, u32[]{:S(2)}, u32[]{:S(2)}) %all-to-all-start.1) | async-done | bytes 32800 | tf_op jit(solution)/shard_map/all_to_all | solution.py:584
  51.8 0.7 %total.1 = f32[4,16]{1,0:T(4,128)} custom-call(f32[128,64]{1,0:T(8,128)S(1)} %bitcast.5), custom_call_target="tpu_custom_call" | custom-call | tf_op jit(solution)/shard_map/total/pallas_call | solution.py:600
Async XLA Ops:
  2.1 24.5 %copy-start = (f32[2,8,512]{2,1,0:T(8,128)S(1)}, f32[2,8,512]{2,1,0:T(8,128)}, u32[]{:S(2)}) copy-start(f32[2,8,512]{2,1,0:T(8,128)} %disorder.3) | copy-start | bytes 98308
  2.1 24.5 %copy-start.1 = (s32[2,8,512]{2,1,0:T(8,128)S(1)}, s32[2,8,512]{2,1,0:T(8,128)}, u32[]{:S(2)}) copy-start(s32[2,8,512]{2,1,0:T(8,128)} %vacancy.3) | copy-start | bytes 98308
  26.7 7.0 %collective-permute-start = (bf16[88,512]{1,0:T(8,128)(2,1)S(1)}, bf16[88,512]{1,0:T(8,128)(2,1)S(1)}, u32[]{:S(2)}, u32[]{:S(2)}) collective-permute-start(bf16[88,512]{1,0:T(8,128)(2,1)S(1)} %get-tuple-element.20), channel_id=1, source_target_pairs={{0,16},{16,32},{32,48},{48,64},{64,80},{80,96},{96,112},{112,0},{1... | collective-permute-start | bytes 270344 | tf_op jit(solution)/shard_map/ppermute | solution.py:542
  30.3 4.0 %collective-permute-start.1 = (bf16[88,512]{1,0:T(8,128)(2,1)S(1)}, bf16[88,512]{1,0:T(8,128)(2,1)S(1)}, u32[]{:S(2)}, u32[]{:S(2)}) collective-permute-start(bf16[88,512]{1,0:T(8,128)(2,1)S(1)} %get-tuple-element.21), channel_id=1, source_target_pairs={{16,0},{32,16},{48,32},{64,48},{80,64},{96,80},{112,96},{0,112},{1... | collective-permute-start | bytes 270344 | tf_op jit(solution)/shard_map/ppermute | solution.py:543
  30.3 11.9 %collective-permute-start.2 = (bf16[80,512]{1,0:T(8,128)(2,1)S(1)}, bf16[80,512]{1,0:T(8,128)(2,1)S(1)}, u32[]{:S(2)}, u32[]{:S(2)}) collective-permute-start(bf16[80,512]{1,0:T(8,128)(2,1)S(1)} %get-tuple-element.22), channel_id=1, source_target_pairs={{0,16},{16,32},{32,48},{48,64},{64,80},{80,96},{96,112},{112,0},{1... | collective-permute-start | bytes 245768 | tf_op jit(solution)/shard_map/ppermute | solution.py:544
  32.1 10.2 %collective-permute-start.3 = (bf16[80,512]{1,0:T(8,128)(2,1)S(1)}, bf16[80,512]{1,0:T(8,128)(2,1)S(1)}, u32[]{:S(2)}, u32[]{:S(2)}) collective-permute-start(bf16[80,512]{1,0:T(8,128)(2,1)S(1)} %get-tuple-element.23), channel_id=1, source_target_pairs={{16,0},{32,16},{48,32},{64,48},{80,64},{96,80},{112,96},{0,112},{1... | collective-permute-start | bytes 245768 | tf_op jit(solution)/shard_map/ppermute | solution.py:545
  36.3 15.5 %all-to-all-start.1 = ((f32[128,1,64]{2,1,0:T(1,128)}), f32[128,1,64]{2,1,0:T(1,128)S(1)}, u32[]{:S(2)}, u32[]{:S(2)}) async-start(f32[128,1,64]{2,1,0:T(1,128)} %bitcast.2), calls=%async_computation.1 | async-start | bytes 131072 | tf_op jit(solution)/shard_map/all_to_all | solution.py:584

commit v8 on v7

--- a/solution.py
+++ b/solution.py
@@ -428,7 +428,7 @@
 
 
 def local_kernel(
-    below, above, below_far, above_far, own_sites, own_start,
+    below, above, above_far, below_far, own_sites, own_start,
     local_out, level, factor, start, real1, imag1, real2, imag2, real3, imag3, real4, products,
 ):
     real4 = Rows(real4, HALO)
@@ -596,7 +596,7 @@
         compiler_params=pltpu.CompilerParams(vmem_limit_bytes=16 * 1024 * 1024),
         cost_estimate=pl.CostEstimate(flops=10**7, bytes_accessed=8 * 10**6, transcendentals=0),
         name="local_moments",
-    )(below, above, below_far, above_far, own_sites, own_start)
+    )(below, above, above_far, below_far, own_sites, own_start)
     trace = pl.pallas_call(
         functools.partial(total_kernel, 2 * WIDTH_X * rows * OWN * columns),
         out_shape=jax.ShapeDtypeStruct((TERMS, R), F32),

time: 52.7 us -> 52.7 us (level)
    ppermute x1, starting transfers between devices: 0.01 us -> 1.43 us  [local(): above_far = lax.ppermute(low_far, 'gx', down)]
    ppermute x1, starting transfers between devices: 1.74 us -> 0.35 us  [local(): below_far = lax.ppermute(high_far, 'gx', up)]
where the time goes in v8:
time: 52.7 us; the launch traced here: 52.5 us
  blocking collectives  24.5 us (46%)
  Pallas kernels  12.5 us (24%)
  starting transfers between devices  11.4 us (22%)
  waiting for transfers between devices  3.44 us (7%)
  between operations  0.7 us (1%)
    all_to_all x1, blocking collectives, local(): lax.all_to_all(outgoing, 'gy', split_axis=0, concat_axis=0, tiled=True)  24.5 us
    pallas_call x1, Pallas kernels, local(): pl.pallas_call(local_kernel, out_shape=jax.ShapeDtypeStruct((TERMS, 2, WI...  6.65 us
    all_to_all x1, starting transfers between devices, local(): lax.all_to_all(partial, ('gx', 'gy'), split_axis=0, concat_axis=0, tiled=...  6 us
    ppermute x1, starting transfers between devices, local(): below = lax.ppermute(high_near, 'gx', up)  3.6 us
    all_to_all x1, waiting for transfers between devices, local(): lax.all_to_all(partial, ('gx', 'gy'), split_axis=0, concat_axis=0, tiled=...  2.9 us
    pallas_call x1, Pallas kernels, local(): pl.pallas_call(border_kernel, out_shape=jax.ShapeDtypeStruct((devices, TE...  1.99 us
    pallas_call x1, Pallas kernels, local(): pl.pallas_call(functools.partial(interior_kernel, columns), out_shape=(si...  1.62 us
    pallas_call x1, Pallas kernels, local(): pl.pallas_call(functools.partial(pack_kernel, columns), out_shape=(jax.Sh...  1.45 us
  transfers between devices with their start and end apart: 5, of which 2 were waited for; matrix products, arithmetic and copies ran while one was open for 0% of the time, Pallas kernels for 20%

profile of v8, /device:TPU:1, one launch (start us, length us, event | category | flops | bytes accessed | tf_op | source)
XLA Modules:
  0.0 52.5 jit_solution(10680754951729978573)
XLA Ops:
  0.6 1.5 %pack.1 = (bf16[16,280,128]{2,1,0:T(8,128)(2,1)S(1)}, s32[8,128]{1,0:T(8,128)S(1)}) custom-call(s32[1,64]{1,0:T(1,128)} %bitcast.6, bf16[2,16,8,512]{3,2,1,0:T(8,128)(2,1)} %stored_hbm.1, f32[2,8,512]{2,1,0:T(8,128)} %disorder.3, s32[2,8,512]{2,1,0:T(8,128)} %vacancy.3), custom_call_target="tpu_custom_call" | custom-call | tf_op jit(solution)/shard_map/pack/pallas_call | solution.py:505
  2.1 0.0 copy-start
  2.1 0.0 copy-start.1
  2.1 24.5 %all_to_all.16.received = bf16[16,280,128]{2,1,0:T(8,128)(2,1)S(1)} all-to-all(bf16[16,280,128]{2,1,0:T(8,128)(2,1)S(1)} %get-tuple-element.19), channel_id=1, replica_groups=mesh['gx'=8,'gy'=16] {'gy'}, dimensions={0} | all-to-all | bytes 2293760 | tf_op jit(solution)/shard_map/all_to_all | solution.py:527
  26.6 0.0 copy-done
  26.6 0.0 copy-done.1
  26.6 0.1 arrange.1
  26.7 3.6 %collective-permute-start = (bf16[88,512]{1,0:T(8,128)(2,1)S(1)}, bf16[88,512]{1,0:T(8,128)(2,1)S(1)}, u32[]{:S(2)}, u32[]{:S(2)}) collective-permute-start(bf16[88,512]{1,0:T(8,128)(2,1)S(1)} %get-tuple-element.20), channel_id=1, source_target_pairs={{0,16},{16,32},{32,48},{48,64},{64,80},{80,96},{96,112},{112,0},{1... | collective-permute-start | bytes 270344 | tf_op jit(solution)/shard_map/ppermute | solution.py:542
  30.3 0.0 collective-permute-start.1
  30.3 1.4 %collective-permute-start.2 = (bf16[80,512]{1,0:T(8,128)(2,1)S(1)}, bf16[80,512]{1,0:T(8,128)(2,1)S(1)}, u32[]{:S(2)}, u32[]{:S(2)}) collective-permute-start(bf16[80,512]{1,0:T(8,128)(2,1)S(1)} %get-tuple-element.22), channel_id=1, source_target_pairs={{16,0},{32,16},{48,32},{64,48},{80,64},{96,80},{112,96},{0,112},{1... | collective-permute-start | bytes 245768 | tf_op jit(solution)/shard_map/ppermute | solution.py:545
  31.7 0.3 collective-permute-start.3
  32.1 1.6 %interior.1 = (f32[2,8,8,640]{3,2,1,0:T(8,128)S(1)}, f32[2,8,8,640]{3,2,1,0:T(8,128)S(1)}, f32[2,8,16,640]{3,2,1,0:T(8,128)S(1)}, f32[2,6,16,640]{3,2,1,0:T(8,12...) custom-call(s32[8,128]{1,0:T(8,128)S(1)} %get-tuple-element.18.table, ...), custom_call_target="tpu_custom_call" | custom-call | flops 10000000 | bytes 8000000 | tf_op jit(solution)/shard_map/interior/pallas_call | solution.py:556
  33.7 0.0 collective-permute-done.below
  33.7 0.5 %collective-permute-done.1.above = bf16[88,512]{1,0:T(8,128)(2,1)S(1)} collective-permute-done((bf16[88,512]{1,0:T(8,128)(2,1)S(1)}, bf16[88,512]{1,0:T(8,128)(2,1)S(1)}, u32[]{:S(2)}, u32[]{:S(2)}) %collective-permute-start.1) | collective-permute-done | bytes 90144 | tf_op jit(solution)/shard_map/ppermute | solution.py:543
  34.3 2.0 %border.1 = f32[128,64]{1,0:T(8,128)} custom-call(bf16[88,512]{1,0:T(8,128)(2,1)S(1)} %collective-permute-done.below, bf16[88,512]{1,0:T(8,128)(2,1)S(1)} %collective-permute-done.1.above, f32[2,8,8,640]{3,2,1,0:T(8,128)S(1)} %get-tuple-element.26.own_level, f32[2,8,8,640]{3,2,1,0:T(8,128)S(1)} %get-tuple-element.27.own_factor, ...), custom_call_target="tpu_custom_call" | custom-call | tf_op jit(solution)/shard_map/border/pallas_call | solution.py:572
  36.3 6.0 %all-to-all-start.1 = ((f32[128,1,64]{2,1,0:T(1,128)}), f32[128,1,64]{2,1,0:T(1,128)S(1)}, u32[]{:S(2)}, u32[]{:S(2)}) async-start(f32[128,1,64]{2,1,0:T(1,128)} %bitcast.2), calls=%async_computation.1 | async-start | bytes 131072 | tf_op jit(solution)/shard_map/all_to_all | solution.py:584
  42.3 0.0 collective-permute-done.2.above_far
  42.3 0.0 collective-permute-done.3.below_far
  42.3 6.6 %local_moments.1 = f32[4,2,8,512]{3,2,1,0:T(8,128)} custom-call(bf16[88,512]{1,0:T(8,128)(2,1)S(1)} %collective-permute-done.below, bf16[88,512]{1,0:T(8,128)(2,1)S(1)} %collective-permute-done.1.above, bf16[80,512]{1,0:T(8,128)(2,1)S(1)} %collective-permute-done.2.above_far, bf16[80,512]{1,0:T(8,128)(2,1)S(1)} %collective-permute-done.3.below_far, ...), custom_call_target="tpu_custom_call" | custom-call | flops 10000000 | bytes 8000000 | tf_op jit(solution)/shard_map/local_moments/pallas_call | solution.py:585
  48.9 2.9 %all-to-all-done.1 = f32[128,1,64]{2,1,0:T(1,128)S(1)} async-done(((f32[128,1,64]{2,1,0:T(1,128)}), f32[128,1,64]{2,1,0:T(1,128)S(1)}, u32[]{:S(2)}, u32[]{:S(2)}) %all-to-all-start.1) | async-done | bytes 32800 | tf_op jit(solution)/shard_map/all_to_all | solution.py:584
  51.8 0.7 %total.1 = f32[4,16]{1,0:T(4,128)} custom-call(f32[128,64]{1,0:T(8,128)S(1)} %bitcast.5), custom_call_target="tpu_custom_call" | custom-call | tf_op jit(solution)/shard_map/total/pallas_call | solution.py:600
Async XLA Ops:
  2.1 24.5 %copy-start = (f32[2,8,512]{2,1,0:T(8,128)S(1)}, f32[2,8,512]{2,1,0:T(8,128)}, u32[]{:S(2)}) copy-start(f32[2,8,512]{2,1,0:T(8,128)} %disorder.3) | copy-start | bytes 98308
  2.1 24.5 %copy-start.1 = (s32[2,8,512]{2,1,0:T(8,128)S(1)}, s32[2,8,512]{2,1,0:T(8,128)}, u32[]{:S(2)}) copy-start(s32[2,8,512]{2,1,0:T(8,128)} %vacancy.3) | copy-start | bytes 98308
  26.7 7.0 %collective-permute-start = (bf16[88,512]{1,0:T(8,128)(2,1)S(1)}, bf16[88,512]{1,0:T(8,128)(2,1)S(1)}, u32[]{:S(2)}, u32[]{:S(2)}) collective-permute-start(bf16[88,512]{1,0:T(8,128)(2,1)S(1)} %get-tuple-element.20), channel_id=1, source_target_pairs={{0,16},{16,32},{32,48},{48,64},{64,80},{80,96},{96,112},{112,0},{1... | collective-permute-start | bytes 270344 | tf_op jit(solution)/shard_map/ppermute | solution.py:542
  30.3 4.0 %collective-permute-start.1 = (bf16[88,512]{1,0:T(8,128)(2,1)S(1)}, bf16[88,512]{1,0:T(8,128)(2,1)S(1)}, u32[]{:S(2)}, u32[]{:S(2)}) collective-permute-start(bf16[88,512]{1,0:T(8,128)(2,1)S(1)} %get-tuple-element.21), channel_id=1, source_target_pairs={{16,0},{32,16},{48,32},{64,48},{80,64},{96,80},{112,96},{0,112},{1... | collective-permute-start | bytes 270344 | tf_op jit(solution)/shard_map/ppermute | solution.py:543
  30.3 12.0 %collective-permute-start.2 = (bf16[80,512]{1,0:T(8,128)(2,1)S(1)}, bf16[80,512]{1,0:T(8,128)(2,1)S(1)}, u32[]{:S(2)}, u32[]{:S(2)}) collective-permute-start(bf16[80,512]{1,0:T(8,128)(2,1)S(1)} %get-tuple-element.22), channel_id=1, source_target_pairs={{16,0},{32,16},{48,32},{64,48},{80,64},{96,80},{112,96},{0,112},{1... | collective-permute-start | bytes 245768 | tf_op jit(solution)/shard_map/ppermute | solution.py:545
  31.7 10.5 %collective-permute-start.3 = (bf16[80,512]{1,0:T(8,128)(2,1)S(1)}, bf16[80,512]{1,0:T(8,128)(2,1)S(1)}, u32[]{:S(2)}, u32[]{:S(2)}) collective-permute-start(bf16[80,512]{1,0:T(8,128)(2,1)S(1)} %get-tuple-element.23), channel_id=1, source_target_pairs={{0,16},{16,32},{32,48},{48,64},{64,80},{80,96},{96,112},{112,0},{1... | collective-permute-start | bytes 245768 | tf_op jit(solution)/shard_map/ppermute | solution.py:544
  36.3 15.6 %all-to-all-start.1 = ((f32[128,1,64]{2,1,0:T(1,128)}), f32[128,1,64]{2,1,0:T(1,128)S(1)}, u32[]{:S(2)}, u32[]{:S(2)}) async-start(f32[128,1,64]{2,1,0:T(1,128)} %bitcast.2), calls=%async_computation.1 | async-start | bytes 131072 | tf_op jit(solution)/shard_map/all_to_all | solution.py:584

commit v9 on v8

--- a/solution.py
+++ b/solution.py
@@ -67,7 +67,11 @@
     me = lax.axis_index("gy")
     first = me * BLOCKS
     total = BLOCKS * columns
-    copies[0].wait()
+    for copy in copies:
+        copy.wait()
+    for b in range(BLOCKS):
+        block = stored[:, :, :, b * BLOCK : (b + 1) * BLOCK]
+        turned[b] = block.reshape(2 * R * WIDTH_X, BLOCK).astype(F32)
     place = lane_index(1, total)
     listed = plan[...]
     spots = [
@@ -80,10 +84,6 @@
     for i, k in enumerate(wanted):
         row = jnp.sum(jnp.where(place == k, source, 0), axis=1, keepdims=True)
         table[i : i + 1, :] = jnp.broadcast_to(row, (1, BLOCK))
-    copies[1].wait()
-    for b in range(BLOCKS):
-        block = stored[:, :, :, b * BLOCK : (b + 1) * BLOCK]
-        turned[b] = block.reshape(2 * R * WIDTH_X, BLOCK).astype(F32)
     lane = lane_index(8, BLOCK)
     edges = [[jnp.zeros((8, BLOCK), F32) for _ in range(2)] for _ in range(BLOCKS)]
     slots = [spot // BLOCKS for spot in spots]
@@ -117,8 +117,6 @@
             old = out[slot, EDGE : EDGE + R, :].astype(F32)
             out[slot, EDGE : EDGE + R, :] = jnp.where(last_half, old, edge).astype(BF16)
 
-    copies[2].wait()
-    copies[3].wait()
     lane16 = lane_index(R, BLOCK)
     ends = []
     for ref in (disorder, vacancy):

time: 52.7 us -> 52.8 us (level)
  no operation moved by 1% of the time
where the time goes in v9:
time: 52.8 us; the launch traced here: 52.5 us
  blocking collectives  24.5 us (46%)
  Pallas kernels  12.5 us (24%)
  starting transfers between devices  11.4 us (22%)
  waiting for transfers between devices  3.44 us (7%)
  between operations  0.7 us (1%)
    all_to_all x1, blocking collectives, local(): lax.all_to_all(outgoing, 'gy', split_axis=0, concat_axis=0, tiled=True)  24.5 us
    pallas_call x1, Pallas kernels, local(): pl.pallas_call(local_kernel, out_shape=jax.ShapeDtypeStruct((TERMS, 2, WI...  6.65 us
    all_to_all x1, starting transfers between devices, local(): lax.all_to_all(partial, ('gx', 'gy'), split_axis=0, concat_axis=0, tiled=...  6 us
    ppermute x1, starting transfers between devices, local(): below = lax.ppermute(high_near, 'gx', up)  3.6 us
    all_to_all x1, waiting for transfers between devices, local(): lax.all_to_all(partial, ('gx', 'gy'), split_axis=0, concat_axis=0, tiled=...  2.9 us
    pallas_call x1, Pallas kernels, local(): pl.pallas_call(border_kernel, out_shape=jax.ShapeDtypeStruct((devices, TE...  1.99 us
    pallas_call x1, Pallas kernels, local(): pl.pallas_call(functools.partial(interior_kernel, columns), out_shape=(si...  1.62 us
    pallas_call x1, Pallas kernels, local(): pl.pallas_call(functools.partial(pack_kernel, columns), out_shape=(jax.Sh...  1.46 us
  transfers between devices with their start and end apart: 5, of which 2 were waited for; matrix products, arithmetic and copies ran while one was open for 0% of the time, Pallas kernels for 20%

profile of v9, /device:TPU:1, one launch (start us, length us, event | category | flops | bytes accessed | tf_op | source)
XLA Modules:
  0.0 52.5 jit_solution(5699376060114989973)
XLA Ops:
  0.6 1.5 %pack.1 = (bf16[16,280,128]{2,1,0:T(8,128)(2,1)S(1)}, s32[8,128]{1,0:T(8,128)S(1)}) custom-call(s32[1,64]{1,0:T(1,128)} %bitcast.6, bf16[2,16,8,512]{3,2,1,0:T(8,128)(2,1)} %stored_hbm.1, f32[2,8,512]{2,1,0:T(8,128)} %disorder.3, s32[2,8,512]{2,1,0:T(8,128)} %vacancy.3), custom_call_target="tpu_custom_call" | custom-call | tf_op jit(solution)/shard_map/pack/pallas_call | solution.py:503
  2.1 0.0 copy-start
  2.1 0.0 copy-start.1
  2.1 24.5 %all_to_all.16.received = bf16[16,280,128]{2,1,0:T(8,128)(2,1)S(1)} all-to-all(bf16[16,280,128]{2,1,0:T(8,128)(2,1)S(1)} %get-tuple-element.19), channel_id=1, replica_groups=mesh['gx'=8,'gy'=16] {'gy'}, dimensions={0} | all-to-all | bytes 2293760 | tf_op jit(solution)/shard_map/all_to_all | solution.py:525
  26.6 0.0 copy-done
  26.6 0.0 copy-done.1
  26.6 0.1 arrange.1
  26.7 3.6 %collective-permute-start = (bf16[88,512]{1,0:T(8,128)(2,1)S(1)}, bf16[88,512]{1,0:T(8,128)(2,1)S(1)}, u32[]{:S(2)}, u32[]{:S(2)}) collective-permute-start(bf16[88,512]{1,0:T(8,128)(2,1)S(1)} %get-tuple-element.20), channel_id=1, source_target_pairs={{0,16},{16,32},{32,48},{48,64},{64,80},{80,96},{96,112},{112,0},{1... | collective-permute-start | bytes 270344 | tf_op jit(solution)/shard_map/ppermute | solution.py:540
  30.3 0.0 collective-permute-start.1
  30.3 1.4 %collective-permute-start.2 = (bf16[80,512]{1,0:T(8,128)(2,1)S(1)}, bf16[80,512]{1,0:T(8,128)(2,1)S(1)}, u32[]{:S(2)}, u32[]{:S(2)}) collective-permute-start(bf16[80,512]{1,0:T(8,128)(2,1)S(1)} %get-tuple-element.22), channel_id=1, source_target_pairs={{16,0},{32,16},{48,32},{64,48},{80,64},{96,80},{112,96},{0,112},{1... | collective-permute-start | bytes 245768 | tf_op jit(solution)/shard_map/ppermute | solution.py:543
  31.8 0.3 collective-permute-start.3
  32.1 1.6 %interior.1 = (f32[2,8,8,640]{3,2,1,0:T(8,128)S(1)}, f32[2,8,8,640]{3,2,1,0:T(8,128)S(1)}, f32[2,8,16,640]{3,2,1,0:T(8,128)S(1)}, f32[2,6,16,640]{3,2,1,0:T(8,12...) custom-call(s32[8,128]{1,0:T(8,128)S(1)} %get-tuple-element.18.table, ...), custom_call_target="tpu_custom_call" | custom-call | flops 10000000 | bytes 8000000 | tf_op jit(solution)/shard_map/interior/pallas_call | solution.py:554
  33.7 0.0 collective-permute-done.below
  33.7 0.5 %collective-permute-done.1.above = bf16[88,512]{1,0:T(8,128)(2,1)S(1)} collective-permute-done((bf16[88,512]{1,0:T(8,128)(2,1)S(1)}, bf16[88,512]{1,0:T(8,128)(2,1)S(1)}, u32[]{:S(2)}, u32[]{:S(2)}) %collective-permute-start.1) | collective-permute-done | bytes 90144 | tf_op jit(solution)/shard_map/ppermute | solution.py:541
  34.3 2.0 %border.1 = f32[128,64]{1,0:T(8,128)} custom-call(bf16[88,512]{1,0:T(8,128)(2,1)S(1)} %collective-permute-done.below, bf16[88,512]{1,0:T(8,128)(2,1)S(1)} %collective-permute-done.1.above, f32[2,8,8,640]{3,2,1,0:T(8,128)S(1)} %get-tuple-element.26.own_level, f32[2,8,8,640]{3,2,1,0:T(8,128)S(1)} %get-tuple-element.27.own_factor, ...), custom_call_target="tpu_custom_call" | custom-call | tf_op jit(solution)/shard_map/border/pallas_call | solution.py:570
  36.3 6.0 %all-to-all-start.1 = ((f32[128,1,64]{2,1,0:T(1,128)}), f32[128,1,64]{2,1,0:T(1,128)S(1)}, u32[]{:S(2)}, u32[]{:S(2)}) async-start(f32[128,1,64]{2,1,0:T(1,128)} %bitcast.2), calls=%async_computation.1 | async-start | bytes 131072 | tf_op jit(solution)/shard_map/all_to_all | solution.py:582
  42.3 0.0 collective-permute-done.2.above_far
  42.3 0.0 collective-permute-done.3.below_far
  42.3 6.6 %local_moments.1 = f32[4,2,8,512]{3,2,1,0:T(8,128)} custom-call(bf16[88,512]{1,0:T(8,128)(2,1)S(1)} %collective-permute-done.below, bf16[88,512]{1,0:T(8,128)(2,1)S(1)} %collective-permute-done.1.above, bf16[80,512]{1,0:T(8,128)(2,1)S(1)} %collective-permute-done.2.above_far, bf16[80,512]{1,0:T(8,128)(2,1)S(1)} %collective-permute-done.3.below_far, ...), custom_call_target="tpu_custom_call" | custom-call | flops 10000000 | bytes 8000000 | tf_op jit(solution)/shard_map/local_moments/pallas_call | solution.py:583
  48.9 2.9 %all-to-all-done.1 = f32[128,1,64]{2,1,0:T(1,128)S(1)} async-done(((f32[128,1,64]{2,1,0:T(1,128)}), f32[128,1,64]{2,1,0:T(1,128)S(1)}, u32[]{:S(2)}, u32[]{:S(2)}) %all-to-all-start.1) | async-done | bytes 32800 | tf_op jit(solution)/shard_map/all_to_all | solution.py:582
  51.8 0.7 %total.1 = f32[4,16]{1,0:T(4,128)} custom-call(f32[128,64]{1,0:T(8,128)S(1)} %bitcast.5), custom_call_target="tpu_custom_call" | custom-call | tf_op jit(solution)/shard_map/total/pallas_call | solution.py:598
Async XLA Ops:
  2.1 24.5 %copy-start = (f32[2,8,512]{2,1,0:T(8,128)S(1)}, f32[2,8,512]{2,1,0:T(8,128)}, u32[]{:S(2)}) copy-start(f32[2,8,512]{2,1,0:T(8,128)} %disorder.3) | copy-start | bytes 98308
  2.1 24.5 %copy-start.1 = (s32[2,8,512]{2,1,0:T(8,128)S(1)}, s32[2,8,512]{2,1,0:T(8,128)}, u32[]{:S(2)}) copy-start(s32[2,8,512]{2,1,0:T(8,128)} %vacancy.3) | copy-start | bytes 98308
  26.7 7.0 %collective-permute-start = (bf16[88,512]{1,0:T(8,128)(2,1)S(1)}, bf16[88,512]{1,0:T(8,128)(2,1)S(1)}, u32[]{:S(2)}, u32[]{:S(2)}) collective-permute-start(bf16[88,512]{1,0:T(8,128)(2,1)S(1)} %get-tuple-element.20), channel_id=1, source_target_pairs={{0,16},{16,32},{32,48},{48,64},{64,80},{80,96},{96,112},{112,0},{1... | collective-permute-start | bytes 270344 | tf_op jit(solution)/shard_map/ppermute | solution.py:540
  30.3 4.0 %collective-permute-start.1 = (bf16[88,512]{1,0:T(8,128)(2,1)S(1)}, bf16[88,512]{1,0:T(8,128)(2,1)S(1)}, u32[]{:S(2)}, u32[]{:S(2)}) collective-permute-start(bf16[88,512]{1,0:T(8,128)(2,1)S(1)} %get-tuple-element.21), channel_id=1, source_target_pairs={{16,0},{32,16},{48,32},{64,48},{80,64},{96,80},{112,96},{0,112},{1... | collective-permute-start | bytes 270344 | tf_op jit(solution)/shard_map/ppermute | solution.py:541
  30.3 12.0 %collective-permute-start.2 = (bf16[80,512]{1,0:T(8,128)(2,1)S(1)}, bf16[80,512]{1,0:T(8,128)(2,1)S(1)}, u32[]{:S(2)}, u32[]{:S(2)}) collective-permute-start(bf16[80,512]{1,0:T(8,128)(2,1)S(1)} %get-tuple-element.22), channel_id=1, source_target_pairs={{16,0},{32,16},{48,32},{64,48},{80,64},{96,80},{112,96},{0,112},{1... | collective-permute-start | bytes 245768 | tf_op jit(solution)/shard_map/ppermute | solution.py:543
  31.8 10.5 %collective-permute-start.3 = (bf16[80,512]{1,0:T(8,128)(2,1)S(1)}, bf16[80,512]{1,0:T(8,128)(2,1)S(1)}, u32[]{:S(2)}, u32[]{:S(2)}) collective-permute-start(bf16[80,512]{1,0:T(8,128)(2,1)S(1)} %get-tuple-element.23), channel_id=1, source_target_pairs={{0,16},{16,32},{32,48},{48,64},{64,80},{80,96},{96,112},{112,0},{1... | collective-permute-start | bytes 245768 | tf_op jit(solution)/shard_map/ppermute | solution.py:542
  36.3 15.6 %all-to-all-start.1 = ((f32[128,1,64]{2,1,0:T(1,128)}), f32[128,1,64]{2,1,0:T(1,128)S(1)}, u32[]{:S(2)}, u32[]{:S(2)}) async-start(f32[128,1,64]{2,1,0:T(1,128)} %bitcast.2), calls=%async_computation.1 | async-start | bytes 131072 | tf_op jit(solution)/shard_map/all_to_all | solution.py:582

commit v10 on v8

--- a/solution.py
+++ b/solution.py
@@ -417,12 +417,11 @@
     moments = jnp.concatenate(
         [one_one, one_two, 2.0 * both - one_one, 2.0 * second - norm], axis=0
     )
-    ones = jnp.ones((8, BLOCK), BF16)
-    total = jnp.zeros((8, TERMS * R), F32)
-    for term in bfloat16_terms(moments):
-        total = total + lax.dot_general(
-            ones, term.astype(BF16), (((1,), (1,)), ((), ())), preferred_element_type=F32
-        )
+    terms = [term.astype(BF16) for term in bfloat16_terms(moments)]
+    total = lax.dot_general(
+        jnp.ones((8, 3 * BLOCK), BF16), jnp.concatenate(terms, axis=1),
+        (((1,), (1,)), ((), ())), preferred_element_type=F32,
+    )
     for i in range(trace_out.shape[0] // 8):
         trace_out[i * 8 : (i + 1) * 8, :] = total
 

time: 52.7 us -> 52.7 us (level)
  transfers between devices with their start and end apart: 5 -> 5, of which waited for: 2 -> 2; matrix products, arithmetic and copies ran while one was open for 0% -> 0% of each run, Pallas kernels for 20% -> 19%
where the time goes in v10:
time: 52.7 us; the launch traced here: 52.5 us
  blocking collectives  24.5 us (46%)
  Pallas kernels  12.5 us (24%)
  starting transfers between devices  11.4 us (22%)
  waiting for transfers between devices  3.44 us (7%)
  between operations  0.7 us (1%)
    all_to_all x1, blocking collectives, local(): lax.all_to_all(outgoing, 'gy', split_axis=0, concat_axis=0, tiled=True)  24.5 us
    pallas_call x1, Pallas kernels, local(): pl.pallas_call(local_kernel, out_shape=jax.ShapeDtypeStruct((TERMS, 2, WI...  6.65 us
    all_to_all x1, starting transfers between devices, local(): lax.all_to_all(partial, ('gx', 'gy'), split_axis=0, concat_axis=0, tiled=...  6 us
    ppermute x1, starting transfers between devices, local(): below = lax.ppermute(high_near, 'gx', up)  3.6 us
    all_to_all x1, waiting for transfers between devices, local(): lax.all_to_all(partial, ('gx', 'gy'), split_axis=0, concat_axis=0, tiled=...  2.9 us
    pallas_call x1, Pallas kernels, local(): pl.pallas_call(border_kernel, out_shape=jax.ShapeDtypeStruct((devices, TE...  1.97 us
    pallas_call x1, Pallas kernels, local(): pl.pallas_call(functools.partial(interior_kernel, columns), out_shape=(si...  1.62 us
    pallas_call x1, Pallas kernels, local(): pl.pallas_call(functools.partial(pack_kernel, columns), out_shape=(jax.Sh...  1.45 us
  transfers between devices with their start and end apart: 5, of which 2 were waited for; matrix products, arithmetic and copies ran while one was open for 0% of the time, Pallas kernels for 19%

profile of v10, /device:TPU:1, one launch (start us, length us, event | category | flops | bytes accessed | tf_op | source)
XLA Modules:
  0.0 52.5 jit_solution(11977973768055731290)
XLA Ops:
  0.6 1.5 %pack.1 = (bf16[16,280,128]{2,1,0:T(8,128)(2,1)S(1)}, s32[8,128]{1,0:T(8,128)S(1)}) custom-call(s32[1,64]{1,0:T(1,128)} %bitcast.6, bf16[2,16,8,512]{3,2,1,0:T(8,128)(2,1)} %stored_hbm.1, f32[2,8,512]{2,1,0:T(8,128)} %disorder.3, s32[2,8,512]{2,1,0:T(8,128)} %vacancy.3), custom_call_target="tpu_custom_call" | custom-call | tf_op jit(solution)/shard_map/pack/pallas_call | solution.py:504
  2.1 0.0 copy-start
  2.1 0.0 copy-start.1
  2.1 24.5 %all_to_all.16.received = bf16[16,280,128]{2,1,0:T(8,128)(2,1)S(1)} all-to-all(bf16[16,280,128]{2,1,0:T(8,128)(2,1)S(1)} %get-tuple-element.19), channel_id=1, replica_groups=mesh['gx'=8,'gy'=16] {'gy'}, dimensions={0} | all-to-all | bytes 2293760 | tf_op jit(solution)/shard_map/all_to_all | solution.py:526
  26.6 0.0 copy-done
  26.6 0.0 copy-done.1
  26.6 0.1 arrange.1
  26.7 3.6 %collective-permute-start = (bf16[88,512]{1,0:T(8,128)(2,1)S(1)}, bf16[88,512]{1,0:T(8,128)(2,1)S(1)}, u32[]{:S(2)}, u32[]{:S(2)}) collective-permute-start(bf16[88,512]{1,0:T(8,128)(2,1)S(1)} %get-tuple-element.20), channel_id=1, source_target_pairs={{0,16},{16,32},{32,48},{48,64},{64,80},{80,96},{96,112},{112,0},{1... | collective-permute-start | bytes 270344 | tf_op jit(solution)/shard_map/ppermute | solution.py:541
  30.3 0.0 collective-permute-start.1
  30.3 1.4 %collective-permute-start.2 = (bf16[80,512]{1,0:T(8,128)(2,1)S(1)}, bf16[80,512]{1,0:T(8,128)(2,1)S(1)}, u32[]{:S(2)}, u32[]{:S(2)}) collective-permute-start(bf16[80,512]{1,0:T(8,128)(2,1)S(1)} %get-tuple-element.22), channel_id=1, source_target_pairs={{16,0},{32,16},{48,32},{64,48},{80,64},{96,80},{112,96},{0,112},{1... | collective-permute-start | bytes 245768 | tf_op jit(solution)/shard_map/ppermute | solution.py:544
  31.7 0.3 collective-permute-start.3
  32.1 1.6 %interior.1 = (f32[2,8,8,640]{3,2,1,0:T(8,128)S(1)}, f32[2,8,8,640]{3,2,1,0:T(8,128)S(1)}, f32[2,8,16,640]{3,2,1,0:T(8,128)S(1)}, f32[2,6,16,640]{3,2,1,0:T(8,12...) custom-call(s32[8,128]{1,0:T(8,128)S(1)} %get-tuple-element.18.table, ...), custom_call_target="tpu_custom_call" | custom-call | flops 10000000 | bytes 8000000 | tf_op jit(solution)/shard_map/interior/pallas_call | solution.py:555
  33.7 0.0 collective-permute-done.below
  33.7 0.5 %collective-permute-done.1.above = bf16[88,512]{1,0:T(8,128)(2,1)S(1)} collective-permute-done((bf16[88,512]{1,0:T(8,128)(2,1)S(1)}, bf16[88,512]{1,0:T(8,128)(2,1)S(1)}, u32[]{:S(2)}, u32[]{:S(2)}) %collective-permute-start.1) | collective-permute-done | bytes 90144 | tf_op jit(solution)/shard_map/ppermute | solution.py:542
  34.3 2.0 %border.1 = f32[128,64]{1,0:T(8,128)} custom-call(bf16[88,512]{1,0:T(8,128)(2,1)S(1)} %collective-permute-done.below, bf16[88,512]{1,0:T(8,128)(2,1)S(1)} %collective-permute-done.1.above, f32[2,8,8,640]{3,2,1,0:T(8,128)S(1)} %get-tuple-element.26.own_level, f32[2,8,8,640]{3,2,1,0:T(8,128)S(1)} %get-tuple-element.27.own_factor, ...), custom_call_target="tpu_custom_call" | custom-call | tf_op jit(solution)/shard_map/border/pallas_call | solution.py:571
  36.2 6.0 %all-to-all-start.1 = ((f32[128,1,64]{2,1,0:T(1,128)}), f32[128,1,64]{2,1,0:T(1,128)S(1)}, u32[]{:S(2)}, u32[]{:S(2)}) async-start(f32[128,1,64]{2,1,0:T(1,128)} %bitcast.2), calls=%async_computation.1 | async-start | bytes 131072 | tf_op jit(solution)/shard_map/all_to_all | solution.py:583
  42.2 0.0 collective-permute-done.2.above_far
  42.3 0.0 collective-permute-done.3.below_far
  42.3 6.6 %local_moments.1 = f32[4,2,8,512]{3,2,1,0:T(8,128)} custom-call(bf16[88,512]{1,0:T(8,128)(2,1)S(1)} %collective-permute-done.below, bf16[88,512]{1,0:T(8,128)(2,1)S(1)} %collective-permute-done.1.above, bf16[80,512]{1,0:T(8,128)(2,1)S(1)} %collective-permute-done.2.above_far, bf16[80,512]{1,0:T(8,128)(2,1)S(1)} %collective-permute-done.3.below_far, ...), custom_call_target="tpu_custom_call" | custom-call | flops 10000000 | bytes 8000000 | tf_op jit(solution)/shard_map/local_moments/pallas_call | solution.py:584
  48.9 2.9 %all-to-all-done.1 = f32[128,1,64]{2,1,0:T(1,128)S(1)} async-done(((f32[128,1,64]{2,1,0:T(1,128)}), f32[128,1,64]{2,1,0:T(1,128)S(1)}, u32[]{:S(2)}, u32[]{:S(2)}) %all-to-all-start.1) | async-done | bytes 32800 | tf_op jit(solution)/shard_map/all_to_all | solution.py:583
  51.8 0.7 %total.1 = f32[4,16]{1,0:T(4,128)} custom-call(f32[128,64]{1,0:T(8,128)S(1)} %bitcast.5), custom_call_target="tpu_custom_call" | custom-call | tf_op jit(solution)/shard_map/total/pallas_call | solution.py:599
Async XLA Ops:
  2.1 24.5 %copy-start = (f32[2,8,512]{2,1,0:T(8,128)S(1)}, f32[2,8,512]{2,1,0:T(8,128)}, u32[]{:S(2)}) copy-start(f32[2,8,512]{2,1,0:T(8,128)} %disorder.3) | copy-start | bytes 98308
  2.1 24.5 %copy-start.1 = (s32[2,8,512]{2,1,0:T(8,128)S(1)}, s32[2,8,512]{2,1,0:T(8,128)}, u32[]{:S(2)}) copy-start(s32[2,8,512]{2,1,0:T(8,128)} %vacancy.3) | copy-start | bytes 98308
  26.7 7.0 %collective-permute-start = (bf16[88,512]{1,0:T(8,128)(2,1)S(1)}, bf16[88,512]{1,0:T(8,128)(2,1)S(1)}, u32[]{:S(2)}, u32[]{:S(2)}) collective-permute-start(bf16[88,512]{1,0:T(8,128)(2,1)S(1)} %get-tuple-element.20), channel_id=1, source_target_pairs={{0,16},{16,32},{32,48},{48,64},{64,80},{80,96},{96,112},{112,0},{1... | collective-permute-start | bytes 270344 | tf_op jit(solution)/shard_map/ppermute | solution.py:541
  30.3 4.0 %collective-permute-start.1 = (bf16[88,512]{1,0:T(8,128)(2,1)S(1)}, bf16[88,512]{1,0:T(8,128)(2,1)S(1)}, u32[]{:S(2)}, u32[]{:S(2)}) collective-permute-start(bf16[88,512]{1,0:T(8,128)(2,1)S(1)} %get-tuple-element.21), channel_id=1, source_target_pairs={{16,0},{32,16},{48,32},{64,48},{80,64},{96,80},{112,96},{0,112},{1... | collective-permute-start | bytes 270344 | tf_op jit(solution)/shard_map/ppermute | solution.py:542
  30.3 11.9 %collective-permute-start.2 = (bf16[80,512]{1,0:T(8,128)(2,1)S(1)}, bf16[80,512]{1,0:T(8,128)(2,1)S(1)}, u32[]{:S(2)}, u32[]{:S(2)}) collective-permute-start(bf16[80,512]{1,0:T(8,128)(2,1)S(1)} %get-tuple-element.22), channel_id=1, source_target_pairs={{16,0},{32,16},{48,32},{64,48},{80,64},{96,80},{112,96},{0,112},{1... | collective-permute-start | bytes 245768 | tf_op jit(solution)/shard_map/ppermute | solution.py:544
  31.7 10.5 %collective-permute-start.3 = (bf16[80,512]{1,0:T(8,128)(2,1)S(1)}, bf16[80,512]{1,0:T(8,128)(2,1)S(1)}, u32[]{:S(2)}, u32[]{:S(2)}) collective-permute-start(bf16[80,512]{1,0:T(8,128)(2,1)S(1)} %get-tuple-element.23), channel_id=1, source_target_pairs={{0,16},{16,32},{32,48},{48,64},{64,80},{80,96},{96,112},{112,0},{1... | collective-permute-start | bytes 245768 | tf_op jit(solution)/shard_map/ppermute | solution.py:543
  36.2 15.6 %all-to-all-start.1 = ((f32[128,1,64]{2,1,0:T(1,128)}), f32[128,1,64]{2,1,0:T(1,128)S(1)}, u32[]{:S(2)}, u32[]{:S(2)}) async-start(f32[128,1,64]{2,1,0:T(1,128)} %bitcast.2), calls=%async_computation.1 | async-start | bytes 131072 | tf_op jit(solution)/shard_map/all_to_all | solution.py:583
